TPU v7x, 128 devices: a whole 4x4x4 slice. The times are simulated.
128 devices in a mesh: tensor: 4 (over x_hi, core), expert: 16 (over z, y), dp: 2 (over x_lo).
Axes of the slice: x: 4 (x_hi: 2, x_lo: 2; x = x_hi * 2 + x_lo), y: 4, z: 4, core: 2. Of those that a mesh axis runs over, the one named last changes fastest.
Arguments:
- queries: bfloat16 [32, 256, 2, 4096], P(('dp', 'expert'), None, None, 'tensor'), parts along dimension 0, may hold values from -6 to 6
- keys: bfloat16 [32, 256, 2, 512], P(('dp', 'expert'), None, None, 'tensor'), parts along dimension 0, may hold values from -6 to 6
- values: bfloat16 [32, 256, 2, 512], P(('dp', 'expert'), None, None, 'tensor'), parts along dimension 0, may hold values from -12 to 12
- q_gain: float32 [128], replicated, may hold values from 0 to 7
- k_gain: float32 [128], replicated, may hold values from 0 to 7
- out_weight: bfloat16 [4096, 4096], P('tensor', 'expert'), may hold values from -0.09375 to 0.09375
- hidden_in: bfloat16 [32, 256, 2, 4096], P(('dp', 'expert'), 'tensor'), parts along dimension 0, may hold values from -3 to 3
- norm_gain: float32 [4096], replicated, may hold values from 0.1 to 1.9
- router: bfloat16 [4096, 64], replicated, may hold values from -4 to 4
- expert_ids: int32 [32, 256, 2, 8], P(('dp', 'expert'), 'tensor'), parts along dimension 0, may hold values from 0 to 63, all different within a row; in each aligned block of 128 rows (0 to 127, 128 to 255, ..., all dimensions but the last counted through in order) at most 17 rows name the same one
- w_gate: bfloat16 [64, 4096, 768], P(('tensor', 'expert')), may hold values from -0.09375 to 0.09375
- w_up: bfloat16 [64, 4096, 768], P(('tensor', 'expert')), may hold values from -0.09375 to 0.09375
- w_down: bfloat16 [64, 768, 4096], P(('tensor', 'expert')), may hold values from -0.21875 to 0.21875
Outputs:
- hidden_out: bfloat16 [32, 256, 2, 4096], P(('dp', 'expert'), 'tensor'), parts along dimension 0
There are 2 independent parts, one for each index of `dp`. A program takes and returns all parts, laid end to end along the dimension named above; an argument that names none is the same for every part. Nothing has to cross between parts.
Inputs may be any that keep to these rules, and one draw needn't show every extreme that they name: `expert_ids`: each row names 8 different experts; among the 128 rows of one device no expert is named by more than 17 rows, a bound that some block reaches.
All inputs are finite; a program needn't handle non-finite values.
Results may differ from a plain program's by a relative error of at most 0.03.
The roundings to bfloat16 on the way count: a program that leaves them out, or rounds other values in their place, can miss the bound.
Values may be sent and summed in bfloat16 or wider, within the bound.
No kernel may reach another device: no remote copies, remote signals or barrier semaphores. Data moves between devices by JAX's collectives and lax.ppermute only.
A program may use at most 256 MiB of HBM per device.

v0:
```python
import functools

import jax
import jax.numpy as jnp
from jax import lax
from jax.experimental import pallas as pl
from jax.experimental.pallas import tpu as pltpu
from jax.sharding import PartitionSpec as P


theta_base = 1000000.0
eps_norm = 1e-06
neg_fill = -1e30
LOG2E = 1.4426950408889634

BF = jnp.bfloat16
F32 = jnp.float32
HD = 128
PB = 256
SEQ = 2
DM = 4096
FF = 768
NE = 64
TOP = 8
ROWS = 128
SLOT = 16
NMAIN = NE * SLOT
NALL = NMAIN + NE
XR = 17 * 32
VMEM_BIG = 60 * 1024 * 1024


def spot(z, y):
    return (z % 4) * 4 + (y % 4)


def y_move(k):
    return [(spot(z, y), spot(z, y + k)) for z in range(4) for y in range(4)]


def z_move(k):
    return [(spot(z, y), spot(z + k, y)) for z in range(4) for y in range(4)]


CORE_SWAP = [(i, i ^ 1) for i in range(4)]
X_SWAP = [(i, i ^ 2) for i in range(4)]


def ring_four(x, move):
    return [x] + [lax.ppermute(x, "expert", move(k)) for k in (1, 2, 3)]


def ring_relay(x, move):
    half = x.shape[0] // 2
    left = lax.ppermute(x, "expert", move(1))
    right = lax.ppermute(x, "expert", move(3))
    lo = lax.ppermute(left[:half], "expert", move(1))
    hi = lax.ppermute(right[half:], "expert", move(3))
    return x, left, right, lo, hi


def rotate_tables(positions):
    freq = theta_base ** (-2.0 * jnp.arange(HD // 2, dtype=F32) / HD)
    ang = positions.astype(F32)[:, None] * freq[None, :]
    cs, sn = jnp.cos(ang), jnp.sin(ang)
    return jnp.concatenate([cs, cs], axis=1), jnp.concatenate([-sn, sn], axis=1)


def keys_kernel(k_ref, v_ref, cos_ref, sin_ref, gain_ref, o_ref):
    cs, sn, gain = cos_ref[...], sin_ref[...], gain_ref[...]
    for s in range(SEQ):
        k = k_ref[:, s * HD : (s + 1) * HD].astype(F32)
        k = k * lax.rsqrt(jnp.mean(k * k, axis=-1, keepdims=True) + eps_norm) * gain
        at = 2 * s * HD
        o_ref[:, at : at + HD] = (k * cs + pltpu.roll(k, HD // 2, 1) * sn).astype(BF)
        o_ref[:, at + HD : at + 2 * HD] = v_ref[:, s * HD : (s + 1) * HD]


def ready_keys(k2, v2, cs, sn, gain):
    return pl.pallas_call(
        keys_kernel, out_shape=jax.ShapeDtypeStruct((PB, 4 * HD), BF), name="ready_keys"
    )(k2, v2, cs, sn, gain)


C2 = HD ** (-0.5) * LOG2E


def attn_part(q, k, v_wide, state, limit):
    m_old, l_old, acc = state
    s = lax.dot_general(q, k, (((1,), (1,)), ((), ())), preferred_element_type=F32)
    if limit is not None:
        row = lax.broadcasted_iota(jnp.int32, (PB, 1), 0)
        s = jnp.where(limit <= row, s, neg_fill)
    m_new = jnp.maximum(m_old, jnp.max(s, axis=-1, keepdims=True))
    p = jnp.exp2((s - m_new) * C2).astype(BF)
    alpha = jnp.exp2((m_old - m_new) * C2)
    pv = jnp.dot(p, v_wide, preferred_element_type=F32)
    return m_new, l_old * alpha + pv[:, HD : HD + 1], acc * alpha + pv[:, :HD]


def keys_of(kv):
    k = kv[:, :HD]
    v = kv[:, HD : 2 * HD]
    return k, jnp.concatenate([v, jnp.ones_like(v)], axis=1)


def put_state(ml_ref, acc_ref, states):
    lane = lax.broadcasted_iota(jnp.int32, (PB, HD), 1)
    (m0, l0, a0), (m1, l1, a1) = states
    ml_ref[...] = jnp.where(
        lane == 0, m0, jnp.where(lane == 1, l0, jnp.where(lane == 2, m1, l1))
    )
    acc_ref[:, :HD] = a0
    acc_ref[:, HD:] = a1


def get_state(ml_ref, acc_ref):
    return [
        (ml_ref[:, 2 * h : 2 * h + 1], ml_ref[:, 2 * h + 1 : 2 * h + 2],
         acc_ref[:, h * HD : (h + 1) * HD])
        for h in range(2)
    ]


def attn_first(sc, q_ref, cos_ref, sin_ref, gain_ref, kv_ref, qr_ref, ml_ref, acc_ref):
    y = sc[3]
    cs, sn, gain = cos_ref[...], sin_ref[...], gain_ref[...]
    k, v = keys_of(kv_ref[...].reshape(1024, 256))
    key = lax.broadcasted_iota(jnp.int32, (1, 1024), 1)
    ahead = key >> 8
    limit = jnp.where(ahead == 0, key & 255, jnp.where(ahead <= y, -1, PB))
    states = []
    for h in range(2):
        q = q_ref[:, h * HD : (h + 1) * HD].astype(F32)
        q = q * lax.rsqrt(jnp.mean(q * q, axis=-1, keepdims=True) + eps_norm) * gain
        q = (q * cs + pltpu.roll(q, HD // 2, 1) * sn).astype(BF)
        qr_ref[:, h * HD : (h + 1) * HD] = q
        start = (
            jnp.full((PB, 1), neg_fill, F32),
            jnp.zeros((PB, 1), F32),
            jnp.zeros((PB, HD), F32),
        )
        states.append(attn_part(q, k, v, start, limit))
    put_state(ml_ref, acc_ref, states)


def attn_next(sc, q_ref, ml_in, acc_in, ka_ref, kb_ref, ml_ref, acc_ref):
    z = sc[2]
    ml_ref[...] = ml_in[...]
    acc_ref[...] = acc_in[...]
    for need, kv_ref in ((1, ka_ref), (3, kb_ref)):

        @pl.when(z >= need)
        def _(kv_ref=kv_ref):
            k, v = keys_of(kv_ref[...].reshape(1024, 256))
            states = [
                attn_part(q_ref[:, h * HD : (h + 1) * HD], k, v, st, None)
                for h, st in enumerate(get_state(ml_ref, acc_ref))
            ]
            put_state(ml_ref, acc_ref, states)


def attn_last(sc, q_ref, ml_in, acc_in, ka_ref, kb_ref, o_ref):
    z = sc[2]

    def finish(states):
        for h, (_, total, acc) in enumerate(states):
            o_ref[:, h * HD : (h + 1) * HD] = (acc / total).astype(BF)

    @pl.when(z >= 2)
    def _():
        kv = jnp.concatenate(
            [ka_ref[...].reshape(512, 256), kb_ref[...].reshape(512, 256)], axis=0
        )
        k, v = keys_of(kv)
        finish(
            [
                attn_part(q_ref[:, h * HD : (h + 1) * HD], k, v, st, None)
                for h, st in enumerate(get_state(ml_in, acc_in))
            ]
        )

    @pl.when(z < 2)
    def _():
        finish(get_state(ml_in, acc_in))


Q_SPEC = pl.BlockSpec((PB, 256), lambda i, sc: (0, i))
ML_SPEC = pl.BlockSpec((PB, HD), lambda i, sc: (0, i))


def kv_spec(n):
    return pl.BlockSpec((n, PB, 256), lambda i, sc: (0, 0, i // 4))


def attn_call(kernel, in_specs, out_specs, out_shape, parts):
    return pl.pallas_call(
        kernel,
        out_shape=out_shape,
        grid_spec=pltpu.PrefetchScalarGridSpec(
            num_scalar_prefetch=1, grid=(8,), in_specs=in_specs, out_specs=out_specs
        ),
        compiler_params=pltpu.CompilerParams(vmem_limit_bytes=VMEM_BIG),
        cost_estimate=pl.CostEstimate(
            flops=parts * 4 * 2**30, bytes_accessed=8 * 2**20, transcendentals=parts * 4 * 2**20
        ),
    )


STATE = (
    jax.ShapeDtypeStruct((PB, 8 * HD), F32),
    jax.ShapeDtypeStruct((PB, SEQ * 1024), F32),
)


def attention(scal, q2, cs, sn, gain, pieces):
    own, left, right, lo, hi = pieces
    table = pl.BlockSpec((PB, HD), lambda i, sc: (0, 0))
    qr, ml, acc = attn_call(
        attn_first,
        [Q_SPEC, table, table, pl.BlockSpec((1, HD), lambda i, sc: (0, 0)), kv_spec(4)],
        (Q_SPEC, ML_SPEC, Q_SPEC),
        (jax.ShapeDtypeStruct((PB, SEQ * 1024), BF),) + STATE,
        1,
    )(scal, q2, cs, sn, gain, own)
    ml, acc = attn_call(
        attn_next, [Q_SPEC, ML_SPEC, Q_SPEC, kv_spec(4), kv_spec(4)], (ML_SPEC, Q_SPEC), STATE, 2
    )(scal, qr, ml, acc, left, right)
    return attn_call(
        attn_last,
        [Q_SPEC, ML_SPEC, Q_SPEC, kv_spec(2), kv_spec(2)],
        Q_SPEC,
        jax.ShapeDtypeStruct((PB, SEQ * 1024), BF),
        1,
    )(scal, qr, ml, acc, lo, hi)


WA = 768
WB = 1024 - WA


def proj_kernel(part, sc, a_ref, *rest):
    n_in = 6 if part == 0 else 7
    w_in, (keep, send, lhs, w, sem) = rest[:n_in], rest[n_in:]
    c, xh = sc[0], sc[1]
    top, low = pl.ds(0, WA), pl.ds(WA, WB)
    two = pl.ds(2 * part, 2)
    moves = [
        (w_in[0].at[two], w.at[:, 0, top]),
        (w_in[1].at[two], w.at[:, 1, top]),
        (w_in[2].at[two], w.at[:, 3, top]),
        (w_in[3], w.at[:, 2, top]),
    ]
    if part == 0:
        moves += [(w_in[4], w.at[0, :, low]), (w_in[5], w.at[1, :, low])]
    else:
        moves += [
            (w_in[4], w.at[1, :, low]),
            (w_in[5], w.at[0, pl.ds(0, 2), low]),
            (w_in[6], w.at[0, pl.ds(2, 2), low]),
        ]
    copies = [pltpu.make_async_copy(a, b, sem.at[i]) for i, (a, b) in enumerate(moves)]
    for cp in copies:
        cp.start()
    for cc in range(2):
        for xx in range(2):
            base = pl.multiple_of(64 * (2 * (xh ^ xx) + (c ^ cc)), 64)
            for s in range(SEQ):
                at = cc * 256 + xx * 128 + s * 64
                lhs[at : at + 64, :] = a_ref[pl.ds(base, 64), s * 1024 : (s + 1) * 1024]
    for cp in copies:
        cp.wait()
    for i in range(2):
        for dy in range(4):
            res = jnp.dot(lhs[...], w[i, dy], preferred_element_type=F32).astype(BF)
            lane = (i * 4 + dy) * 256
            keep[:, lane : lane + 256] = res[:256]
            send[:, lane : lane + 256] = res[256:]


def project(part, scal, attn, pa, pb):
    pieces = list(pa[:3]) + [pa[3 + part]]
    pieces += [pb[0], pb[1]] if part == 0 else [pb[2], pb[3], pb[4]]
    full = pl.BlockSpec(memory_space=pltpu.VMEM)
    return pl.pallas_call(
        functools.partial(proj_kernel, part),
        out_shape=(
            jax.ShapeDtypeStruct((256, DM // 2), BF),
            jax.ShapeDtypeStruct((256, DM // 2), BF),
        ),
        in_specs=[pl.BlockSpec(memory_space=pltpu.SMEM), full]
        + [pl.BlockSpec(memory_space=pl.ANY)] * len(pieces),
        out_specs=(full, full),
        scratch_shapes=[
            pltpu.VMEM((512, 1024), BF),
            pltpu.VMEM((2, 4, 1024, 256), BF),
            pltpu.SemaphoreType.DMA((8,)),
        ],
        compiler_params=pltpu.CompilerParams(vmem_limit_bytes=VMEM_BIG),
        cost_estimate=pl.CostEstimate(
            flops=2 * 2**30, bytes_accessed=7 * 2**20, transcendentals=0
        ),
    )(scal, attn, *pieces)


def dispatch_kernel(
    sc, k0, k1, g0, g1, r0, r1, h_ref, gain_ref, tgt_ref, st_ref, nm_ref, x_ref
):
    z, y = sc[2], sc[3]
    square = jnp.zeros((ROWS, 1), F32)
    for dz in range(4):
        k_ref, g_ref, r_ref = (k0, g0, r0) if dz < 2 else (k1, g1, r1)
        for dy in range(4):
            here = (dz & 1) * 1024 + dy * 256
            there = pl.multiple_of((((z - dz) & 3) * 4 + ((y - dy) & 3)) * 256, 256)
            span = slice(here, here + 256)
            total = (
                h_ref[:, pl.ds(there, 256)].astype(F32)
                + (k_ref[:, span].astype(F32) + g_ref[:, span].astype(F32))
                + r_ref[:, span].astype(F32)
            )
            st = total.astype(BF)
            st_ref[:, pl.ds(there, 256)] = st
            sf = st.astype(F32)
            square = square + jnp.sum(sf * sf, axis=-1, keepdims=True)
    scale = lax.rsqrt(square / DM + eps_norm)
    nm_ref[...] = (st_ref[...].astype(F32) * scale * gain_ref[...]).astype(BF)
    line = lax.broadcasted_iota(jnp.int32, (NALL, ROWS), 0)
    hit = jnp.zeros((NALL, ROWS), F32)
    for k in range(TOP):
        hit = jnp.where(line == tgt_ref[k : k + 1, :], 1.0, hit)
    pick = hit.astype(BF)
    for j in range(8):
        n = nm_ref[:, j * 512 : (j + 1) * 512]
        main = jnp.dot(pick[:NMAIN], n, preferred_element_type=F32).astype(BF)
        for i in range(4):
            f = 4 * j + i
            x_ref[:, f * SLOT : (f + 1) * SLOT, :] = main[:, i * 128 : (i + 1) * 128].reshape(
                NE, SLOT, 128
            )
    ov = jnp.dot(pick[NMAIN:], nm_ref[...], preferred_element_type=F32).astype(BF)
    x_ref[:, 512:544, :] = ov.reshape(NE, 32, 128)


def dispatch(scal, keeps, gots, rests, hid, gain, tgt_t):
    at = lambda i, sc: (0, 0)
    half = pl.BlockSpec((ROWS, DM // 2), at)
    line = pl.BlockSpec((ROWS, DM), at)
    return pl.pallas_call(
        dispatch_kernel,
        out_shape=(
            jax.ShapeDtypeStruct((ROWS, DM), BF),
            jax.ShapeDtypeStruct((ROWS, DM), BF),
            jax.ShapeDtypeStruct((NE, XR, 128), BF),
        ),
        grid_spec=pltpu.PrefetchScalarGridSpec(
            num_scalar_prefetch=1,
            grid=(1,),
            in_specs=[half] * 6
            + [line, pl.BlockSpec((1, DM), at), pl.BlockSpec((TOP, ROWS), at)],
            out_specs=(line, line, pl.BlockSpec((NE, XR, 128), lambda i, sc: (0, 0, 0))),
        ),
        compiler_params=pltpu.CompilerParams(vmem_limit_bytes=VMEM_BIG),
        cost_estimate=pl.CostEstimate(
            flops=2**30, bytes_accessed=14 * 2**20, transcendentals=0
        ),
        name="dispatch",
    )(scal, *keeps, *gots, *rests, hid, gain, tgt_t)


def expert_kernel(x_ref, xo_ref, wg_ref, wu_ref, wd_ref, y_hbm, ga, ua, inner, xov, yb, yo, sem):
    step = pl.program_id(0)

    @pl.when(step == 0)
    def _():
        xov[...] = xo_ref[...].reshape(NE, DM)

    @pl.when(step < 4)
    def _():
        pieces = [
            x_ref[:, i * SLOT : (i + 1) * SLOT, :].reshape(NMAIN, 128) for i in range(8)
        ]
        main = jnp.concatenate(pieces, axis=1)
        lane = pl.multiple_of(step * 1024, 1024)
        rows = jnp.concatenate([main, xov[:, pl.ds(lane, 1024)]], axis=0)
        g = jnp.dot(rows, wg_ref[0], preferred_element_type=F32)
        u = jnp.dot(rows, wu_ref[0], preferred_element_type=F32)

        @pl.when(step == 0)
        def _():
            ga[...] = g
            ua[...] = u

        @pl.when(step > 0)
        def _():
            ga[...] += g
            ua[...] += u

    @pl.when(step == 4)
    def _():
        g = ga[...]
        inner[...] = (g / (1.0 + jnp.exp(-g)) * ua[...]).astype(BF)

    for j in range(4):

        @pl.when(step == 4 + j)
        def _(j=j):
            slot = j % 2
            out = jnp.dot(inner[...], wd_ref[0], preferred_element_type=F32).astype(BF)
            if j >= 2:
                pltpu.make_async_copy(
                    yb.at[slot], y_hbm.at[:, pl.ds((j - 2) * 128, 128)], sem.at[slot]
                ).wait()
            for i in range(8):
                yb[slot, :, i * SLOT : (i + 1) * SLOT, :] = out[
                    :NMAIN, i * 128 : (i + 1) * 128
                ].reshape(NE, SLOT, 128)
            xov[:, j * 1024 : (j + 1) * 1024] = out[NMAIN:]
            pltpu.make_async_copy(
                yb.at[slot], y_hbm.at[:, pl.ds(j * 128, 128)], sem.at[slot]
            ).start()
            if j == 3:
                yo[...] = xov[...].reshape(NE, 32, 128)
                last = pltpu.make_async_copy(yo, y_hbm.at[:, pl.ds(512, 32)], sem.at[2])
                last.start()
                for k in (2, 3):
                    pltpu.make_async_copy(
                        yb.at[k % 2], y_hbm.at[:, pl.ds(k * 128, 128)], sem.at[k % 2]
                    ).wait()
                last.wait()


def run_experts(x, wg, wu, wd):
    lo = lambda i: jnp.minimum(i, 3)
    return pl.pallas_call(
        expert_kernel,
        grid=(8,),
        out_shape=jax.ShapeDtypeStruct((NE, XR, 128), BF),
        in_specs=[
            pl.BlockSpec((NE, 128, 128), lambda i: (0, lo(i), 0)),
            pl.BlockSpec((NE, 32, 128), lambda i: (0, 16, 0)),
            pl.BlockSpec((1, 1024, FF), lambda i: (0, lo(i), 0)),
            pl.BlockSpec((1, 1024, FF), lambda i: (0, lo(i), 0)),
            pl.BlockSpec((1, FF, 1024), lambda i: (0, 0, jnp.maximum(i - 4, 0))),
        ],
        out_specs=pl.BlockSpec(memory_space=pl.ANY),
        scratch_shapes=[
            pltpu.VMEM((NALL, FF), F32),
            pltpu.VMEM((NALL, FF), F32),
            pltpu.VMEM((NALL, FF), BF),
            pltpu.VMEM((NE, DM), BF),
            pltpu.VMEM((2, NE, 128, 128), BF),
            pltpu.VMEM((NE, 32, 128), BF),
            pltpu.SemaphoreType.DMA((3,)),
        ],
        compiler_params=pltpu.CompilerParams(vmem_limit_bytes=VMEM_BIG),
        cost_estimate=pl.CostEstimate(
            flops=20 * 2**30, bytes_accessed=36 * 2**20, transcendentals=2**20
        ),
        name="experts",
    )(x, x, wg, wu, wd)


def combine_kernel(y_ref, yo_ref, st_ref, tgt_ref, gate_ref, o_ref, gm, go, yov):
    step = pl.program_id(0)

    @pl.when(step == 0)
    def _():
        yov[...] = yo_ref[...].reshape(NE, DM)
        lane = lax.broadcasted_iota(jnp.int32, (ROWS, NALL), 1)
        mix = jnp.zeros((ROWS, NALL), F32)
        for k in range(TOP):
            mix = jnp.where(lane == tgt_ref[:, k : k + 1], gate_ref[:, k : k + 1], mix)
        hi = mix.astype(BF)
        lo = (mix - hi.astype(F32)).astype(BF)
        gm[:ROWS] = hi[:, :NMAIN]
        gm[ROWS:] = lo[:, :NMAIN]
        go[:ROWS] = hi[:, NMAIN:]
        go[ROWS:] = lo[:, NMAIN:]

    pieces = [y_ref[:, i * SLOT : (i + 1) * SLOT, :].reshape(NMAIN, 128) for i in range(8)]
    main = jnp.concatenate(pieces, axis=1)
    at = pl.multiple_of(step * 1024, 1024)
    both = jnp.dot(gm[...], main, preferred_element_type=F32) + jnp.dot(
        go[...], yov[:, pl.ds(at, 1024)], preferred_element_type=F32
    )
    r = lax.broadcasted_iota(jnp.int32, (ROWS, ROWS), 0)
    c = lax.broadcasted_iota(jnp.int32, (ROWS, ROWS), 1)
    turn = jnp.where(c == (r & 1) * 64 + (r >> 1), 1.0, 0.0).astype(BF)
    st = jnp.dot(turn, st_ref[...], preferred_element_type=F32)
    o_ref[...] = (st + (both[:ROWS] + both[ROWS:])).astype(BF)


def combine(y, stream, tgt, gates):
    return pl.pallas_call(
        combine_kernel,
        grid=(4,),
        out_shape=jax.ShapeDtypeStruct((ROWS, DM), BF),
        in_specs=[
            pl.BlockSpec((NE, 128, 128), lambda i: (0, i, 0)),
            pl.BlockSpec((NE, 32, 128), lambda i: (0, 16, 0)),
            pl.BlockSpec((ROWS, 1024), lambda i: (0, i)),
            pl.BlockSpec((ROWS, TOP), lambda i: (0, 0)),
            pl.BlockSpec((ROWS, TOP), lambda i: (0, 0)),
        ],
        out_specs=pl.BlockSpec((ROWS, 1024), lambda i: (0, i)),
        scratch_shapes=[
            pltpu.VMEM((2 * ROWS, NMAIN), BF),
            pltpu.VMEM((2 * ROWS, NE), BF),
            pltpu.VMEM((NE, DM), BF),
        ],
        compiler_params=pltpu.CompilerParams(vmem_limit_bytes=VMEM_BIG),
        cost_estimate=pl.CostEstimate(
            flops=2 * 2**30, bytes_accessed=11 * 2**20, transcendentals=0
        ),
        name="combine",
    )(y, y, stream, tgt, gates)


def slots(ids):
    catalog = jnp.arange(NE, dtype=jnp.int32)
    hits = jnp.any(ids[:, :, None] == catalog, axis=1).astype(BF)
    below = (jnp.arange(ROWS)[:, None] > jnp.arange(ROWS)[None, :]).astype(BF)
    before = jnp.dot(below, hits, preferred_element_type=F32)
    slot = jnp.sum(
        jnp.where(ids[:, :, None] == catalog, before[:, None, :], 0.0), axis=-1
    ).astype(jnp.int32)
    return jnp.where(slot < SLOT, ids * SLOT + slot, NMAIN + ids)


def on_device(
    queries,
    keys,
    values,
    q_gain,
    k_gain,
    out_weight,
    hidden_in,
    norm_gain,
    router,
    expert_ids,
    w_gate,
    w_up,
    w_down,
):
    t, e = lax.axis_index("tensor"), lax.axis_index("expert")
    scal = jnp.stack([t & 1, t >> 1, e >> 2, e & 3]).astype(jnp.int32)
    cs, sn = rotate_tables(e * PB + jnp.arange(PB, dtype=jnp.int32))

    kv = ready_keys(
        keys[0].reshape(PB, SEQ * HD), values[0].reshape(PB, SEQ * HD), cs, sn, k_gain.reshape(1, HD)
    )
    kv, weight = lax.optimization_barrier((kv, out_weight))
    kv_all = ring_relay(jnp.stack(ring_four(kv, y_move)), z_move)
    wa_all = ring_relay(jnp.stack(ring_four(weight[:WA], z_move)), y_move)
    wb_all = ring_relay(jnp.stack(ring_four(weight[WA:], y_move)), z_move)

    q2 = queries[0].reshape(PB, SEQ * 1024)
    ids = expert_ids[0].reshape(ROWS, TOP)
    tgt = slots(ids)
    tgt_t = jnp.transpose(tgt.reshape(64, SEQ, TOP), (2, 1, 0)).reshape(TOP, ROWS)
    hid = jnp.transpose(hidden_in[0], (1, 0, 2)).reshape(ROWS, DM)

    attn = attention(scal, q2, cs, sn, q_gain.reshape(1, HD), kv_all)
    keeps, gots, rests = [], [], []
    for part in range(2):
        keep, send = project(part, scal, attn, wa_all, wb_all)
        got = lax.ppermute(send, "tensor", CORE_SWAP)
        other = (keep[128:].astype(F32) + got[128:].astype(F32)).astype(BF)
        keeps.append(keep)
        gots.append(got)
        rests.append(lax.ppermute(other, "tensor", X_SWAP))
    stream, normed, x = dispatch(
        scal, keeps, gots, rests, hid, norm_gain.reshape(1, DM), tgt_t
    )
    arrived = lax.all_to_all(x, ("tensor", "expert"), split_axis=0, concat_axis=0, tiled=True)

    logits = jnp.dot(normed, router, preferred_element_type=F32)
    logits = jnp.transpose(logits.reshape(SEQ, 64, NE), (1, 0, 2)).reshape(ROWS, NE)
    chosen = ids[:, :, None] == jnp.arange(NE, dtype=jnp.int32)
    gates = jax.nn.softmax(jnp.sum(jnp.where(chosen, logits[:, None, :], 0.0), axis=-1), axis=-1)

    done = run_experts(arrived, w_gate, w_up, w_down)
    back = lax.all_to_all(done, ("tensor", "expert"), split_axis=0, concat_axis=0, tiled=True)
    out = combine(back, stream, tgt, gates)
    return out.reshape(hidden_in.shape)


def solution(mesh):
    return jax.shard_map(
        on_device,
        mesh=mesh,
        in_specs=(
            P(("dp", "expert"), None, None, "tensor"),
            P(("dp", "expert"), None, None, "tensor"),
            P(("dp", "expert"), None, None, "tensor"),
            P(),
            P(),
            P("tensor", "expert"),
            P(("dp", "expert"), "tensor", None, None),
            P(),
            P(),
            P(("dp", "expert"), "tensor", None, None),
            P(("tensor", "expert"), None, None),
            P(("tensor", "expert"), None, None),
            P(("tensor", "expert"), None, None),
        ),
        out_specs=P(("dp", "expert"), "tensor", None, None),
        check_vma=False,
    )
```

profile of v0, /device:TPU:25, one launch (start us, length us, event | category | flops | bytes accessed | tf_op | source)
XLA Modules:
  0.0 508.7 jit_solution(11403191836318385393)
XLA Ops:
  0.0 0.5 fusion.2
  0.6 1.7 copy_bitcast_fusion
  2.3 0.8 pad_maximum_fusion.3
  3.1 2.1 ready_keys.1
  5.3 1.7 collective-permute-start.7
  7.0 3.3 collective-permute-start.8
  10.3 0.7 collective-permute-start.9
  11.1 2.2 collective-permute-start.14
  13.4 4.6 collective-permute-done.7
  17.9 9.3 %collective-permute-done.8 = bf16[768,256]{1,0:T(8,128)(2,1)S(1)} collective-permute-done((bf16[768,256]{1,0:T(8,128)(2,1)S(1)}, bf16[768,256]{1,0:T(8,128)(2,1)S(1)}, u32[]{:S(2)}, u32[]{:S(2)}) %collective-permute-start.8) | collective-permute-done | bytes 393248 | tf_op jit(solution)/shard_map/ppermute | solution.py:50
  27.5 0.5 collective-permute-start.11
  28.0 0.2 copy-done.8
  28.2 2.0 collective-permute-start
  30.2 0.2 collective-permute-start.1
  30.5 0.3 collective-permute-start.2
  30.8 2.1 collective-permute-start.15
  32.9 44.3 %collective-permute-done.15 = bf16[256,256]{1,0:T(8,128)(2,1)S(1)} collective-permute-done((bf16[256,256]{1,0:T(8,128)(2,1)S(1)}, bf16[256,256]{1,0:T(8,128)(2,1)S(1)}, u32[]{:S(2)}, u32[]{:S(2)}) %collective-permute-start.15) | collective-permute-done | bytes 131104 | tf_op jit(solution)/shard_map/ppermute | solution.py:50
  77.2 0.9 pad_maximum_fusion.2.rest_4_
  78.1 2.3 collective-permute-start.16
  80.4 1.1 pad_maximum_fusion.1.kv_ref
  81.6 2.7 collective-permute-start.4
  84.2 9.0 %collective-permute-done.16.rest_5_ = bf16[4,256,256]{2,1,0:T(8,128)(2,1)} collective-permute-done((bf16[4,256,256]{2,1,0:T(8,128)(2,1)}, bf16[4,256,256]{2,1,0:T(8,128)(2,1)}, u32[]{:S(2)}, u32[]{:S(2)}) %collective-permute-start.16) | collective-permute-done | bytes 524320 | tf_op jit(solution)/shard_map/ppermute | solution.py:55
  93.3 1.2 collective-permute-start.18
  94.5 1.2 copy.48
  95.7 0.6 pad_add_fusion.sc
  96.3 15.8 %shard_map.127 = (bf16[256,2048]{1,0:T(8,128)(2,1)}, f32[256,1024]{1,0:T(8,128)}, f32[256,2048]{1,0:T(8,128)}) custom-call(s32[4]{0:T(128)} %pad_add_fusion.sc, bf16[256,2048]{1,0:T(8,128)(2,1)} %bitcast.59, f32[256,128]{1,0:T(8,128)} %get-tuple-element.42.cos_ref, f32[256,128]{1,0:T(8,128)} %get-tuple-element.43.sin_ref, f32[1,128]{1,0:T(1,128)} %bitcast.78, ...), custom_call_target="tpu_custom_call" | custom-call | flops 4294967296 | bytes 8388608 | tf_op jit(solution)/shard_map/pallas_call | solution.py:219
  112.1 1.7 slice.52
  113.8 3.5 collective-permute-done.18.rest_4_
  117.3 1.2 collective-permute-start.19
  118.4 1.7 slice.53
  120.1 1.1 slice.48
  121.2 0.3 collective-permute-start.5
  121.5 1.1 slice.49
  122.6 2.5 collective-permute-start.6
  125.1 1.2 slice.51
  126.2 0.5 collective-permute-start.17
  126.8 7.9 %shard_map.128 = (f32[256,1024]{1,0:T(8,128)}, f32[256,2048]{1,0:T(8,128)}) custom-call(s32[4]{0:T(128)} %pad_add_fusion.sc, bf16[256,2048]{1,0:T(8,128)(2,1)} %get-tuple-element.20.q_ref, f32[256,1024]{1,0:T(8,128)} %get-tuple-element.21.ml_in, f32[256,2048]{1,0:T(8,128)} %get-tuple-element.22.acc_in, bf16[4,256,512]{2,1,0:T(8,128)(2,1)} %collective-permute-done.3.ka_ref, ...), custom_call_target="tpu_custom_call" | custom-call | flops 8589934592 | bytes 8388608 | tf_op jit(solution)/shard_map/pallas_call | solution.py:226
  134.7 19.0 %collective-permute-start.20 = (bf16[2,256,256]{2,1,0:T(8,128)(2,1)}, bf16[2,256,256]{2,1,0:T(8,128)(2,1)S(1)}, u32[]{:S(2)}, u32[]{:S(2)}) collective-permute-start(bf16[2,256,256]{2,1,0:T(8,128)(2,1)} %slice.53), channel_id=1, source_target_pairs={{0,24},{2,26},{4,28},{6,30},{8,0},{10,2},{12,4},{14,6},{16,8},{18,... | collective-permute-start | bytes 786440 | tf_op jit(solution)/shard_map/ppermute | solution.py:58
  153.7 2.1 slice.50
  155.8 2.7 collective-permute-start.12
  158.4 7.4 %shard_map.129.a_ref = bf16[256,2048]{1,0:T(8,128)(2,1)} custom-call(s32[4]{0:T(128)} %pad_add_fusion.sc, bf16[256,2048]{1,0:T(8,128)(2,1)} %get-tuple-element.20.q_ref, f32[256,1024]{1,0:T(8,128)} %get-tuple-element.23.ml_in, f32[256,2048]{1,0:T(8,128)} %get-tuple-element.24.acc_in, bf16[2,256,512]{2,1,0:T(8,128)(2,1)} %collective-permute-done.5.ka_ref, ...), custom_call_target="tpu_custom_call" | custom-call | flops 4294967296 | bytes 8388608 | tf_op jit(solution)/shard_map/pallas_call | solution.py:229
  165.9 0.7 copy-done.13
  166.5 7.0 %shard_map.131 = (bf16[256,2048]{1,0:T(8,128)(2,1)}, bf16[256,2048]{1,0:T(8,128)(2,1)}) custom-call(s32[4]{0:T(128)} %pad_add_fusion.sc, bf16[256,2048]{1,0:T(8,128)(2,1)} %shard_map.129.a_ref, bf16[4,768,256]{2,1,0:T(8,128)(2,1)} %copy-done.4, bf16[4,768,256]{2,1,0:T(8,128)(2,1)} %collective-permute-done.10.rest_1_, ...), custom_call_target="tpu_custom_call" | custom-call | flops 2147483648 | bytes 7340032 | tf_op jit(solution)/shard_map/pallas_call | solution.py:285
  173.6 4.2 collective-permute-start.22
  177.8 0.9 copy-done.12
  178.7 7.1 %shard_map.130 = (bf16[256,2048]{1,0:T(8,128)(2,1)}, bf16[256,2048]{1,0:T(8,128)(2,1)}) custom-call(s32[4]{0:T(128)} %pad_add_fusion.sc, bf16[256,2048]{1,0:T(8,128)(2,1)} %shard_map.129.a_ref, bf16[4,768,256]{2,1,0:T(8,128)(2,1)} %copy-done.4, bf16[4,768,256]{2,1,0:T(8,128)(2,1)} %collective-permute-done.10.rest_1_, ...), custom_call_target="tpu_custom_call" | custom-call | flops 2147483648 | bytes 7340032 | tf_op jit(solution)/shard_map/pallas_call | solution.py:285
  186.1 0.9 add_convert_fusion
  187.0 2.7 collective-permute-start.24
  189.8 2.0 add_convert_fusion.1
  191.8 1.8 collective-permute-start.23
  194.0 0.7 reshape.48.tgt_ref
  194.6 1.6 copy.38
  196.2 5.5 %collective-permute-done.24.r1 = bf16[128,2048]{1,0:T(8,128)(2,1)S(1)} collective-permute-done((bf16[128,2048]{1,0:T(8,128)(2,1)}, bf16[128,2048]{1,0:T(8,128)(2,1)S(1)}, u32[]{:S(2)}, u32[]{:S(2)}) %collective-permute-start.24) | collective-permute-done | bytes 524320 | tf_op jit(solution)/shard_map/ppermute | solution.py:572
  201.8 11.3 %collective-permute-done.23.r0 = bf16[128,2048]{1,0:T(8,128)(2,1)} collective-permute-done((bf16[128,2048]{1,0:T(8,128)(2,1)}, bf16[128,2048]{1,0:T(8,128)(2,1)}, u32[]{:S(2)}, u32[]{:S(2)}) %collective-permute-start.23) | collective-permute-done | bytes 524320 | tf_op jit(solution)/shard_map/ppermute | solution.py:572
  213.1 9.8 %dispatch.1 = (bf16[128,4096]{1,0:T(8,128)(2,1)}, bf16[128,4096]{1,0:T(8,128)(2,1)}, bf16[64,544,128]{2,1,0:T(8,128)(2,1)}) custom-call(s32[4]{0:T(128)} %pad_add_fusion.sc, bf16[256,2048]{1,0:T(8,128)(2,1)} %get-tuple-element.26.k0, bf16[256,2048]{1,0:T(8,128)(2,1)} %get-tuple-element.27.k1, bf16[256,2048]{1,0:T(8,128)(2,1)} %collective-permute-done.21.g0, ...), custom_call_target="tpu_custom_call" | custom-call | flops 1073741824 | bytes 14680064 | tf_op jit(solution)/shard_map/dispatch/pallas_call | solution.py:349
  222.9 120.5 %all_to_all.10.x_ref.xo_ref = bf16[64,544,128]{2,1,0:T(8,128)(2,1)} all-to-all(bf16[64,544,128]{2,1,0:T(8,128)(2,1)} %get-tuple-element.30), channel_id=1, replica_groups=mesh['tensor'=4,'expert'=16,'dp'=2] {'tensor','expert'}, dimensions={0} | all-to-all | bytes 17825792 | tf_op jit(solution)/shard_map/all_to_all | solution.py:576
  343.4 30.9 %experts.1 = bf16[64,544,128]{2,1,0:T(8,128)(2,1)} custom-call(bf16[64,544,128]{2,1,0:T(8,128)(2,1)} %all_to_all.10.x_ref.xo_ref, bf16[64,544,128]{2,1,0:T(8,128)(2,1)} %all_to_all.10.x_ref.xo_ref, bf16[1,4096,768]{2,1,0:T(8,128)(2,1)} %wg_ref.1, bf16[1,4096,768]{2,1,0:T(8,128)(2,1)} %wu_ref.1, bf16[1,768,4096]{2,1,0:T(8,128)(2,1)} %wd_ref.1), custom_call_target="tpu_custom_call" | custom-call | flops 21474836480 | bytes 37748736 | tf_op jit(solution)/shard_map/experts/pallas_call | solution.py:435
  374.3 8.8 %all-to-all-start.1 = ((bf16[64,544,128]{2,1,0:T(8,128)(2,1)}), bf16[64,544,128]{2,1,0:T(8,128)(2,1)}, u32[]{:S(2)}, u32[]{:S(2)}) async-start(bf16[64,544,128]{2,1,0:T(8,128)(2,1)} %experts.1), calls=%async_computation.1 | async-start | bytes 17825792 | tf_op jit(solution)/shard_map/all_to_all | solution.py:584
  383.1 0.6 add_select_fusion.tgt_ref
  383.8 0.5 fusion.5
  384.7 0.7 broadcast_divide_fusion.gate_ref
  385.4 112.3 %all-to-all-done.1.y_ref.yo_ref = bf16[64,544,128]{2,1,0:T(8,128)(2,1)} async-done(((bf16[64,544,128]{2,1,0:T(8,128)(2,1)}), bf16[64,544,128]{2,1,0:T(8,128)(2,1)}, u32[]{:S(2)}, u32[]{:S(2)}) %all-to-all-start.1) | async-done | bytes 8912928 | tf_op jit(solution)/shard_map/all_to_all | solution.py:584
  497.8 8.2 %combine.1 = bf16[128,4096]{1,0:T(8,128)(2,1)} custom-call(bf16[64,544,128]{2,1,0:T(8,128)(2,1)} %all-to-all-done.1.y_ref.yo_ref, bf16[64,544,128]{2,1,0:T(8,128)(2,1)} %all-to-all-done.1.y_ref.yo_ref, bf16[128,4096]{1,0:T(8,128)(2,1)} %get-tuple-element.31.st_ref, s32[128,8]{1,0:T(8,128)} %add_select_fusion.tgt_ref, f32[128,8]{1,0:T(8,128)} %broadcast_divide_fusion.gate_ref), custom_call_target="tpu_custom_call" | custom-call | flops 2147483648 | bytes 11534336 | tf_op jit(solution)/shard_map/combine/pallas_call | solution.py:495
  505.9 2.5 reshape.50
  (69 shorter events, 1.6 us)
Async XLA Ops:
  0.0 383.8 %copy-start = (bf16[4096,64]{0,1:T(8,128)(2,1)S(1)}, bf16[4096,64]{0,1:T(8,128)(2,1)}, u32[]{:S(2)}) copy-start(bf16[4096,64]{0,1:T(8,128)(2,1)} %param.21) | copy-start | bytes 1572868
  0.0 5.2 %copy-start.10 = (bf16[1024,256]{1,0:T(8,128)(2,1)S(1)}, bf16[1024,256]{1,0:T(8,128)(2,1)}, u32[]{:S(2)}) copy-start(bf16[1024,256]{1,0:T(8,128)(2,1)} %param.18) | copy-start | bytes 1572868
  5.3 12.6 %collective-permute-start.7 = (bf16[768,256]{1,0:T(8,128)(2,1)S(1)}, bf16[768,256]{1,0:T(8,128)(2,1)S(1)}, u32[]{:S(2)}, u32[]{:S(2)}) collective-permute-start(bf16[768,256]{1,0:T(8,128)(2,1)S(1)} %get-tuple-element.38), channel_id=1, source_target_pairs={{0,8},{2,10},{4,12},{6,14},{8,16},{10,18},{12,20},{14,22},{16,24},... | collective-permute-start | bytes 1179656 | tf_op jit(solution)/shard_map/ppermute | solution.py:50
  7.0 20.3 %collective-permute-start.8 = (bf16[768,256]{1,0:T(8,128)(2,1)S(1)}, bf16[768,256]{1,0:T(8,128)(2,1)S(1)}, u32[]{:S(2)}, u32[]{:S(2)}) collective-permute-start(bf16[768,256]{1,0:T(8,128)(2,1)S(1)} %get-tuple-element.38), channel_id=1, source_target_pairs={{0,16},{2,18},{4,20},{6,22},{8,24},{10,26},{12,28},{14,30},{16,0},... | collective-permute-start | bytes 1179656 | tf_op jit(solution)/shard_map/ppermute | solution.py:50
  10.3 17.0 %collective-permute-start.9 = (bf16[768,256]{1,0:T(8,128)(2,1)S(1)}, bf16[768,256]{1,0:T(8,128)(2,1)S(1)}, u32[]{:S(2)}, u32[]{:S(2)}) collective-permute-start(bf16[768,256]{1,0:T(8,128)(2,1)S(1)} %get-tuple-element.38), channel_id=1, source_target_pairs={{0,24},{2,26},{4,28},{6,30},{8,0},{10,2},{12,4},{14,6},{16,8},{18,... | collective-permute-start | bytes 1179656 | tf_op jit(solution)/shard_map/ppermute | solution.py:50
  11.0 19.4 %collective-permute-start.13 = (bf16[256,256]{1,0:T(8,128)(2,1)S(1)}, bf16[256,256]{1,0:T(8,128)(2,1)S(1)}, u32[]{:S(2)}, u32[]{:S(2)}) collective-permute-start(bf16[256,256]{1,0:T(8,128)(2,1)S(1)} %get-tuple-element.36), channel_id=1, source_target_pairs={{0,2},{2,4},{4,6},{6,0},{8,10},{10,12},{12,14},{14,8},{16,18},{18,... | collective-permute-start | bytes 393224 | tf_op jit(solution)/shard_map/ppermute | solution.py:50
  11.1 19.7 %collective-permute-start.14 = (bf16[256,256]{1,0:T(8,128)(2,1)S(1)}, bf16[256,256]{1,0:T(8,128)(2,1)S(1)}, u32[]{:S(2)}, u32[]{:S(2)}) collective-permute-start(bf16[256,256]{1,0:T(8,128)(2,1)S(1)} %get-tuple-element.36), channel_id=1, source_target_pairs={{0,4},{2,6},{4,0},{6,2},{8,12},{10,14},{12,8},{14,10},{16,20},{18,... | collective-permute-start | bytes 393224 | tf_op jit(solution)/shard_map/ppermute | solution.py:50
  27.2 1.0 copy-start.8
  27.4 56.8 %copy-start.4 = (bf16[4,768,256]{2,1,0:T(8,128)(2,1)}, bf16[4,768,256]{2,1,0:T(8,128)(2,1)S(1)}, u32[]{:S(2)}) copy-start(bf16[4,768,256]{2,1,0:T(8,128)(2,1)S(1)} %pad_maximum_fusion.rest_0_) | copy-start | bytes 4718596
  27.5 97.6 %collective-permute-start.11 = (bf16[4,768,256]{2,1,0:T(8,128)(2,1)S(1)}, bf16[4,768,256]{2,1,0:T(8,128)(2,1)}, u32[]{:S(2)}, u32[]{:S(2)}) collective-permute-start(bf16[4,768,256]{2,1,0:T(8,128)(2,1)S(1)} %pad_maximum_fusion.rest_0_), channel_id=1, source_target_pairs={{0,6},{2,0},{4,2},{6,4},{8,14},{10,8},{12,10},{14,12},{16,22},{18,... | collective-permute-start | bytes 4718600 | tf_op jit(solution)/shard_map/ppermute | solution.py:56
  28.2 52.2 %collective-permute-start = (bf16[256,512]{1,0:T(8,128)(2,1)S(1)}, bf16[256,512]{1,0:T(8,128)(2,1)S(1)}, u32[]{:S(2)}, u32[]{:S(2)}) collective-permute-start(bf16[256,512]{1,0:T(8,128)(2,1)S(1)} %copy-done.8), channel_id=1, source_target_pairs={{0,2},{2,4},{4,6},{6,0},{8,10},{10,12},{12,14},{14,8},{16,18},{18,... | collective-permute-start | bytes 786440 | tf_op jit(solution)/shard_map/ppermute | solution.py:50
  30.2 50.2 %collective-permute-start.1 = (bf16[256,512]{1,0:T(8,128)(2,1)S(1)}, bf16[256,512]{1,0:T(8,128)(2,1)S(1)}, u32[]{:S(2)}, u32[]{:S(2)}) collective-permute-start(bf16[256,512]{1,0:T(8,128)(2,1)S(1)} %copy-done.8), channel_id=1, source_target_pairs={{0,4},{2,6},{4,0},{6,2},{8,12},{10,14},{12,8},{14,10},{16,20},{18,... | collective-permute-start | bytes 786440 | tf_op jit(solution)/shard_map/ppermute | solution.py:50
  30.5 50.0 %collective-permute-start.2 = (bf16[256,512]{1,0:T(8,128)(2,1)S(1)}, bf16[256,512]{1,0:T(8,128)(2,1)S(1)}, u32[]{:S(2)}, u32[]{:S(2)}) collective-permute-start(bf16[256,512]{1,0:T(8,128)(2,1)S(1)} %copy-done.8), channel_id=1, source_target_pairs={{0,6},{2,0},{4,2},{6,4},{8,14},{10,8},{12,10},{14,12},{16,22},{18,... | collective-permute-start | bytes 786440 | tf_op jit(solution)/shard_map/ppermute | solution.py:50
  30.8 46.4 %collective-permute-start.15 = (bf16[256,256]{1,0:T(8,128)(2,1)S(1)}, bf16[256,256]{1,0:T(8,128)(2,1)S(1)}, u32[]{:S(2)}, u32[]{:S(2)}) collective-permute-start(bf16[256,256]{1,0:T(8,128)(2,1)S(1)} %get-tuple-element.36), channel_id=1, source_target_pairs={{0,6},{2,0},{4,2},{6,4},{8,14},{10,8},{12,10},{14,12},{16,22},{18,... | collective-permute-start | bytes 393224 | tf_op jit(solution)/shard_map/ppermute | solution.py:50
  77.2 17.3 %copy-start.5 = (bf16[1,256,2,1024]{3,2,1,0:T(2,128)(2,1)S(1)}, bf16[1,256,2,1024]{3,2,1,0:T(2,128)(2,1)}, u32[]{:S(2)}) copy-start(bf16[1,256,2,1024]{3,2,1,0:T(2,128)(2,1)} %param.13) | copy-start | bytes 3145732
  78.1 15.2 %collective-permute-start.16 = (bf16[4,256,256]{2,1,0:T(8,128)(2,1)}, bf16[4,256,256]{2,1,0:T(8,128)(2,1)}, u32[]{:S(2)}, u32[]{:S(2)}) collective-permute-start(bf16[4,256,256]{2,1,0:T(8,128)(2,1)} %pad_maximum_fusion.2.rest_4_), channel_id=1, source_target_pairs={{0,8},{2,10},{4,12},{6,14},{8,16},{10,18},{12,20},{14,22},{16,24},... | collective-permute-start | bytes 1572872 | tf_op jit(solution)/shard_map/ppermute | solution.py:55
  81.5 38.5 %collective-permute-start.3 = (bf16[4,256,512]{2,1,0:T(8,128)(2,1)}, bf16[4,256,512]{2,1,0:T(8,128)(2,1)}, u32[]{:S(2)}, u32[]{:S(2)}) collective-permute-start(bf16[4,256,512]{2,1,0:T(8,128)(2,1)} %pad_maximum_fusion.1.kv_ref), channel_id=1, source_target_pairs={{0,8},{2,10},{4,12},{6,14},{8,16},{10,18},{12,20},{14,22},{16,24},... | collective-permute-start | bytes 3145736 | tf_op jit(solution)/shard_map/ppermute | solution.py:55
  81.6 39.9 %collective-permute-start.4 = (bf16[4,256,512]{2,1,0:T(8,128)(2,1)}, bf16[4,256,512]{2,1,0:T(8,128)(2,1)}, u32[]{:S(2)}, u32[]{:S(2)}) collective-permute-start(bf16[4,256,512]{2,1,0:T(8,128)(2,1)} %pad_maximum_fusion.1.kv_ref), channel_id=1, source_target_pairs={{0,24},{2,26},{4,28},{6,30},{8,0},{10,2},{12,4},{14,6},{16,8},{18,... | collective-permute-start | bytes 3145736 | tf_op jit(solution)/shard_map/ppermute | solution.py:56
  84.2 50.5 %collective-permute-start.10 = (bf16[4,768,256]{2,1,0:T(8,128)(2,1)S(1)}, bf16[4,768,256]{2,1,0:T(8,128)(2,1)}, u32[]{:S(2)}, u32[]{:S(2)}) collective-permute-start(bf16[4,768,256]{2,1,0:T(8,128)(2,1)S(1)} %pad_maximum_fusion.rest_0_), channel_id=1, source_target_pairs={{0,2},{2,4},{4,6},{6,0},{8,10},{10,12},{12,14},{14,8},{16,18},{18,... | collective-permute-start | bytes 4718600 | tf_op jit(solution)/shard_map/ppermute | solution.py:55
  93.3 24.0 %collective-permute-start.18 = (bf16[4,256,256]{2,1,0:T(8,128)(2,1)}, bf16[4,256,256]{2,1,0:T(8,128)(2,1)}, u32[]{:S(2)}, u32[]{:S(2)}) collective-permute-start(bf16[4,256,256]{2,1,0:T(8,128)(2,1)} %pad_maximum_fusion.2.rest_4_), channel_id=1, source_target_pairs={{0,24},{2,26},{4,28},{6,30},{8,0},{10,2},{12,4},{14,6},{16,8},{18,... | collective-permute-start | bytes 1572872 | tf_op jit(solution)/shard_map/ppermute | solution.py:56
  117.3 48.6 %collective-permute-start.19 = (bf16[2,256,256]{2,1,0:T(8,128)(2,1)}, bf16[2,256,256]{2,1,0:T(8,128)(2,1)}, u32[]{:S(2)}, u32[]{:S(2)}) collective-permute-start(bf16[2,256,256]{2,1,0:T(8,128)(2,1)} %slice.52), channel_id=1, source_target_pairs={{0,8},{2,10},{4,12},{6,14},{8,16},{10,18},{12,20},{14,22},{16,24},... | collective-permute-start | bytes 786440 | tf_op jit(solution)/shard_map/ppermute | solution.py:57
  121.2 34.6 %collective-permute-start.5 = (bf16[2,256,512]{2,1,0:T(8,128)(2,1)S(1)}, bf16[2,256,512]{2,1,0:T(8,128)(2,1)}, u32[]{:S(2)}, u32[]{:S(2)}) collective-permute-start(bf16[2,256,512]{2,1,0:T(8,128)(2,1)S(1)} %slice.48), channel_id=1, source_target_pairs={{0,8},{2,10},{4,12},{6,14},{8,16},{10,18},{12,20},{14,22},{16,24},... | collective-permute-start | bytes 1572872 | tf_op jit(solution)/shard_map/ppermute | solution.py:57
  122.6 35.9 %collective-permute-start.6 = (bf16[2,256,512]{2,1,0:T(8,128)(2,1)S(1)}, bf16[2,256,512]{2,1,0:T(8,128)(2,1)}, u32[]{:S(2)}, u32[]{:S(2)}) collective-permute-start(bf16[2,256,512]{2,1,0:T(8,128)(2,1)S(1)} %slice.49), channel_id=1, source_target_pairs={{0,24},{2,26},{4,28},{6,30},{8,0},{10,2},{12,4},{14,6},{16,8},{18,... | collective-permute-start | bytes 1572872 | tf_op jit(solution)/shard_map/ppermute | solution.py:58
  126.2 39.6 %collective-permute-start.17 = (bf16[2,768,256]{2,1,0:T(8,128)(2,1)S(1)}, bf16[2,768,256]{2,1,0:T(8,128)(2,1)}, u32[]{:S(2)}, u32[]{:S(2)}) collective-permute-start(bf16[2,768,256]{2,1,0:T(8,128)(2,1)S(1)} %slice.51), channel_id=1, source_target_pairs={{0,6},{2,0},{4,2},{6,4},{8,14},{10,8},{12,10},{14,12},{16,22},{18,... | collective-permute-start | bytes 2359304 | tf_op jit(solution)/shard_map/ppermute | solution.py:58
  134.7 31.1 %collective-permute-start.20 = (bf16[2,256,256]{2,1,0:T(8,128)(2,1)}, bf16[2,256,256]{2,1,0:T(8,128)(2,1)S(1)}, u32[]{:S(2)}, u32[]{:S(2)}) collective-permute-start(bf16[2,256,256]{2,1,0:T(8,128)(2,1)} %slice.53), channel_id=1, source_target_pairs={{0,24},{2,26},{4,28},{6,30},{8,0},{10,2},{12,4},{14,6},{16,8},{18,... | collective-permute-start | bytes 786440 | tf_op jit(solution)/shard_map/ppermute | solution.py:58
  155.8 22.0 %collective-permute-start.12 = (bf16[2,768,256]{2,1,0:T(8,128)(2,1)}, bf16[2,768,256]{2,1,0:T(8,128)(2,1)S(1)}, u32[]{:S(2)}, u32[]{:S(2)}) collective-permute-start(bf16[2,768,256]{2,1,0:T(8,128)(2,1)} %slice.50), channel_id=1, source_target_pairs={{0,2},{2,4},{4,6},{6,0},{8,10},{10,12},{12,14},{14,8},{16,18},{18,... | collective-permute-start | bytes 2359304 | tf_op jit(solution)/shard_map/ppermute | solution.py:57
  165.8 0.7 copy-start.13
  173.5 12.3 %copy-start.11 = (s32[1,64,2,8]{1,3,2,0:T(8,128)S(1)}, s32[1,64,2,8]{1,3,2,0:T(8,128)}, u32[]{:S(2)}) copy-start(s32[1,64,2,8]{1,3,2,0:T(8,128)} %param.22) | copy-start | bytes 12292
  173.6 12.6 %copy-start.1 = (bf16[256,2048]{1,0:T(8,128)(2,1)S(1)}, bf16[256,2048]{1,0:T(8,128)(2,1)}, u32[]{:S(2)}) copy-start(bf16[256,2048]{1,0:T(8,128)(2,1)} %get-tuple-element.27.k1) | copy-start | bytes 3145732
  173.6 12.5 %collective-permute-start.22 = (bf16[256,2048]{1,0:T(8,128)(2,1)}, bf16[256,2048]{1,0:T(8,128)(2,1)S(1)}, u32[]{:S(2)}, u32[]{:S(2)}) collective-permute-start(bf16[256,2048]{1,0:T(8,128)(2,1)} %get-tuple-element.29), channel_id=1, source_target_pairs={{0,32},{32,0},{64,96},{96,64},{1,33},{33,1},{65,97},{97,65},{2,34}... | collective-permute-start | bytes 3145736 | tf_op jit(solution)/shard_map/ppermute | solution.py:568
  177.8 0.9 copy-start.12
  185.8 4.0 collective-permute-start.21
  186.0 3.8 copy-start.3
  186.1 5.7 %copy-start.2 = (bf16[256,2048]{1,0:T(8,128)(2,1)}, bf16[256,2048]{1,0:T(8,128)(2,1)S(1)}, u32[]{:S(2)}) copy-start(bf16[256,2048]{1,0:T(8,128)(2,1)S(1)} %collective-permute-done.22.g1) | copy-start | bytes 3145732
  187.0 7.6 %copy-start.6 = (bf16[1,64,2,4096]{3,2,1,0:T(2,128)(2,1)S(1)}, bf16[1,64,2,4096]{3,2,1,0:T(2,128)(2,1)}, u32[]{:S(2)}) copy-start(bf16[1,64,2,4096]{3,2,1,0:T(2,128)(2,1)} %param.19) | copy-start | bytes 3145732
  187.0 14.7 %collective-permute-start.24 = (bf16[128,2048]{1,0:T(8,128)(2,1)}, bf16[128,2048]{1,0:T(8,128)(2,1)S(1)}, u32[]{:S(2)}, u32[]{:S(2)}) collective-permute-start(bf16[128,2048]{1,0:T(8,128)(2,1)} %add_convert_fusion), channel_id=1, source_target_pairs={{0,64},{32,96},{64,0},{96,32},{1,65},{33,97},{65,1},{97,33},{2,66}... | collective-permute-start | bytes 1572872 | tf_op jit(solution)/shard_map/ppermute | solution.py:572
  191.8 21.3 %collective-permute-start.23 = (bf16[128,2048]{1,0:T(8,128)(2,1)}, bf16[128,2048]{1,0:T(8,128)(2,1)}, u32[]{:S(2)}, u32[]{:S(2)}) collective-permute-start(bf16[128,2048]{1,0:T(8,128)(2,1)} %add_convert_fusion.1), channel_id=1, source_target_pairs={{0,64},{32,96},{64,0},{96,32},{1,65},{33,97},{65,1},{97,33},{2,66}... | collective-permute-start | bytes 1572872 | tf_op jit(solution)/shard_map/ppermute | solution.py:572
  201.8 11.3 %copy-start.9 = (bf16[128,2048]{1,0:T(8,128)(2,1)}, bf16[128,2048]{1,0:T(8,128)(2,1)S(1)}, u32[]{:S(2)}) copy-start(bf16[128,2048]{1,0:T(8,128)(2,1)S(1)} %collective-permute-done.24.r1) | copy-start | bytes 1572868
  374.3 9.5 %copy-start.7 = (bf16[128,4096]{1,0:T(8,128)(2,1)S(1)}, bf16[128,4096]{1,0:T(8,128)(2,1)}, u32[]{:S(2)}) copy-start(bf16[128,4096]{1,0:T(8,128)(2,1)} %get-tuple-element.32) | copy-start | bytes 3145732
  374.3 123.5 %all-to-all-start.1 = ((bf16[64,544,128]{2,1,0:T(8,128)(2,1)}), bf16[64,544,128]{2,1,0:T(8,128)(2,1)}, u32[]{:S(2)}, u32[]{:S(2)}) async-start(bf16[64,544,128]{2,1,0:T(8,128)(2,1)} %experts.1), calls=%async_computation.1 | async-start | bytes 17825792 | tf_op jit(solution)/shard_map/all_to_all | solution.py:584
where the time goes:
time: 517 us; the launch traced here: 509 us
  waiting for transfers between devices  200 us (39%)
  blocking collectives  120 us (23%)
  Pallas kernels  96.1 us (19%)
  starting transfers between devices  63.3 us (12%)
  local copies, waits for them, and re-layouts  19 us (4%)
  other arithmetic  8.69 us (2%)
    all_to_all x1, blocking collectives, on_device(): lax.all_to_all(x, ('tensor', 'expert'), split_axis=0, concat_axis=0, tile...  120 us
    all_to_all x1, waiting for transfers between devices, on_device(): lax.all_to_all(done, ('tensor', 'expert'), split_axis=0, concat_axis=0, t...  112 us
    ppermute x9, waiting for transfers between devices, ring_four(): return [x] + [lax.ppermute(x, 'expert', move(k)) for k in (1, 2, 3)]  58.2 us
    pallas_call x1, Pallas kernels, run_experts(): pl.pallas_call(expert_kernel, grid=(8,), out_shape=jax.ShapeDtypeStruct((...  30.9 us
    ppermute x3, starting transfers between devices, ring_relay(): hi = lax.ppermute(right[half:], 'expert', move(3))  22 us
    ppermute x2, waiting for transfers between devices, on_device(): rests.append(lax.ppermute(other, 'tensor', X_SWAP))  16.9 us
    pallas_call x1, Pallas kernels, attention(): attn_call(attn_first, [Q_SPEC, table, table, pl.BlockSpec((1, HD), lambda...  15.8 us
    pallas_call x2, Pallas kernels, project(): pl.pallas_call(functools.partial(proj_kernel, part), out_shape=(jax.Shape...  14 us
  transfers between devices with their start and end apart: 26, of which 8 were waited for; matrix products, arithmetic and copies ran while one was open for 4% of the time, Pallas kernels for 9%

commit v1 on v0

--- a/solution.py
+++ b/solution.py
@@ -71,126 +71,155 @@
     for s in range(SEQ):
         k = k_ref[:, s * HD : (s + 1) * HD].astype(F32)
         k = k * lax.rsqrt(jnp.mean(k * k, axis=-1, keepdims=True) + eps_norm) * gain
-        at = 2 * s * HD
-        o_ref[:, at : at + HD] = (k * cs + pltpu.roll(k, HD // 2, 1) * sn).astype(BF)
-        o_ref[:, at + HD : at + 2 * HD] = v_ref[:, s * HD : (s + 1) * HD]
+        o_ref[s, 0:PB, :] = (k * cs + pltpu.roll(k, HD // 2, 1) * sn).astype(BF)
+        v = jnp.transpose(v_ref[:, s * HD : (s + 1) * HD].astype(F32)).astype(BF)
+        o_ref[s, PB : PB + HD, :] = v[:, :HD]
+        o_ref[s, PB + HD :, :] = v[:, HD:]
 
 
 def ready_keys(k2, v2, cs, sn, gain):
     return pl.pallas_call(
-        keys_kernel, out_shape=jax.ShapeDtypeStruct((PB, 4 * HD), BF), name="ready_keys"
+        keys_kernel, out_shape=jax.ShapeDtypeStruct((SEQ, 2 * PB, HD), BF), name="ready_keys"
     )(k2, v2, cs, sn, gain)
 
 
 C2 = HD ** (-0.5) * LOG2E
-
-
-def attn_part(q, k, v_wide, state, limit):
-    m_old, l_old, acc = state
-    s = lax.dot_general(q, k, (((1,), (1,)), ((), ())), preferred_element_type=F32)
-    if limit is not None:
-        row = lax.broadcasted_iota(jnp.int32, (PB, 1), 0)
-        s = jnp.where(limit <= row, s, neg_fill)
-    m_new = jnp.maximum(m_old, jnp.max(s, axis=-1, keepdims=True))
-    p = jnp.exp2((s - m_new) * C2).astype(BF)
-    alpha = jnp.exp2((m_old - m_new) * C2)
-    pv = jnp.dot(p, v_wide, preferred_element_type=F32)
-    return m_new, l_old * alpha + pv[:, HD : HD + 1], acc * alpha + pv[:, :HD]
-
-
-def keys_of(kv):
-    k = kv[:, :HD]
-    v = kv[:, HD : 2 * HD]
-    return k, jnp.concatenate([v, jnp.ones_like(v)], axis=1)
-
-
-def put_state(ml_ref, acc_ref, states):
-    lane = lax.broadcasted_iota(jnp.int32, (PB, HD), 1)
-    (m0, l0, a0), (m1, l1, a1) = states
-    ml_ref[...] = jnp.where(
-        lane == 0, m0, jnp.where(lane == 1, l0, jnp.where(lane == 2, m1, l1))
+VR = HD + 16
+HEADS = 8
+
+
+def attn_part(q_ref, key_of, val_of, load, save, s_buf, mask):
+    ones = jnp.ones((16, PB), BF)
+
+    def score(h, j):
+        q = q_ref[:, pl.ds(pl.multiple_of(h * HD, HD), HD)]
+        s = lax.dot_general(key_of(j), q, (((1,), (1,)), ((), ())), preferred_element_type=F32)
+        return s if mask is None else mask(j, s)
+
+    top = None
+    for j in range(4):
+        s = score(0, j)
+        s_buf[0, j] = s
+        part = jnp.max(s, axis=0, keepdims=True)
+        top = part if j == 0 else jnp.maximum(top, part)
+
+    def body(h, top):
+        slot = h & 1
+        m_old, acc = load(h)
+        m_new = jnp.maximum(m_old, top)
+        mc = m_new * C2
+        acc = acc * jnp.exp2(m_old * C2 - mc)
+        nxt = None
+        for j in range(4):
+            s = score((h + 1) & (HEADS - 1), j)
+            p = jnp.exp2(s_buf[slot, j] * C2 - mc).astype(BF)
+            s_buf[1 - slot, j] = s
+            part = jnp.max(s, axis=0, keepdims=True)
+            nxt = part if j == 0 else jnp.maximum(nxt, part)
+            acc = acc + jnp.dot(
+                jnp.concatenate([val_of(j), ones], axis=0), p, preferred_element_type=F32
+            )
+        save(h, m_new, acc)
+        return nxt
+
+    lax.fori_loop(0, HEADS, body, top)
+
+
+def block_keys(kv_ref):
+    return (
+        lambda j: kv_ref[j, 0, 0:PB, :],
+        lambda j: jnp.concatenate(
+            [kv_ref[j, 0, PB : PB + HD, :], kv_ref[j, 0, PB + HD :, :]], axis=1
+        ),
     )
-    acc_ref[:, :HD] = a0
-    acc_ref[:, HD:] = a1
-
-
-def get_state(ml_ref, acc_ref):
-    return [
-        (ml_ref[:, 2 * h : 2 * h + 1], ml_ref[:, 2 * h + 1 : 2 * h + 2],
-         acc_ref[:, h * HD : (h + 1) * HD])
-        for h in range(2)
-    ]
-
-
-def attn_first(sc, q_ref, cos_ref, sin_ref, gain_ref, kv_ref, qr_ref, ml_ref, acc_ref):
+
+
+def attn_first(sc, q_ref, cos_ref, sin_ref, gain_ref, kv_ref, qr_ref, m_ref, acc_ref, s_buf):
     y = sc[3]
     cs, sn, gain = cos_ref[...], sin_ref[...], gain_ref[...]
-    k, v = keys_of(kv_ref[...].reshape(1024, 256))
-    key = lax.broadcasted_iota(jnp.int32, (1, 1024), 1)
-    ahead = key >> 8
-    limit = jnp.where(ahead == 0, key & 255, jnp.where(ahead <= y, -1, PB))
-    states = []
-    for h in range(2):
+    for h in range(HEADS):
         q = q_ref[:, h * HD : (h + 1) * HD].astype(F32)
         q = q * lax.rsqrt(jnp.mean(q * q, axis=-1, keepdims=True) + eps_norm) * gain
-        q = (q * cs + pltpu.roll(q, HD // 2, 1) * sn).astype(BF)
-        qr_ref[:, h * HD : (h + 1) * HD] = q
-        start = (
-            jnp.full((PB, 1), neg_fill, F32),
-            jnp.zeros((PB, 1), F32),
-            jnp.zeros((PB, HD), F32),
-        )
-        states.append(attn_part(q, k, v, start, limit))
-    put_state(ml_ref, acc_ref, states)
-
-
-def attn_next(sc, q_ref, ml_in, acc_in, ka_ref, kb_ref, ml_ref, acc_ref):
+        qr_ref[:, h * HD : (h + 1) * HD] = (q * cs + pltpu.roll(q, HD // 2, 1) * sn).astype(BF)
+
+    def mask(j, s):
+        if j > 0:
+            return s + jnp.where(j <= y, 0.0, neg_fill)
+        key = lax.broadcasted_iota(jnp.int32, (PB, PB), 0)
+        row = lax.broadcasted_iota(jnp.int32, (PB, PB), 1)
+        return jnp.where(key <= row, s, neg_fill)
+
+    def load(h):
+        return jnp.full((1, PB), neg_fill, F32), jnp.zeros((VR, PB), F32)
+
+    def save(h, m, acc):
+        m_ref[h] = jnp.broadcast_to(m, (8, PB))
+        acc_ref[h] = acc
+
+    key_of, val_of = block_keys(kv_ref)
+    attn_part(qr_ref, key_of, val_of, load, save, s_buf, mask)
+
+
+def attn_next(sc, q_ref, m_in, acc_in, ka_ref, kb_ref, m_ref, acc_ref, s_buf):
     z = sc[2]
-    ml_ref[...] = ml_in[...]
-    acc_ref[...] = acc_in[...]
-    for need, kv_ref in ((1, ka_ref), (3, kb_ref)):
+
+    @pl.when(z == 0)
+    def _():
+        m_ref[...] = m_in[...]
+        acc_ref[...] = acc_in[...]
+
+    for need, kv_ref, m_from, acc_from in ((1, ka_ref, m_in, acc_in), (3, kb_ref, m_ref, acc_ref)):
 
         @pl.when(z >= need)
-        def _(kv_ref=kv_ref):
-            k, v = keys_of(kv_ref[...].reshape(1024, 256))
-            states = [
-                attn_part(q_ref[:, h * HD : (h + 1) * HD], k, v, st, None)
-                for h, st in enumerate(get_state(ml_ref, acc_ref))
-            ]
-            put_state(ml_ref, acc_ref, states)
-
-
-def attn_last(sc, q_ref, ml_in, acc_in, ka_ref, kb_ref, o_ref):
+        def _(kv_ref=kv_ref, m_from=m_from, acc_from=acc_from):
+            def load(h):
+                return m_from[h, 0:1, :], acc_from[h]
+
+            def save(h, m, acc):
+                m_ref[h] = jnp.broadcast_to(m, (8, PB))
+                acc_ref[h] = acc
+
+            key_of, val_of = block_keys(kv_ref)
+            attn_part(q_ref, key_of, val_of, load, save, s_buf, None)
+
+
+def attn_last(sc, q_ref, m_in, acc_in, ka_ref, kb_ref, o_ref, s_buf):
     z = sc[2]
 
-    def finish(states):
-        for h, (_, total, acc) in enumerate(states):
-            o_ref[:, h * HD : (h + 1) * HD] = (acc / total).astype(BF)
+    def finish(h, acc):
+        out = jnp.transpose(acc[:HD] / acc[HD : HD + 1])
+        o_ref[:, pl.ds(pl.multiple_of(h * HD, HD), HD)] = out.astype(BF)
 
     @pl.when(z >= 2)
     def _():
-        kv = jnp.concatenate(
-            [ka_ref[...].reshape(512, 256), kb_ref[...].reshape(512, 256)], axis=0
-        )
-        k, v = keys_of(kv)
-        finish(
-            [
-                attn_part(q_ref[:, h * HD : (h + 1) * HD], k, v, st, None)
-                for h, st in enumerate(get_state(ml_in, acc_in))
-            ]
+        ka, va = block_keys(ka_ref)
+        kb, vb = block_keys(kb_ref)
+        attn_part(
+            q_ref,
+            lambda j: ka(j) if j < 2 else kb(j - 2),
+            lambda j: va(j) if j < 2 else vb(j - 2),
+            lambda h: (m_in[h, 0:1, :], acc_in[h]),
+            lambda h, m, acc: finish(h, acc),
+            s_buf,
+            None,
         )
 
     @pl.when(z < 2)
     def _():
-        finish(get_state(ml_in, acc_in))
-
-
-Q_SPEC = pl.BlockSpec((PB, 256), lambda i, sc: (0, i))
-ML_SPEC = pl.BlockSpec((PB, HD), lambda i, sc: (0, i))
+        def body(h, _):
+            finish(h, acc_in[h])
+            return 0
+
+        lax.fori_loop(0, HEADS, body, 0)
+
+
+Q_SPEC = pl.BlockSpec((PB, 1024), lambda i, sc: (0, i))
+M_SPEC = pl.BlockSpec((HEADS, 8, PB), lambda i, sc: (i, 0, 0))
+A_SPEC = pl.BlockSpec((HEADS, VR, PB), lambda i, sc: (i, 0, 0))
 
 
 def kv_spec(n):
-    return pl.BlockSpec((n, PB, 256), lambda i, sc: (0, 0, i // 4))
+    return pl.BlockSpec((n, 1, 2 * PB, HD), lambda i, sc: (0, i, 0, 0))
 
 
 def attn_call(kernel, in_specs, out_specs, out_shape, parts):
@@ -198,7 +227,11 @@
         kernel,
         out_shape=out_shape,
         grid_spec=pltpu.PrefetchScalarGridSpec(
-            num_scalar_prefetch=1, grid=(8,), in_specs=in_specs, out_specs=out_specs
+            num_scalar_prefetch=1,
+            grid=(SEQ,),
+            in_specs=in_specs,
+            out_specs=out_specs,
+            scratch_shapes=[pltpu.VMEM((2, 4, PB, PB), F32)],
         ),
         compiler_params=pltpu.CompilerParams(vmem_limit_bytes=VMEM_BIG),
         cost_estimate=pl.CostEstimate(
@@ -208,31 +241,31 @@
 
 
 STATE = (
-    jax.ShapeDtypeStruct((PB, 8 * HD), F32),
-    jax.ShapeDtypeStruct((PB, SEQ * 1024), F32),
+    jax.ShapeDtypeStruct((SEQ * HEADS, 8, PB), F32),
+    jax.ShapeDtypeStruct((SEQ * HEADS, VR, PB), F32),
 )
 
 
 def attention(scal, q2, cs, sn, gain, pieces):
     own, left, right, lo, hi = pieces
     table = pl.BlockSpec((PB, HD), lambda i, sc: (0, 0))
-    qr, ml, acc = attn_call(
+    qr, m, acc = attn_call(
         attn_first,
         [Q_SPEC, table, table, pl.BlockSpec((1, HD), lambda i, sc: (0, 0)), kv_spec(4)],
-        (Q_SPEC, ML_SPEC, Q_SPEC),
+        (Q_SPEC, M_SPEC, A_SPEC),
         (jax.ShapeDtypeStruct((PB, SEQ * 1024), BF),) + STATE,
         1,
     )(scal, q2, cs, sn, gain, own)
-    ml, acc = attn_call(
-        attn_next, [Q_SPEC, ML_SPEC, Q_SPEC, kv_spec(4), kv_spec(4)], (ML_SPEC, Q_SPEC), STATE, 2
-    )(scal, qr, ml, acc, left, right)
+    m, acc = attn_call(
+        attn_next, [Q_SPEC, M_SPEC, A_SPEC, kv_spec(4), kv_spec(4)], (M_SPEC, A_SPEC), STATE, 2
+    )(scal, qr, m, acc, left, right)
     return attn_call(
         attn_last,
-        [Q_SPEC, ML_SPEC, Q_SPEC, kv_spec(2), kv_spec(2)],
+        [Q_SPEC, M_SPEC, A_SPEC, kv_spec(2), kv_spec(2)],
         Q_SPEC,
         jax.ShapeDtypeStruct((PB, SEQ * 1024), BF),
         1,
-    )(scal, qr, ml, acc, lo, hi)
+    )(scal, qr, m, acc, lo, hi)
 
 
 WA = 768
@@ -260,18 +293,19 @@
             (w_in[6], w.at[0, pl.ds(2, 2), low]),
         ]
     copies = [pltpu.make_async_copy(a, b, sem.at[i]) for i, (a, b) in enumerate(moves)]
-    for cp in copies:
+    for cp in copies[4:] + copies[:4]:
         cp.start()
-    for cc in range(2):
+    for cc in (1, 0):
         for xx in range(2):
             base = pl.multiple_of(64 * (2 * (xh ^ xx) + (c ^ cc)), 64)
             for s in range(SEQ):
                 at = cc * 256 + xx * 128 + s * 64
                 lhs[at : at + 64, :] = a_ref[pl.ds(base, 64), s * 1024 : (s + 1) * 1024]
-    for cp in copies:
+    for cp in copies[4:]:
         cp.wait()
-    for i in range(2):
-        for dy in range(4):
+    for cp, dy in zip(copies[:4], (0, 1, 3, 2)):
+        cp.wait()
+        for i in range(2):
             res = jnp.dot(lhs[...], w[i, dy], preferred_element_type=F32).astype(BF)
             lane = (i * 4 + dy) * 256
             keep[:, lane : lane + 256] = res[:256]

time: 517 us -> 511 us (0.988)
  Pallas kernels: 96.1 us -> 87.3 us
    pallas_call x3, Pallas kernels: 17.4 us -> 11.5 us  [the longest x1 4.86 us: attention(): attn_call(attn_last, [Q_SPEC, M_SPEC, A_SPEC, kv_spec(2), kv_spec(2)], Q_...]
  transfers between devices with their start and end apart: 26 -> 26, of which waited for: 8 -> 8; matrix products, arithmetic and copies ran while one was open for 4% -> 4% of each run, Pallas kernels for 9% -> 7%
where the time goes in v1:
time: 511 us; the launch traced here: 502 us
  waiting for transfers between devices  203 us (40%)
  blocking collectives  120 us (23%)
  Pallas kernels  87.3 us (17%)
  starting transfers between devices  62.4 us (12%)
  local copies, waits for them, and re-layouts  19 us (4%)
  other arithmetic  8.72 us (2%)
    all_to_all x1, blocking collectives, on_device(): lax.all_to_all(x, ('tensor', 'expert'), split_axis=0, concat_axis=0, tile...  120 us
    all_to_all x1, waiting for transfers between devices, on_device(): lax.all_to_all(done, ('tensor', 'expert'), split_axis=0, concat_axis=0, t...  112 us
    ppermute x9, waiting for transfers between devices, ring_four(): return [x] + [lax.ppermute(x, 'expert', move(k)) for k in (1, 2, 3)]  58.2 us
    pallas_call x1, Pallas kernels, run_experts(): pl.pallas_call(expert_kernel, grid=(8,), out_shape=jax.ShapeDtypeStruct((...  30.9 us
    ppermute x3, starting transfers between devices, ring_relay(): hi = lax.ppermute(right[half:], 'expert', move(3))  20.1 us
    ppermute x2, waiting for transfers between devices, on_device(): rests.append(lax.ppermute(other, 'tensor', X_SWAP))  17.7 us
    pallas_call x2, Pallas kernels, project(): pl.pallas_call(functools.partial(proj_kernel, part), out_shape=(jax.Shape...  13.7 us
    pallas_call x1, Pallas kernels, attention(): attn_call(attn_first, [Q_SPEC, table, table, pl.BlockSpec((1, HD), lambda...  13.2 us
  transfers between devices with their start and end apart: 26, of which 8 were waited for; matrix products, arithmetic and copies ran while one was open for 4% of the time, Pallas kernels for 7%

profile of v1, /device:TPU:25, one launch (start us, length us, event | category | flops | bytes accessed | tf_op | source)
XLA Modules:
  0.0 501.7 jit_solution(16315961933119902099)
XLA Ops:
  0.0 0.5 fusion.2
  0.6 1.7 copy_bitcast_fusion
  2.3 0.9 pad_maximum_fusion.3
  3.1 2.2 ready_keys.1
  5.4 1.7 collective-permute-start.7
  7.1 3.3 collective-permute-start.8
  10.4 0.7 collective-permute-start.9
  11.3 2.2 collective-permute-start.14
  13.5 4.6 collective-permute-done.7
  18.1 9.3 %collective-permute-done.8 = bf16[768,256]{1,0:T(8,128)(2,1)S(1)} collective-permute-done((bf16[768,256]{1,0:T(8,128)(2,1)S(1)}, bf16[768,256]{1,0:T(8,128)(2,1)S(1)}, u32[]{:S(2)}, u32[]{:S(2)}) %collective-permute-start.8) | collective-permute-done | bytes 393248 | tf_op jit(solution)/shard_map/ppermute | solution.py:50
  27.6 0.5 collective-permute-start.11
  28.1 0.2 copy-done.8
  28.3 2.0 collective-permute-start
  30.4 0.2 collective-permute-start.1
  30.6 0.3 collective-permute-start.2
  30.9 2.1 collective-permute-start.15
  33.0 44.3 %collective-permute-done.15 = bf16[256,256]{1,0:T(8,128)(2,1)S(1)} collective-permute-done((bf16[256,256]{1,0:T(8,128)(2,1)S(1)}, bf16[256,256]{1,0:T(8,128)(2,1)S(1)}, u32[]{:S(2)}, u32[]{:S(2)}) %collective-permute-start.15) | collective-permute-done | bytes 131104 | tf_op jit(solution)/shard_map/ppermute | solution.py:50
  77.4 0.9 pad_maximum_fusion.2.rest_4_
  78.2 2.3 collective-permute-start.16
  80.5 1.1 pad_maximum_fusion.1.kv_ref
  81.7 2.7 collective-permute-start.4
  84.3 9.1 %collective-permute-done.16.rest_5_ = bf16[4,256,256]{2,1,0:T(8,128)(2,1)} collective-permute-done((bf16[4,256,256]{2,1,0:T(8,128)(2,1)}, bf16[4,256,256]{2,1,0:T(8,128)(2,1)}, u32[]{:S(2)}, u32[]{:S(2)}) %collective-permute-start.16) | collective-permute-done | bytes 524320 | tf_op jit(solution)/shard_map/ppermute | solution.py:55
  93.4 1.2 collective-permute-start.18
  94.6 1.2 copy.48
  95.9 0.7 pad_add_fusion.sc
  96.5 13.2 %shard_map.127 = (bf16[256,2048]{1,0:T(8,128)(2,1)}, f32[16,8,256]{2,1,0:T(8,128)}, f32[16,144,256]{2,1,0:T(8,128)}) custom-call(s32[4]{0:T(128)} %pad_add_fusion.sc, bf16[256,2048]{1,0:T(8,128)(2,1)} %bitcast.59, f32[256,128]{1,0:T(8,128)} %get-tuple-element.42.cos_ref, f32[256,128]{1,0:T(8,128)} %get-tuple-element.43.sin_ref, f32[1,128]{1,0:T(1,128)} %bitcast.78, ...), custom_call_target="tpu_custom_call" | custom-call | flops 4294967296 | bytes 8388608 | tf_op jit(solution)/shard_map/pallas_call | solution.py:252
  109.7 1.7 slice.52
  111.4 6.0 %collective-permute-done.18.rest_4_ = bf16[4,256,256]{2,1,0:T(8,128)(2,1)} collective-permute-done((bf16[4,256,256]{2,1,0:T(8,128)(2,1)}, bf16[4,256,256]{2,1,0:T(8,128)(2,1)}, u32[]{:S(2)}, u32[]{:S(2)}) %collective-permute-start.18) | collective-permute-done | bytes 524320 | tf_op jit(solution)/shard_map/ppermute | solution.py:56
  117.4 1.2 collective-permute-start.19
  118.5 1.7 slice.53
  120.2 1.1 slice.48
  121.3 0.3 collective-permute-start.5
  121.6 1.1 slice.49
  122.7 2.5 collective-permute-start.6
  125.2 1.2 slice.51
  126.4 4.4 shard_map.128
  130.9 17.6 %collective-permute-start.20 = (bf16[2,256,256]{2,1,0:T(8,128)(2,1)}, bf16[2,256,256]{2,1,0:T(8,128)(2,1)S(1)}, u32[]{:S(2)}, u32[]{:S(2)}) collective-permute-start(bf16[2,256,256]{2,1,0:T(8,128)(2,1)} %slice.53), channel_id=1, source_target_pairs={{0,24},{2,26},{4,28},{6,30},{8,0},{10,2},{12,4},{14,6},{16,8},{18,... | collective-permute-start | bytes 786440 | tf_op jit(solution)/shard_map/ppermute | solution.py:58
  148.4 2.1 slice.50
  150.5 2.6 collective-permute-start.12
  153.2 4.9 shard_map.129.a_ref
  158.0 0.7 copy-done.13
  158.7 6.9 %shard_map.131 = (bf16[256,2048]{1,0:T(8,128)(2,1)}, bf16[256,2048]{1,0:T(8,128)(2,1)}) custom-call(s32[4]{0:T(128)} %pad_add_fusion.sc, bf16[256,2048]{1,0:T(8,128)(2,1)} %shard_map.129.a_ref, bf16[4,768,256]{2,1,0:T(8,128)(2,1)} %copy-done.4, bf16[4,768,256]{2,1,0:T(8,128)(2,1)} %collective-permute-done.10.rest_1_, ...), custom_call_target="tpu_custom_call" | custom-call | flops 2147483648 | bytes 7340032 | tf_op jit(solution)/shard_map/pallas_call | solution.py:319
  165.7 4.2 collective-permute-start.22
  169.9 0.9 copy-done.12
  170.8 6.8 %shard_map.130 = (bf16[256,2048]{1,0:T(8,128)(2,1)}, bf16[256,2048]{1,0:T(8,128)(2,1)}) custom-call(s32[4]{0:T(128)} %pad_add_fusion.sc, bf16[256,2048]{1,0:T(8,128)(2,1)} %shard_map.129.a_ref, bf16[4,768,256]{2,1,0:T(8,128)(2,1)} %copy-done.4, bf16[4,768,256]{2,1,0:T(8,128)(2,1)} %collective-permute-done.10.rest_1_, ...), custom_call_target="tpu_custom_call" | custom-call | flops 2147483648 | bytes 7340032 | tf_op jit(solution)/shard_map/pallas_call | solution.py:319
  177.6 1.4 collective-permute-start.21
  179.3 0.9 add_convert_fusion
  180.2 2.7 collective-permute-start.24
  183.0 2.0 add_convert_fusion.1
  185.0 1.4 collective-permute-start.23
  186.8 0.7 reshape.48.tgt_ref
  187.5 1.6 copy.38
  189.0 6.4 %collective-permute-done.24.r1 = bf16[128,2048]{1,0:T(8,128)(2,1)S(1)} collective-permute-done((bf16[128,2048]{1,0:T(8,128)(2,1)}, bf16[128,2048]{1,0:T(8,128)(2,1)S(1)}, u32[]{:S(2)}, u32[]{:S(2)}) %collective-permute-start.24) | collective-permute-done | bytes 524320 | tf_op jit(solution)/shard_map/ppermute | solution.py:606
  195.4 11.3 %collective-permute-done.23.r0 = bf16[128,2048]{1,0:T(8,128)(2,1)} collective-permute-done((bf16[128,2048]{1,0:T(8,128)(2,1)}, bf16[128,2048]{1,0:T(8,128)(2,1)}, u32[]{:S(2)}, u32[]{:S(2)}) %collective-permute-start.23) | collective-permute-done | bytes 524320 | tf_op jit(solution)/shard_map/ppermute | solution.py:606
  206.8 9.8 %dispatch.1 = (bf16[128,4096]{1,0:T(8,128)(2,1)}, bf16[128,4096]{1,0:T(8,128)(2,1)}, bf16[64,544,128]{2,1,0:T(8,128)(2,1)}) custom-call(s32[4]{0:T(128)} %pad_add_fusion.sc, bf16[256,2048]{1,0:T(8,128)(2,1)} %get-tuple-element.26.k0, bf16[256,2048]{1,0:T(8,128)(2,1)} %get-tuple-element.27.k1, bf16[256,2048]{1,0:T(8,128)(2,1)} %collective-permute-done.21.g0, ...), custom_call_target="tpu_custom_call" | custom-call | flops 1073741824 | bytes 14680064 | tf_op jit(solution)/shard_map/dispatch/pallas_call | solution.py:383
  216.6 119.8 %all_to_all.10.x_ref.xo_ref = bf16[64,544,128]{2,1,0:T(8,128)(2,1)} all-to-all(bf16[64,544,128]{2,1,0:T(8,128)(2,1)} %get-tuple-element.30), channel_id=1, replica_groups=mesh['tensor'=4,'expert'=16,'dp'=2] {'tensor','expert'}, dimensions={0} | all-to-all | bytes 17825792 | tf_op jit(solution)/shard_map/all_to_all | solution.py:610
  336.3 30.9 %experts.1 = bf16[64,544,128]{2,1,0:T(8,128)(2,1)} custom-call(bf16[64,544,128]{2,1,0:T(8,128)(2,1)} %all_to_all.10.x_ref.xo_ref, bf16[64,544,128]{2,1,0:T(8,128)(2,1)} %all_to_all.10.x_ref.xo_ref, bf16[1,4096,768]{2,1,0:T(8,128)(2,1)} %wg_ref.1, bf16[1,4096,768]{2,1,0:T(8,128)(2,1)} %wu_ref.1, bf16[1,768,4096]{2,1,0:T(8,128)(2,1)} %wd_ref.1), custom_call_target="tpu_custom_call" | custom-call | flops 21474836480 | bytes 37748736 | tf_op jit(solution)/shard_map/experts/pallas_call | solution.py:469
  367.2 8.8 %all-to-all-start.1 = ((bf16[64,544,128]{2,1,0:T(8,128)(2,1)}), bf16[64,544,128]{2,1,0:T(8,128)(2,1)}, u32[]{:S(2)}, u32[]{:S(2)}) async-start(bf16[64,544,128]{2,1,0:T(8,128)(2,1)} %experts.1), calls=%async_computation.1 | async-start | bytes 17825792 | tf_op jit(solution)/shard_map/all_to_all | solution.py:618
  376.1 0.6 add_select_fusion.tgt_ref
  376.7 0.5 fusion.5
  377.7 0.7 broadcast_divide_fusion.gate_ref
  378.4 112.3 %all-to-all-done.1.y_ref.yo_ref = bf16[64,544,128]{2,1,0:T(8,128)(2,1)} async-done(((bf16[64,544,128]{2,1,0:T(8,128)(2,1)}), bf16[64,544,128]{2,1,0:T(8,128)(2,1)}, u32[]{:S(2)}, u32[]{:S(2)}) %all-to-all-start.1) | async-done | bytes 8912928 | tf_op jit(solution)/shard_map/all_to_all | solution.py:618
  490.7 8.2 %combine.1 = bf16[128,4096]{1,0:T(8,128)(2,1)} custom-call(bf16[64,544,128]{2,1,0:T(8,128)(2,1)} %all-to-all-done.1.y_ref.yo_ref, bf16[64,544,128]{2,1,0:T(8,128)(2,1)} %all-to-all-done.1.y_ref.yo_ref, bf16[128,4096]{1,0:T(8,128)(2,1)} %get-tuple-element.31.st_ref, s32[128,8]{1,0:T(8,128)} %add_select_fusion.tgt_ref, f32[128,8]{1,0:T(8,128)} %broadcast_divide_fusion.gate_ref), custom_call_target="tpu_custom_call" | custom-call | flops 2147483648 | bytes 11534336 | tf_op jit(solution)/shard_map/combine/pallas_call | solution.py:529
  498.9 2.5 reshape.50
  (69 shorter events, 1.6 us)
Async XLA Ops:
  0.0 376.7 %copy-start = (bf16[4096,64]{0,1:T(8,128)(2,1)S(1)}, bf16[4096,64]{0,1:T(8,128)(2,1)}, u32[]{:S(2)}) copy-start(bf16[4096,64]{0,1:T(8,128)(2,1)} %param.21) | copy-start | bytes 1572868
  0.0 5.4 %copy-start.10 = (bf16[1024,256]{1,0:T(8,128)(2,1)S(1)}, bf16[1024,256]{1,0:T(8,128)(2,1)}, u32[]{:S(2)}) copy-start(bf16[1024,256]{1,0:T(8,128)(2,1)} %param.18) | copy-start | bytes 1572868
  5.4 12.6 %collective-permute-start.7 = (bf16[768,256]{1,0:T(8,128)(2,1)S(1)}, bf16[768,256]{1,0:T(8,128)(2,1)S(1)}, u32[]{:S(2)}, u32[]{:S(2)}) collective-permute-start(bf16[768,256]{1,0:T(8,128)(2,1)S(1)} %get-tuple-element.38), channel_id=1, source_target_pairs={{0,8},{2,10},{4,12},{6,14},{8,16},{10,18},{12,20},{14,22},{16,24},... | collective-permute-start | bytes 1179656 | tf_op jit(solution)/shard_map/ppermute | solution.py:50
  7.1 20.3 %collective-permute-start.8 = (bf16[768,256]{1,0:T(8,128)(2,1)S(1)}, bf16[768,256]{1,0:T(8,128)(2,1)S(1)}, u32[]{:S(2)}, u32[]{:S(2)}) collective-permute-start(bf16[768,256]{1,0:T(8,128)(2,1)S(1)} %get-tuple-element.38), channel_id=1, source_target_pairs={{0,16},{2,18},{4,20},{6,22},{8,24},{10,26},{12,28},{14,30},{16,0},... | collective-permute-start | bytes 1179656 | tf_op jit(solution)/shard_map/ppermute | solution.py:50
  10.4 17.0 %collective-permute-start.9 = (bf16[768,256]{1,0:T(8,128)(2,1)S(1)}, bf16[768,256]{1,0:T(8,128)(2,1)S(1)}, u32[]{:S(2)}, u32[]{:S(2)}) collective-permute-start(bf16[768,256]{1,0:T(8,128)(2,1)S(1)} %get-tuple-element.38), channel_id=1, source_target_pairs={{0,24},{2,26},{4,28},{6,30},{8,0},{10,2},{12,4},{14,6},{16,8},{18,... | collective-permute-start | bytes 1179656 | tf_op jit(solution)/shard_map/ppermute | solution.py:50
  11.2 19.4 %collective-permute-start.13 = (bf16[256,256]{1,0:T(8,128)(2,1)S(1)}, bf16[256,256]{1,0:T(8,128)(2,1)S(1)}, u32[]{:S(2)}, u32[]{:S(2)}) collective-permute-start(bf16[256,256]{1,0:T(8,128)(2,1)S(1)} %get-tuple-element.36), channel_id=1, source_target_pairs={{0,2},{2,4},{4,6},{6,0},{8,10},{10,12},{12,14},{14,8},{16,18},{18,... | collective-permute-start | bytes 393224 | tf_op jit(solution)/shard_map/ppermute | solution.py:50
  11.3 19.7 %collective-permute-start.14 = (bf16[256,256]{1,0:T(8,128)(2,1)S(1)}, bf16[256,256]{1,0:T(8,128)(2,1)S(1)}, u32[]{:S(2)}, u32[]{:S(2)}) collective-permute-start(bf16[256,256]{1,0:T(8,128)(2,1)S(1)} %get-tuple-element.36), channel_id=1, source_target_pairs={{0,4},{2,6},{4,0},{6,2},{8,12},{10,14},{12,8},{14,10},{16,20},{18,... | collective-permute-start | bytes 393224 | tf_op jit(solution)/shard_map/ppermute | solution.py:50
  27.4 1.0 copy-start.8
  27.6 56.7 %copy-start.4 = (bf16[4,768,256]{2,1,0:T(8,128)(2,1)}, bf16[4,768,256]{2,1,0:T(8,128)(2,1)S(1)}, u32[]{:S(2)}) copy-start(bf16[4,768,256]{2,1,0:T(8,128)(2,1)S(1)} %pad_maximum_fusion.rest_0_) | copy-start | bytes 4718596
  27.6 97.6 %collective-permute-start.11 = (bf16[4,768,256]{2,1,0:T(8,128)(2,1)S(1)}, bf16[4,768,256]{2,1,0:T(8,128)(2,1)}, u32[]{:S(2)}, u32[]{:S(2)}) collective-permute-start(bf16[4,768,256]{2,1,0:T(8,128)(2,1)S(1)} %pad_maximum_fusion.rest_0_), channel_id=1, source_target_pairs={{0,6},{2,0},{4,2},{6,4},{8,14},{10,8},{12,10},{14,12},{16,22},{18,... | collective-permute-start | bytes 4718600 | tf_op jit(solution)/shard_map/ppermute | solution.py:56
  28.3 52.2 %collective-permute-start = (bf16[2,512,128]{2,1,0:T(8,128)(2,1)S(1)}, bf16[2,512,128]{2,1,0:T(8,128)(2,1)S(1)}, u32[]{:S(2)}, u32[]{:S(2)}) collective-permute-start(bf16[2,512,128]{2,1,0:T(8,128)(2,1)S(1)} %copy-done.8), channel_id=1, source_target_pairs={{0,2},{2,4},{4,6},{6,0},{8,10},{10,12},{12,14},{14,8},{16,18},{18,... | collective-permute-start | bytes 786440 | tf_op jit(solution)/shard_map/ppermute | solution.py:50
  30.4 50.2 %collective-permute-start.1 = (bf16[2,512,128]{2,1,0:T(8,128)(2,1)S(1)}, bf16[2,512,128]{2,1,0:T(8,128)(2,1)S(1)}, u32[]{:S(2)}, u32[]{:S(2)}) collective-permute-start(bf16[2,512,128]{2,1,0:T(8,128)(2,1)S(1)} %copy-done.8), channel_id=1, source_target_pairs={{0,4},{2,6},{4,0},{6,2},{8,12},{10,14},{12,8},{14,10},{16,20},{18,... | collective-permute-start | bytes 786440 | tf_op jit(solution)/shard_map/ppermute | solution.py:50
  30.6 49.9 %collective-permute-start.2 = (bf16[2,512,128]{2,1,0:T(8,128)(2,1)S(1)}, bf16[2,512,128]{2,1,0:T(8,128)(2,1)S(1)}, u32[]{:S(2)}, u32[]{:S(2)}) collective-permute-start(bf16[2,512,128]{2,1,0:T(8,128)(2,1)S(1)} %copy-done.8), channel_id=1, source_target_pairs={{0,6},{2,0},{4,2},{6,4},{8,14},{10,8},{12,10},{14,12},{16,22},{18,... | collective-permute-start | bytes 786440 | tf_op jit(solution)/shard_map/ppermute | solution.py:50
  30.9 46.4 %collective-permute-start.15 = (bf16[256,256]{1,0:T(8,128)(2,1)S(1)}, bf16[256,256]{1,0:T(8,128)(2,1)S(1)}, u32[]{:S(2)}, u32[]{:S(2)}) collective-permute-start(bf16[256,256]{1,0:T(8,128)(2,1)S(1)} %get-tuple-element.36), channel_id=1, source_target_pairs={{0,6},{2,0},{4,2},{6,4},{8,14},{10,8},{12,10},{14,12},{16,22},{18,... | collective-permute-start | bytes 393224 | tf_op jit(solution)/shard_map/ppermute | solution.py:50
  77.3 17.3 %copy-start.5 = (bf16[1,256,2,1024]{3,2,1,0:T(2,128)(2,1)S(1)}, bf16[1,256,2,1024]{3,2,1,0:T(2,128)(2,1)}, u32[]{:S(2)}) copy-start(bf16[1,256,2,1024]{3,2,1,0:T(2,128)(2,1)} %param.13) | copy-start | bytes 3145732
  78.2 15.2 %collective-permute-start.16 = (bf16[4,256,256]{2,1,0:T(8,128)(2,1)}, bf16[4,256,256]{2,1,0:T(8,128)(2,1)}, u32[]{:S(2)}, u32[]{:S(2)}) collective-permute-start(bf16[4,256,256]{2,1,0:T(8,128)(2,1)} %pad_maximum_fusion.2.rest_4_), channel_id=1, source_target_pairs={{0,8},{2,10},{4,12},{6,14},{8,16},{10,18},{12,20},{14,22},{16,24},... | collective-permute-start | bytes 1572872 | tf_op jit(solution)/shard_map/ppermute | solution.py:55
  81.6 38.5 %collective-permute-start.3 = (bf16[4,2,512,128]{3,2,1,0:T(8,128)(2,1)}, bf16[4,2,512,128]{3,2,1,0:T(8,128)(2,1)}, u32[]{:S(2)}, u32[]{:S(2)}) collective-permute-start(bf16[4,2,512,128]{3,2,1,0:T(8,128)(2,1)} %pad_maximum_fusion.1.kv_ref), channel_id=1, source_target_pairs={{0,8},{2,10},{4,12},{6,14},{8,16},{10,18},{12,20},{14,22},{16,24},... | collective-permute-start | bytes 3145736 | tf_op jit(solution)/shard_map/ppermute | solution.py:55
  81.7 39.9 %collective-permute-start.4 = (bf16[4,2,512,128]{3,2,1,0:T(8,128)(2,1)}, bf16[4,2,512,128]{3,2,1,0:T(8,128)(2,1)}, u32[]{:S(2)}, u32[]{:S(2)}) collective-permute-start(bf16[4,2,512,128]{3,2,1,0:T(8,128)(2,1)} %pad_maximum_fusion.1.kv_ref), channel_id=1, source_target_pairs={{0,24},{2,26},{4,28},{6,30},{8,0},{10,2},{12,4},{14,6},{16,8},{18,... | collective-permute-start | bytes 3145736 | tf_op jit(solution)/shard_map/ppermute | solution.py:56
  84.3 46.5 %collective-permute-start.10 = (bf16[4,768,256]{2,1,0:T(8,128)(2,1)S(1)}, bf16[4,768,256]{2,1,0:T(8,128)(2,1)}, u32[]{:S(2)}, u32[]{:S(2)}) collective-permute-start(bf16[4,768,256]{2,1,0:T(8,128)(2,1)S(1)} %pad_maximum_fusion.rest_0_), channel_id=1, source_target_pairs={{0,2},{2,4},{4,6},{6,0},{8,10},{10,12},{12,14},{14,8},{16,18},{18,... | collective-permute-start | bytes 4718600 | tf_op jit(solution)/shard_map/ppermute | solution.py:55
  93.4 24.0 %collective-permute-start.18 = (bf16[4,256,256]{2,1,0:T(8,128)(2,1)}, bf16[4,256,256]{2,1,0:T(8,128)(2,1)}, u32[]{:S(2)}, u32[]{:S(2)}) collective-permute-start(bf16[4,256,256]{2,1,0:T(8,128)(2,1)} %pad_maximum_fusion.2.rest_4_), channel_id=1, source_target_pairs={{0,24},{2,26},{4,28},{6,30},{8,0},{10,2},{12,4},{14,6},{16,8},{18,... | collective-permute-start | bytes 1572872 | tf_op jit(solution)/shard_map/ppermute | solution.py:56
  117.4 40.7 %collective-permute-start.19 = (bf16[2,256,256]{2,1,0:T(8,128)(2,1)}, bf16[2,256,256]{2,1,0:T(8,128)(2,1)}, u32[]{:S(2)}, u32[]{:S(2)}) collective-permute-start(bf16[2,256,256]{2,1,0:T(8,128)(2,1)} %slice.52), channel_id=1, source_target_pairs={{0,8},{2,10},{4,12},{6,14},{8,16},{10,18},{12,20},{14,22},{16,24},... | collective-permute-start | bytes 786440 | tf_op jit(solution)/shard_map/ppermute | solution.py:57
  121.3 29.2 %collective-permute-start.5 = (bf16[2,2,512,128]{3,2,1,0:T(8,128)(2,1)S(1)}, bf16[2,2,512,128]{3,2,1,0:T(8,128)(2,1)}, u32[]{:S(2)}, u32[]{:S(2)}) collective-permute-start(bf16[2,2,512,128]{3,2,1,0:T(8,128)(2,1)S(1)} %slice.48), channel_id=1, source_target_pairs={{0,8},{2,10},{4,12},{6,14},{8,16},{10,18},{12,20},{14,22},{16,24},... | collective-permute-start | bytes 1572872 | tf_op jit(solution)/shard_map/ppermute | solution.py:57
  122.7 30.5 %collective-permute-start.6 = (bf16[2,2,512,128]{3,2,1,0:T(8,128)(2,1)S(1)}, bf16[2,2,512,128]{3,2,1,0:T(8,128)(2,1)}, u32[]{:S(2)}, u32[]{:S(2)}) collective-permute-start(bf16[2,2,512,128]{3,2,1,0:T(8,128)(2,1)S(1)} %slice.49), channel_id=1, source_target_pairs={{0,24},{2,26},{4,28},{6,30},{8,0},{10,2},{12,4},{14,6},{16,8},{18,... | collective-permute-start | bytes 1572872 | tf_op jit(solution)/shard_map/ppermute | solution.py:58
  126.4 31.7 %collective-permute-start.17 = (bf16[2,768,256]{2,1,0:T(8,128)(2,1)S(1)}, bf16[2,768,256]{2,1,0:T(8,128)(2,1)}, u32[]{:S(2)}, u32[]{:S(2)}) collective-permute-start(bf16[2,768,256]{2,1,0:T(8,128)(2,1)S(1)} %slice.51), channel_id=1, source_target_pairs={{0,6},{2,0},{4,2},{6,4},{8,14},{10,8},{12,10},{14,12},{16,22},{18,... | collective-permute-start | bytes 2359304 | tf_op jit(solution)/shard_map/ppermute | solution.py:58
  130.9 27.2 %collective-permute-start.20 = (bf16[2,256,256]{2,1,0:T(8,128)(2,1)}, bf16[2,256,256]{2,1,0:T(8,128)(2,1)S(1)}, u32[]{:S(2)}, u32[]{:S(2)}) collective-permute-start(bf16[2,256,256]{2,1,0:T(8,128)(2,1)} %slice.53), channel_id=1, source_target_pairs={{0,24},{2,26},{4,28},{6,30},{8,0},{10,2},{12,4},{14,6},{16,8},{18,... | collective-permute-start | bytes 786440 | tf_op jit(solution)/shard_map/ppermute | solution.py:58
  150.5 19.4 %collective-permute-start.12 = (bf16[2,768,256]{2,1,0:T(8,128)(2,1)}, bf16[2,768,256]{2,1,0:T(8,128)(2,1)S(1)}, u32[]{:S(2)}, u32[]{:S(2)}) collective-permute-start(bf16[2,768,256]{2,1,0:T(8,128)(2,1)} %slice.50), channel_id=1, source_target_pairs={{0,2},{2,4},{4,6},{6,0},{8,10},{10,12},{12,14},{14,8},{16,18},{18,... | collective-permute-start | bytes 2359304 | tf_op jit(solution)/shard_map/ppermute | solution.py:57
  158.0 0.7 copy-start.13
  165.6 13.4 %copy-start.11 = (s32[1,64,2,8]{1,3,2,0:T(8,128)S(1)}, s32[1,64,2,8]{1,3,2,0:T(8,128)}, u32[]{:S(2)}) copy-start(s32[1,64,2,8]{1,3,2,0:T(8,128)} %param.22) | copy-start | bytes 12292
  165.7 13.6 %copy-start.1 = (bf16[256,2048]{1,0:T(8,128)(2,1)S(1)}, bf16[256,2048]{1,0:T(8,128)(2,1)}, u32[]{:S(2)}) copy-start(bf16[256,2048]{1,0:T(8,128)(2,1)} %get-tuple-element.27.k1) | copy-start | bytes 3145732
  165.7 13.6 %collective-permute-start.22 = (bf16[256,2048]{1,0:T(8,128)(2,1)}, bf16[256,2048]{1,0:T(8,128)(2,1)S(1)}, u32[]{:S(2)}, u32[]{:S(2)}) collective-permute-start(bf16[256,2048]{1,0:T(8,128)(2,1)} %get-tuple-element.29), channel_id=1, source_target_pairs={{0,32},{32,0},{64,96},{96,64},{1,33},{33,1},{65,97},{97,65},{2,34}... | collective-permute-start | bytes 3145736 | tf_op jit(solution)/shard_map/ppermute | solution.py:602
  169.9 0.9 copy-start.12
  177.6 5.3 %collective-permute-start.21 = (bf16[256,2048]{1,0:T(8,128)(2,1)}, bf16[256,2048]{1,0:T(8,128)(2,1)}, u32[]{:S(2)}, u32[]{:S(2)}) collective-permute-start(bf16[256,2048]{1,0:T(8,128)(2,1)} %get-tuple-element.28), channel_id=1, source_target_pairs={{0,32},{32,0},{64,96},{96,64},{1,33},{33,1},{65,97},{97,65},{2,34}... | collective-permute-start | bytes 3145736 | tf_op jit(solution)/shard_map/ppermute | solution.py:602
  179.2 3.8 copy-start.3
  179.3 5.7 %copy-start.2 = (bf16[256,2048]{1,0:T(8,128)(2,1)}, bf16[256,2048]{1,0:T(8,128)(2,1)S(1)}, u32[]{:S(2)}) copy-start(bf16[256,2048]{1,0:T(8,128)(2,1)S(1)} %collective-permute-done.22.g1) | copy-start | bytes 3145732
  180.2 7.2 %copy-start.6 = (bf16[1,64,2,4096]{3,2,1,0:T(2,128)(2,1)S(1)}, bf16[1,64,2,4096]{3,2,1,0:T(2,128)(2,1)}, u32[]{:S(2)}) copy-start(bf16[1,64,2,4096]{3,2,1,0:T(2,128)(2,1)} %param.19) | copy-start | bytes 3145732
  180.2 15.2 %collective-permute-start.24 = (bf16[128,2048]{1,0:T(8,128)(2,1)}, bf16[128,2048]{1,0:T(8,128)(2,1)S(1)}, u32[]{:S(2)}, u32[]{:S(2)}) collective-permute-start(bf16[128,2048]{1,0:T(8,128)(2,1)} %add_convert_fusion), channel_id=1, source_target_pairs={{0,64},{32,96},{64,0},{96,32},{1,65},{33,97},{65,1},{97,33},{2,66}... | collective-permute-start | bytes 1572872 | tf_op jit(solution)/shard_map/ppermute | solution.py:606
  185.0 21.8 %collective-permute-start.23 = (bf16[128,2048]{1,0:T(8,128)(2,1)}, bf16[128,2048]{1,0:T(8,128)(2,1)}, u32[]{:S(2)}, u32[]{:S(2)}) collective-permute-start(bf16[128,2048]{1,0:T(8,128)(2,1)} %add_convert_fusion.1), channel_id=1, source_target_pairs={{0,64},{32,96},{64,0},{96,32},{1,65},{33,97},{65,1},{97,33},{2,66}... | collective-permute-start | bytes 1572872 | tf_op jit(solution)/shard_map/ppermute | solution.py:606
  195.4 11.3 %copy-start.9 = (bf16[128,2048]{1,0:T(8,128)(2,1)}, bf16[128,2048]{1,0:T(8,128)(2,1)S(1)}, u32[]{:S(2)}) copy-start(bf16[128,2048]{1,0:T(8,128)(2,1)S(1)} %collective-permute-done.24.r1) | copy-start | bytes 1572868
  367.2 9.5 %copy-start.7 = (bf16[128,4096]{1,0:T(8,128)(2,1)S(1)}, bf16[128,4096]{1,0:T(8,128)(2,1)}, u32[]{:S(2)}) copy-start(bf16[128,4096]{1,0:T(8,128)(2,1)} %get-tuple-element.32) | copy-start | bytes 3145732
  367.2 123.5 %all-to-all-start.1 = ((bf16[64,544,128]{2,1,0:T(8,128)(2,1)}), bf16[64,544,128]{2,1,0:T(8,128)(2,1)}, u32[]{:S(2)}, u32[]{:S(2)}) async-start(bf16[64,544,128]{2,1,0:T(8,128)(2,1)} %experts.1), calls=%async_computation.1 | async-start | bytes 17825792 | tf_op jit(solution)/shard_map/all_to_all | solution.py:618

commit v2 on v1

--- a/solution.py
+++ b/solution.py
@@ -268,32 +268,18 @@
     )(scal, qr, m, acc, lo, hi)
 
 
-WA = 768
-WB = 1024 - WA
-
-
 def proj_kernel(part, sc, a_ref, *rest):
-    n_in = 6 if part == 0 else 7
-    w_in, (keep, send, lhs, w, sem) = rest[:n_in], rest[n_in:]
+    w_in, (keep, send, lhs, w, sem) = rest[:4], rest[4:]
     c, xh = sc[0], sc[1]
-    top, low = pl.ds(0, WA), pl.ds(WA, WB)
     two = pl.ds(2 * part, 2)
     moves = [
-        (w_in[0].at[two], w.at[:, 0, top]),
-        (w_in[1].at[two], w.at[:, 1, top]),
-        (w_in[2].at[two], w.at[:, 3, top]),
-        (w_in[3], w.at[:, 2, top]),
+        (w_in[0].at[two], w.at[:, 0]),
+        (w_in[1].at[two], w.at[:, 1]),
+        (w_in[2].at[two], w.at[:, 3]),
+        (w_in[3], w.at[:, 2]),
     ]
-    if part == 0:
-        moves += [(w_in[4], w.at[0, :, low]), (w_in[5], w.at[1, :, low])]
-    else:
-        moves += [
-            (w_in[4], w.at[1, :, low]),
-            (w_in[5], w.at[0, pl.ds(0, 2), low]),
-            (w_in[6], w.at[0, pl.ds(2, 2), low]),
-        ]
     copies = [pltpu.make_async_copy(a, b, sem.at[i]) for i, (a, b) in enumerate(moves)]
-    for cp in copies[4:] + copies[:4]:
+    for cp in copies:
         cp.start()
     for cc in (1, 0):
         for xx in range(2):
@@ -301,9 +287,7 @@
             for s in range(SEQ):
                 at = cc * 256 + xx * 128 + s * 64
                 lhs[at : at + 64, :] = a_ref[pl.ds(base, 64), s * 1024 : (s + 1) * 1024]
-    for cp in copies[4:]:
-        cp.wait()
-    for cp, dy in zip(copies[:4], (0, 1, 3, 2)):
+    for cp, dy in zip(copies, (0, 1, 3, 2)):
         cp.wait()
         for i in range(2):
             res = jnp.dot(lhs[...], w[i, dy], preferred_element_type=F32).astype(BF)
@@ -312,9 +296,8 @@
             send[:, lane : lane + 256] = res[256:]
 
 
-def project(part, scal, attn, pa, pb):
+def project(part, scal, attn, pa):
     pieces = list(pa[:3]) + [pa[3 + part]]
-    pieces += [pb[0], pb[1]] if part == 0 else [pb[2], pb[3], pb[4]]
     full = pl.BlockSpec(memory_space=pltpu.VMEM)
     return pl.pallas_call(
         functools.partial(proj_kernel, part),
@@ -328,7 +311,7 @@
         scratch_shapes=[
             pltpu.VMEM((512, 1024), BF),
             pltpu.VMEM((2, 4, 1024, 256), BF),
-            pltpu.SemaphoreType.DMA((8,)),
+            pltpu.SemaphoreType.DMA((4,)),
         ],
         compiler_params=pltpu.CompilerParams(vmem_limit_bytes=VMEM_BIG),
         cost_estimate=pl.CostEstimate(
@@ -338,7 +321,7 @@
 
 
 def dispatch_kernel(
-    sc, k0, k1, g0, g1, r0, r1, h_ref, gain_ref, tgt_ref, st_ref, nm_ref, x_ref
+    sc, k0, k1, g0, g1, r0, r1, h_ref, gain_ref, tgt_ref, st_ref, nm_ref, x_hbm, x_ref, sem
 ):
     z, y = sc[2], sc[3]
     square = jnp.zeros((ROWS, 1), F32)
@@ -364,6 +347,14 @@
     for k in range(TOP):
         hit = jnp.where(line == tgt_ref[k : k + 1, :], 1.0, hit)
     pick = hit.astype(BF)
+    copies = [
+        pltpu.make_async_copy(
+            x_ref.at[:, pl.ds(j * 64, 64 if j < 8 else 32)],
+            x_hbm.at[:, pl.ds(j * 64, 64 if j < 8 else 32)],
+            sem.at[j],
+        )
+        for j in range(9)
+    ]
     for j in range(8):
         n = nm_ref[:, j * 512 : (j + 1) * 512]
         main = jnp.dot(pick[:NMAIN], n, preferred_element_type=F32).astype(BF)
@@ -372,8 +363,12 @@
             x_ref[:, f * SLOT : (f + 1) * SLOT, :] = main[:, i * 128 : (i + 1) * 128].reshape(
                 NE, SLOT, 128
             )
+        copies[j].start()
     ov = jnp.dot(pick[NMAIN:], nm_ref[...], preferred_element_type=F32).astype(BF)
     x_ref[:, 512:544, :] = ov.reshape(NE, 32, 128)
+    copies[8].start()
+    for cp in copies:
+        cp.wait()
 
 
 def dispatch(scal, keeps, gots, rests, hid, gain, tgt_t):
@@ -392,7 +387,8 @@
             grid=(1,),
             in_specs=[half] * 6
             + [line, pl.BlockSpec((1, DM), at), pl.BlockSpec((TOP, ROWS), at)],
-            out_specs=(line, line, pl.BlockSpec((NE, XR, 128), lambda i, sc: (0, 0, 0))),
+            out_specs=(line, line, pl.BlockSpec(memory_space=pl.ANY)),
+            scratch_shapes=[pltpu.VMEM((NE, XR, 128), BF), pltpu.SemaphoreType.DMA((9,))],
         ),
         compiler_params=pltpu.CompilerParams(vmem_limit_bytes=VMEM_BIG),
         cost_estimate=pl.CostEstimate(
@@ -495,28 +491,43 @@
     )(x, x, wg, wu, wd)
 
 
-def combine_kernel(y_ref, yo_ref, st_ref, tgt_ref, gate_ref, o_ref, gm, go, yov):
+def mix_kernel(tgt_ref, gate_ref, gm, go):
+    lane = lax.broadcasted_iota(jnp.int32, (ROWS, NALL), 1)
+    mix = jnp.zeros((ROWS, NALL), F32)
+    for k in range(TOP):
+        mix = jnp.where(lane == tgt_ref[:, k : k + 1], gate_ref[:, k : k + 1], mix)
+    hi = mix.astype(BF)
+    lo = (mix - hi.astype(F32)).astype(BF)
+    gm[:ROWS] = hi[:, :NMAIN]
+    gm[ROWS:] = lo[:, :NMAIN]
+    go[:ROWS] = hi[:, NMAIN:]
+    go[ROWS:] = lo[:, NMAIN:]
+
+
+def mixing(tgt, gates):
+    return pl.pallas_call(
+        mix_kernel,
+        out_shape=(
+            jax.ShapeDtypeStruct((2 * ROWS, NMAIN), BF),
+            jax.ShapeDtypeStruct((2 * ROWS, NE), BF),
+        ),
+        cost_estimate=pl.CostEstimate(flops=2**22, bytes_accessed=2**20, transcendentals=0),
+        name="mixing",
+    )(tgt, gates)
+
+
+def combine_kernel(y_ref, yo_ref, st_ref, gm_ref, go_ref, o_ref, yov):
     step = pl.program_id(0)
 
     @pl.when(step == 0)
     def _():
         yov[...] = yo_ref[...].reshape(NE, DM)
-        lane = lax.broadcasted_iota(jnp.int32, (ROWS, NALL), 1)
-        mix = jnp.zeros((ROWS, NALL), F32)
-        for k in range(TOP):
-            mix = jnp.where(lane == tgt_ref[:, k : k + 1], gate_ref[:, k : k + 1], mix)
-        hi = mix.astype(BF)
-        lo = (mix - hi.astype(F32)).astype(BF)
-        gm[:ROWS] = hi[:, :NMAIN]
-        gm[ROWS:] = lo[:, :NMAIN]
-        go[:ROWS] = hi[:, NMAIN:]
-        go[ROWS:] = lo[:, NMAIN:]
 
     pieces = [y_ref[:, i * SLOT : (i + 1) * SLOT, :].reshape(NMAIN, 128) for i in range(8)]
     main = jnp.concatenate(pieces, axis=1)
     at = pl.multiple_of(step * 1024, 1024)
-    both = jnp.dot(gm[...], main, preferred_element_type=F32) + jnp.dot(
-        go[...], yov[:, pl.ds(at, 1024)], preferred_element_type=F32
+    both = jnp.dot(gm_ref[...], main, preferred_element_type=F32) + jnp.dot(
+        go_ref[...], yov[:, pl.ds(at, 1024)], preferred_element_type=F32
     )
     r = lax.broadcasted_iota(jnp.int32, (ROWS, ROWS), 0)
     c = lax.broadcasted_iota(jnp.int32, (ROWS, ROWS), 1)
@@ -525,7 +536,7 @@
     o_ref[...] = (st + (both[:ROWS] + both[ROWS:])).astype(BF)
 
 
-def combine(y, stream, tgt, gates):
+def combine(y, stream, gm, go):
     return pl.pallas_call(
         combine_kernel,
         grid=(4,),
@@ -534,21 +545,17 @@
             pl.BlockSpec((NE, 128, 128), lambda i: (0, i, 0)),
             pl.BlockSpec((NE, 32, 128), lambda i: (0, 16, 0)),
             pl.BlockSpec((ROWS, 1024), lambda i: (0, i)),
-            pl.BlockSpec((ROWS, TOP), lambda i: (0, 0)),
-            pl.BlockSpec((ROWS, TOP), lambda i: (0, 0)),
+            pl.BlockSpec((2 * ROWS, NMAIN), lambda i: (0, 0)),
+            pl.BlockSpec((2 * ROWS, NE), lambda i: (0, 0)),
         ],
         out_specs=pl.BlockSpec((ROWS, 1024), lambda i: (0, i)),
-        scratch_shapes=[
-            pltpu.VMEM((2 * ROWS, NMAIN), BF),
-            pltpu.VMEM((2 * ROWS, NE), BF),
-            pltpu.VMEM((NE, DM), BF),
-        ],
+        scratch_shapes=[pltpu.VMEM((NE, DM), BF)],
         compiler_params=pltpu.CompilerParams(vmem_limit_bytes=VMEM_BIG),
         cost_estimate=pl.CostEstimate(
             flops=2 * 2**30, bytes_accessed=11 * 2**20, transcendentals=0
         ),
         name="combine",
-    )(y, y, stream, tgt, gates)
+    )(y, y, stream, gm, go)
 
 
 def slots(ids):
@@ -584,10 +591,8 @@
     kv = ready_keys(
         keys[0].reshape(PB, SEQ * HD), values[0].reshape(PB, SEQ * HD), cs, sn, k_gain.reshape(1, HD)
     )
-    kv, weight = lax.optimization_barrier((kv, out_weight))
     kv_all = ring_relay(jnp.stack(ring_four(kv, y_move)), z_move)
-    wa_all = ring_relay(jnp.stack(ring_four(weight[:WA], z_move)), y_move)
-    wb_all = ring_relay(jnp.stack(ring_four(weight[WA:], y_move)), z_move)
+    w_all = ring_relay(jnp.stack(ring_four(out_weight, z_move)), y_move)
 
     q2 = queries[0].reshape(PB, SEQ * 1024)
     ids = expert_ids[0].reshape(ROWS, TOP)
@@ -598,7 +603,7 @@
     attn = attention(scal, q2, cs, sn, q_gain.reshape(1, HD), kv_all)
     keeps, gots, rests = [], [], []
     for part in range(2):
-        keep, send = project(part, scal, attn, wa_all, wb_all)
+        keep, send = project(part, scal, attn, w_all)
         got = lax.ppermute(send, "tensor", CORE_SWAP)
         other = (keep[128:].astype(F32) + got[128:].astype(F32)).astype(BF)
         keeps.append(keep)
@@ -616,7 +621,7 @@
 
     done = run_experts(arrived, w_gate, w_up, w_down)
     back = lax.all_to_all(done, ("tensor", "expert"), split_axis=0, concat_axis=0, tiled=True)
-    out = combine(back, stream, tgt, gates)
+    out = combine(back, stream, *mixing(tgt, gates))
     return out.reshape(hidden_in.shape)
 
 

time: 511 us -> 495 us (0.969)
  the two profiles are of different devices: /device:TPU:25 before, /device:TPU:45 now
where the time goes in v2:
time: 495 us; the launch traced here: 493 us
  waiting for transfers between devices  205 us (41%)
  blocking collectives  128 us (26%)
  Pallas kernels  95.8 us (19%)
  starting transfers between devices  37 us (7%)
  local copies, waits for them, and re-layouts  16.2 us (3%)
  other arithmetic  10.5 us (2%)
    all_to_all x1, blocking collectives, on_device(): lax.all_to_all(x, ('tensor', 'expert'), split_axis=0, concat_axis=0, tile...  128 us
    all_to_all x1, waiting for transfers between devices, on_device(): lax.all_to_all(done, ('tensor', 'expert'), split_axis=0, concat_axis=0, t...  108 us
    ppermute x6, waiting for transfers between devices, ring_four(): return [x] + [lax.ppermute(x, 'expert', move(k)) for k in (1, 2, 3)]  69.4 us
    pallas_call x1, Pallas kernels, run_experts(): pl.pallas_call(expert_kernel, grid=(8,), out_shape=jax.ShapeDtypeStruct((...  30.8 us
    ppermute x2, waiting for transfers between devices, on_device(): rests.append(lax.ppermute(other, 'tensor', X_SWAP))  18.4 us
    all_to_all x1, starting transfers between devices, on_device(): lax.all_to_all(done, ('tensor', 'expert'), split_axis=0, concat_axis=0, t...  14.1 us
    pallas_call x2, Pallas kernels, project(): pl.pallas_call(functools.partial(proj_kernel, part), out_shape=(jax.Shape...  13.2 us
    pallas_call x1, Pallas kernels, attention(): attn_call(attn_first, [Q_SPEC, table, table, pl.BlockSpec((1, HD), lambda...  13.2 us
  transfers between devices with their start and end apart: 19, of which 11 were waited for; matrix products, arithmetic and copies ran while one was open for 5% of the time, Pallas kernels for 10%

profile of v2, /device:TPU:45, one launch (start us, length us, event | category | flops | bytes accessed | tf_op | source)
XLA Modules:
  0.0 492.8 jit_solution(1019269142949002545)
XLA Ops:
  0.0 1.6 collective-permute-start.7
  1.6 1.1 collective-permute-start.8
  2.8 2.0 collective-permute-start.9
  4.8 8.2 %collective-permute-done.7 = bf16[1024,256]{1,0:T(8,128)(2,1)S(1)} collective-permute-done((bf16[1024,256]{1,0:T(8,128)(2,1)}, bf16[1024,256]{1,0:T(8,128)(2,1)S(1)}, u32[]{:S(2)}, u32[]{:S(2)}) %collective-permute-start.7) | collective-permute-done | bytes 524320 | tf_op jit(solution)/shard_map/ppermute | solution.py:50
  13.0 3.0 collective-permute-done.8
  16.0 11.7 %collective-permute-done.9 = bf16[1024,256]{1,0:T(8,128)(2,1)S(1)} collective-permute-done((bf16[1024,256]{1,0:T(8,128)(2,1)}, bf16[1024,256]{1,0:T(8,128)(2,1)S(1)}, u32[]{:S(2)}, u32[]{:S(2)}) %collective-permute-start.9) | collective-permute-done | bytes 524320 | tf_op jit(solution)/shard_map/ppermute | solution.py:50
  27.7 0.8 copy-done.8
  28.5 1.7 pad_maximum_fusion.rest_0_
  30.2 0.2 collective-permute-start.11
  30.4 1.3 collective-permute-start.10
  31.7 0.5 fusion.2
  32.3 0.8 pad_maximum_fusion.2
  33.1 0.7 copy_bitcast_fusion
  33.9 2.2 ready_keys.1
  36.1 1.3 collective-permute-start
  37.4 1.9 collective-permute-start.1
  39.3 2.1 collective-permute-start.2
  41.4 42.4 %collective-permute-done = bf16[2,512,128]{2,1,0:T(8,128)(2,1)S(1)} collective-permute-done((bf16[2,512,128]{2,1,0:T(8,128)(2,1)}, bf16[2,512,128]{2,1,0:T(8,128)(2,1)S(1)}, u32[]{:S(2)}, u32[]{:S(2)}) %collective-permute-start) | collective-permute-done | bytes 262176 | tf_op jit(solution)/shard_map/ppermute | solution.py:50
  83.8 4.1 collective-permute-done.2
  87.8 2.1 pad_maximum_fusion.1.kv_ref
  89.9 1.5 collective-permute-start.4
  91.4 2.5 copy.48
  93.8 0.6 pad_add_fusion.sc
  94.5 13.2 %shard_map.127 = (bf16[256,2048]{1,0:T(8,128)(2,1)}, f32[16,8,256]{2,1,0:T(8,128)}, f32[16,144,256]{2,1,0:T(8,128)}) custom-call(s32[4]{0:T(128)} %pad_add_fusion.sc, bf16[256,2048]{1,0:T(8,128)(2,1)} %bitcast.53, f32[256,128]{1,0:T(8,128)} %get-tuple-element.38.cos_ref, f32[256,128]{1,0:T(8,128)} %get-tuple-element.39.sin_ref, f32[1,128]{1,0:T(1,128)} %bitcast.70, ...), custom_call_target="tpu_custom_call" | custom-call | flops 4294967296 | bytes 8388608 | tf_op jit(solution)/shard_map/pallas_call | solution.py:252
  107.6 5.6 %collective-permute-done.3.ka_ref = bf16[4,2,512,128]{3,2,1,0:T(8,128)(2,1)} collective-permute-done((bf16[4,2,512,128]{3,2,1,0:T(8,128)(2,1)}, bf16[4,2,512,128]{3,2,1,0:T(8,128)(2,1)}, u32[]{:S(2)}, u32[]{:S(2)}) %collective-permute-start.3) | collective-permute-done | bytes 1048608 | tf_op jit(solution)/shard_map/ppermute | solution.py:55
  113.2 1.1 slice.32
  114.3 0.7 collective-permute-start.5
  115.1 1.1 slice.33
  116.1 1.5 collective-permute-start.6
  117.6 2.3 slice.35
  120.0 1.6 collective-permute-start.13
  121.5 2.3 slice.34
  123.8 1.0 collective-permute-start.12
  124.8 12.4 %shard_map.128 = (f32[16,8,256]{2,1,0:T(8,128)}, f32[16,144,256]{2,1,0:T(8,128)}) custom-call(s32[4]{0:T(128)} %pad_add_fusion.sc, bf16[256,2048]{1,0:T(8,128)(2,1)} %get-tuple-element.19.q_ref, f32[16,8,256]{2,1,0:T(8,128)} %get-tuple-element.20.m_in, f32[16,144,256]{2,1,0:T(8,128)} %get-tuple-element.21.acc_in, ...), custom_call_target="tpu_custom_call" | custom-call | flops 8589934592 | bytes 8388608 | tf_op jit(solution)/shard_map/pallas_call | solution.py:259
  137.2 4.9 shard_map.129.a_ref
  142.1 1.9 collective-permute-done.13.rest_3_
  143.9 6.7 %shard_map.131 = (bf16[256,2048]{1,0:T(8,128)(2,1)}, bf16[256,2048]{1,0:T(8,128)(2,1)}) custom-call(s32[4]{0:T(128)} %pad_add_fusion.sc, bf16[256,2048]{1,0:T(8,128)(2,1)} %shard_map.129.a_ref, bf16[4,1024,256]{2,1,0:T(8,128)(2,1)} %copy-done.1, bf16[4,1024,256]{2,1,0:T(8,128)(2,1)} %collective-permute-done.10.rest_1_, ...), custom_call_target="tpu_custom_call" | custom-call | flops 2147483648 | bytes 7340032 | tf_op jit(solution)/shard_map/pallas_call | solution.py:302
  150.6 3.2 collective-permute-start.15
  153.8 6.6 %shard_map.130 = (bf16[256,2048]{1,0:T(8,128)(2,1)}, bf16[256,2048]{1,0:T(8,128)(2,1)}) custom-call(s32[4]{0:T(128)} %pad_add_fusion.sc, bf16[256,2048]{1,0:T(8,128)(2,1)} %shard_map.129.a_ref, bf16[4,1024,256]{2,1,0:T(8,128)(2,1)} %copy-done.1, bf16[4,1024,256]{2,1,0:T(8,128)(2,1)} %collective-permute-done.10.rest_1_, ...), custom_call_target="tpu_custom_call" | custom-call | flops 2147483648 | bytes 7340032 | tf_op jit(solution)/shard_map/pallas_call | solution.py:302
  160.4 0.2 collective-permute-start.14
  160.5 0.1 copy.39
  160.8 1.1 add_convert_fusion
  161.9 0.2 collective-permute-start.17
  162.1 1.4 collective-permute-done.14.g0
  163.4 2.1 add_convert_fusion.1
  165.6 1.4 collective-permute-start.16
  167.0 0.1 fusion.1
  167.2 0.1 copy.41
  167.4 0.7 reshape.48.tgt_ref
  168.0 1.6 copy.38
  169.6 7.0 %collective-permute-done.17.r1 = bf16[128,2048]{1,0:T(8,128)(2,1)S(1)} collective-permute-done((bf16[128,2048]{1,0:T(8,128)(2,1)}, bf16[128,2048]{1,0:T(8,128)(2,1)S(1)}, u32[]{:S(2)}, u32[]{:S(2)}) %collective-permute-start.17) | collective-permute-done | bytes 524320 | tf_op jit(solution)/shard_map/ppermute | solution.py:611
  176.6 11.3 %collective-permute-done.16.r0 = bf16[128,2048]{1,0:T(8,128)(2,1)} collective-permute-done((bf16[128,2048]{1,0:T(8,128)(2,1)}, bf16[128,2048]{1,0:T(8,128)(2,1)}, u32[]{:S(2)}, u32[]{:S(2)}) %collective-permute-start.16) | collective-permute-done | bytes 524320 | tf_op jit(solution)/shard_map/ppermute | solution.py:611
  188.0 9.1 %dispatch.1 = (bf16[128,4096]{1,0:T(8,128)(2,1)}, bf16[128,4096]{1,0:T(8,128)(2,1)}, bf16[64,544,128]{2,1,0:T(8,128)(2,1)}) custom-call(s32[4]{0:T(128)} %pad_add_fusion.sc, bf16[256,2048]{1,0:T(8,128)(2,1)} %get-tuple-element.24.k0, bf16[256,2048]{1,0:T(8,128)(2,1)} %get-tuple-element.25.k1, bf16[256,2048]{1,0:T(8,128)(2,1)} %collective-permute-done.14.g0, ...), custom_call_target="tpu_custom_call" | custom-call | flops 1073741824 | bytes 14680064 | tf_op jit(solution)/shard_map/dispatch/pallas_call | solution.py:378
  197.1 127.7 %all_to_all.10.x_ref.xo_ref = bf16[64,544,128]{2,1,0:T(8,128)(2,1)} all-to-all(bf16[64,544,128]{2,1,0:T(8,128)(2,1)} %get-tuple-element.28), channel_id=1, replica_groups=mesh['tensor'=4,'expert'=16,'dp'=2] {'tensor','expert'}, dimensions={0} | all-to-all | bytes 17825792 | tf_op jit(solution)/shard_map/all_to_all | solution.py:615
  324.7 30.8 %experts.1 = bf16[64,544,128]{2,1,0:T(8,128)(2,1)} custom-call(bf16[64,544,128]{2,1,0:T(8,128)(2,1)} %all_to_all.10.x_ref.xo_ref, bf16[64,544,128]{2,1,0:T(8,128)(2,1)} %all_to_all.10.x_ref.xo_ref, bf16[1,4096,768]{2,1,0:T(8,128)(2,1)} %wg_ref.1, bf16[1,4096,768]{2,1,0:T(8,128)(2,1)} %wu_ref.1, bf16[1,768,4096]{2,1,0:T(8,128)(2,1)} %wd_ref.1), custom_call_target="tpu_custom_call" | custom-call | flops 21474836480 | bytes 37748736 | tf_op jit(solution)/shard_map/experts/pallas_call | solution.py:465
  355.6 14.1 %all-to-all-start.1 = ((bf16[64,544,128]{2,1,0:T(8,128)(2,1)}), bf16[64,544,128]{2,1,0:T(8,128)(2,1)}, u32[]{:S(2)}, u32[]{:S(2)}) async-start(bf16[64,544,128]{2,1,0:T(8,128)(2,1)} %experts.1), calls=%async_computation.1 | async-start | bytes 17825792 | tf_op jit(solution)/shard_map/all_to_all | solution.py:623
  369.7 0.6 add_select_fusion.tgt_ref
  370.4 0.5 fusion.5
  371.2 0.1 copy.47
  371.3 0.7 broadcast_divide_fusion.gate_ref
  372.1 2.6 mixing.1
  374.7 108.2 %all-to-all-done.1.y_ref.yo_ref = bf16[64,544,128]{2,1,0:T(8,128)(2,1)} async-done(((bf16[64,544,128]{2,1,0:T(8,128)(2,1)}), bf16[64,544,128]{2,1,0:T(8,128)(2,1)}, u32[]{:S(2)}, u32[]{:S(2)}) %all-to-all-start.1) | async-done | bytes 8912928 | tf_op jit(solution)/shard_map/all_to_all | solution.py:623
  482.8 7.4 %combine.1 = bf16[128,4096]{1,0:T(8,128)(2,1)} custom-call(bf16[64,544,128]{2,1,0:T(8,128)(2,1)} %all-to-all-done.1.y_ref.yo_ref, bf16[64,544,128]{2,1,0:T(8,128)(2,1)} %all-to-all-done.1.y_ref.yo_ref, bf16[128,4096]{1,0:T(8,128)(2,1)} %get-tuple-element.29.st_ref, bf16[256,1024]{1,0:T(8,128)(2,1)} %get-tuple-element.31.gm_ref, ...), custom_call_target="tpu_custom_call" | custom-call | flops 2147483648 | bytes 11534336 | tf_op jit(solution)/shard_map/combine/pallas_call | solution.py:540
  490.3 2.5 reshape.50
  (47 shorter events, 0.7 us)
Async XLA Ops:
  0.0 370.4 %copy-start = (bf16[4096,64]{0,1:T(8,128)(2,1)S(1)}, bf16[4096,64]{0,1:T(8,128)(2,1)}, u32[]{:S(2)}) copy-start(bf16[4096,64]{0,1:T(8,128)(2,1)} %param.21) | copy-start | bytes 1572868
  0.0 13.0 %collective-permute-start.7 = (bf16[1024,256]{1,0:T(8,128)(2,1)}, bf16[1024,256]{1,0:T(8,128)(2,1)S(1)}, u32[]{:S(2)}, u32[]{:S(2)}) collective-permute-start(bf16[1024,256]{1,0:T(8,128)(2,1)} %param.18), channel_id=1, source_target_pairs={{0,8},{2,10},{4,12},{6,14},{8,16},{10,18},{12,20},{14,22},{16,24},... | collective-permute-start | bytes 1572872 | tf_op jit(solution)/shard_map/ppermute | solution.py:50
  1.6 14.3 %collective-permute-start.8 = (bf16[1024,256]{1,0:T(8,128)(2,1)}, bf16[1024,256]{1,0:T(8,128)(2,1)S(1)}, u32[]{:S(2)}, u32[]{:S(2)}) collective-permute-start(bf16[1024,256]{1,0:T(8,128)(2,1)} %param.18), channel_id=1, source_target_pairs={{0,16},{2,18},{4,20},{6,22},{8,24},{10,26},{12,28},{14,30},{16,0},... | collective-permute-start | bytes 1572872 | tf_op jit(solution)/shard_map/ppermute | solution.py:50
  2.8 24.9 %collective-permute-start.9 = (bf16[1024,256]{1,0:T(8,128)(2,1)}, bf16[1024,256]{1,0:T(8,128)(2,1)S(1)}, u32[]{:S(2)}, u32[]{:S(2)}) collective-permute-start(bf16[1024,256]{1,0:T(8,128)(2,1)} %param.18), channel_id=1, source_target_pairs={{0,24},{2,26},{4,28},{6,30},{8,0},{10,2},{12,4},{14,6},{16,8},{18,... | collective-permute-start | bytes 1572872 | tf_op jit(solution)/shard_map/ppermute | solution.py:50
  16.0 11.7 %copy-start.7 = (bf16[1024,256]{1,0:T(8,128)(2,1)}, bf16[1024,256]{1,0:T(8,128)(2,1)S(1)}, u32[]{:S(2)}) copy-start(bf16[1024,256]{1,0:T(8,128)(2,1)S(1)} %collective-permute-done.8) | copy-start | bytes 1572868
  27.7 0.8 copy-start.8
  28.5 4.6 copy-start.9
  28.5 4.6 copy-start.10
  30.2 59.7 %copy-start.1 = (bf16[4,1024,256]{2,1,0:T(8,128)(2,1)}, bf16[4,1024,256]{2,1,0:T(8,128)(2,1)S(1)}, u32[]{:S(2)}) copy-start(bf16[4,1024,256]{2,1,0:T(8,128)(2,1)S(1)} %pad_maximum_fusion.rest_0_) | copy-start | bytes 6291460
  30.2 87.5 %collective-permute-start.11 = (bf16[4,1024,256]{2,1,0:T(8,128)(2,1)S(1)}, bf16[4,1024,256]{2,1,0:T(8,128)(2,1)}, u32[]{:S(2)}, u32[]{:S(2)}) collective-permute-start(bf16[4,1024,256]{2,1,0:T(8,128)(2,1)S(1)} %pad_maximum_fusion.rest_0_), channel_id=1, source_target_pairs={{0,6},{2,0},{4,2},{6,4},{8,14},{10,8},{12,10},{14,12},{16,22},{18,... | collective-permute-start | bytes 6291464 | tf_op jit(solution)/shard_map/ppermute | solution.py:56
  30.4 91.1 %collective-permute-start.10 = (bf16[4,1024,256]{2,1,0:T(8,128)(2,1)S(1)}, bf16[4,1024,256]{2,1,0:T(8,128)(2,1)}, u32[]{:S(2)}, u32[]{:S(2)}) collective-permute-start(bf16[4,1024,256]{2,1,0:T(8,128)(2,1)S(1)} %pad_maximum_fusion.rest_0_), channel_id=1, source_target_pairs={{0,2},{2,4},{4,6},{6,0},{8,10},{10,12},{12,14},{14,8},{16,18},{18,... | collective-permute-start | bytes 6291464 | tf_op jit(solution)/shard_map/ppermute | solution.py:55
  36.1 47.7 %collective-permute-start = (bf16[2,512,128]{2,1,0:T(8,128)(2,1)}, bf16[2,512,128]{2,1,0:T(8,128)(2,1)S(1)}, u32[]{:S(2)}, u32[]{:S(2)}) collective-permute-start(bf16[2,512,128]{2,1,0:T(8,128)(2,1)} %ready_keys.1), channel_id=1, source_target_pairs={{0,2},{2,4},{4,6},{6,0},{8,10},{10,12},{12,14},{14,8},{16,18},{18,... | collective-permute-start | bytes 786440 | tf_op jit(solution)/shard_map/ppermute | solution.py:50
  37.4 46.4 %collective-permute-start.1 = (bf16[2,512,128]{2,1,0:T(8,128)(2,1)}, bf16[2,512,128]{2,1,0:T(8,128)(2,1)S(1)}, u32[]{:S(2)}, u32[]{:S(2)}) collective-permute-start(bf16[2,512,128]{2,1,0:T(8,128)(2,1)} %ready_keys.1), channel_id=1, source_target_pairs={{0,4},{2,6},{4,0},{6,2},{8,12},{10,14},{12,8},{14,10},{16,20},{18,... | collective-permute-start | bytes 786440 | tf_op jit(solution)/shard_map/ppermute | solution.py:50
  39.3 48.5 %collective-permute-start.2 = (bf16[2,512,128]{2,1,0:T(8,128)(2,1)}, bf16[2,512,128]{2,1,0:T(8,128)(2,1)S(1)}, u32[]{:S(2)}, u32[]{:S(2)}) collective-permute-start(bf16[2,512,128]{2,1,0:T(8,128)(2,1)} %ready_keys.1), channel_id=1, source_target_pairs={{0,6},{2,0},{4,2},{6,4},{8,14},{10,8},{12,10},{14,12},{16,22},{18,... | collective-permute-start | bytes 786440 | tf_op jit(solution)/shard_map/ppermute | solution.py:50
  89.9 23.3 %collective-permute-start.3 = (bf16[4,2,512,128]{3,2,1,0:T(8,128)(2,1)}, bf16[4,2,512,128]{3,2,1,0:T(8,128)(2,1)}, u32[]{:S(2)}, u32[]{:S(2)}) collective-permute-start(bf16[4,2,512,128]{3,2,1,0:T(8,128)(2,1)} %pad_maximum_fusion.1.kv_ref), channel_id=1, source_target_pairs={{0,8},{2,10},{4,12},{6,14},{8,16},{10,18},{12,20},{14,22},{16,24},... | collective-permute-start | bytes 3145736 | tf_op jit(solution)/shard_map/ppermute | solution.py:55
  89.9 25.1 %collective-permute-start.4 = (bf16[4,2,512,128]{3,2,1,0:T(8,128)(2,1)}, bf16[4,2,512,128]{3,2,1,0:T(8,128)(2,1)}, u32[]{:S(2)}, u32[]{:S(2)}) collective-permute-start(bf16[4,2,512,128]{3,2,1,0:T(8,128)(2,1)} %pad_maximum_fusion.1.kv_ref), channel_id=1, source_target_pairs={{0,24},{2,26},{4,28},{6,30},{8,0},{10,2},{12,4},{14,6},{16,8},{18,... | collective-permute-start | bytes 3145736 | tf_op jit(solution)/shard_map/ppermute | solution.py:56
  114.3 22.9 %collective-permute-start.5 = (bf16[2,2,512,128]{3,2,1,0:T(8,128)(2,1)S(1)}, bf16[2,2,512,128]{3,2,1,0:T(8,128)(2,1)}, u32[]{:S(2)}, u32[]{:S(2)}) collective-permute-start(bf16[2,2,512,128]{3,2,1,0:T(8,128)(2,1)S(1)} %slice.32), channel_id=1, source_target_pairs={{0,8},{2,10},{4,12},{6,14},{8,16},{10,18},{12,20},{14,22},{16,24},... | collective-permute-start | bytes 1572872 | tf_op jit(solution)/shard_map/ppermute | solution.py:57
  116.1 21.1 %collective-permute-start.6 = (bf16[2,2,512,128]{3,2,1,0:T(8,128)(2,1)S(1)}, bf16[2,2,512,128]{3,2,1,0:T(8,128)(2,1)}, u32[]{:S(2)}, u32[]{:S(2)}) collective-permute-start(bf16[2,2,512,128]{3,2,1,0:T(8,128)(2,1)S(1)} %slice.33), channel_id=1, source_target_pairs={{0,24},{2,26},{4,28},{6,30},{8,0},{10,2},{12,4},{14,6},{16,8},{18,... | collective-permute-start | bytes 1572872 | tf_op jit(solution)/shard_map/ppermute | solution.py:58
  120.0 24.0 %collective-permute-start.13 = (bf16[2,1024,256]{2,1,0:T(8,128)(2,1)}, bf16[2,1024,256]{2,1,0:T(8,128)(2,1)}, u32[]{:S(2)}, u32[]{:S(2)}) collective-permute-start(bf16[2,1024,256]{2,1,0:T(8,128)(2,1)} %slice.35), channel_id=1, source_target_pairs={{0,6},{2,0},{4,2},{6,4},{8,14},{10,8},{12,10},{14,12},{16,22},{18,... | collective-permute-start | bytes 3145736 | tf_op jit(solution)/shard_map/ppermute | solution.py:58
  123.8 30.0 %collective-permute-start.12 = (bf16[2,1024,256]{2,1,0:T(8,128)(2,1)}, bf16[2,1024,256]{2,1,0:T(8,128)(2,1)}, u32[]{:S(2)}, u32[]{:S(2)}) collective-permute-start(bf16[2,1024,256]{2,1,0:T(8,128)(2,1)} %slice.34), channel_id=1, source_target_pairs={{0,2},{2,4},{4,6},{6,0},{8,10},{10,12},{12,14},{14,8},{16,18},{18,... | collective-permute-start | bytes 3145736 | tf_op jit(solution)/shard_map/ppermute | solution.py:57
  150.6 9.9 %copy-start.11 = (s32[1,64,2,8]{1,3,2,0:T(8,128)S(1)}, s32[1,64,2,8]{1,3,2,0:T(8,128)}, u32[]{:S(2)}) copy-start(s32[1,64,2,8]{1,3,2,0:T(8,128)} %param.22) | copy-start | bytes 12292
  150.6 10.2 %copy-start.2 = (bf16[256,2048]{1,0:T(8,128)(2,1)S(1)}, bf16[256,2048]{1,0:T(8,128)(2,1)}, u32[]{:S(2)}) copy-start(bf16[256,2048]{1,0:T(8,128)(2,1)} %get-tuple-element.25.k1) | copy-start | bytes 3145732
  150.6 10.1 %collective-permute-start.15 = (bf16[256,2048]{1,0:T(8,128)(2,1)}, bf16[256,2048]{1,0:T(8,128)(2,1)S(1)}, u32[]{:S(2)}, u32[]{:S(2)}) collective-permute-start(bf16[256,2048]{1,0:T(8,128)(2,1)} %get-tuple-element.27), channel_id=1, source_target_pairs={{0,32},{32,0},{64,96},{96,64},{1,33},{33,1},{65,97},{97,65},{2,34}... | collective-permute-start | bytes 3145736 | tf_op jit(solution)/shard_map/ppermute | solution.py:607
  160.4 3.1 collective-permute-start.14
  160.8 8.8 %copy-start.3 = (bf16[256,2048]{1,0:T(8,128)(2,1)}, bf16[256,2048]{1,0:T(8,128)(2,1)S(1)}, u32[]{:S(2)}) copy-start(bf16[256,2048]{1,0:T(8,128)(2,1)S(1)} %collective-permute-done.15.g1) | copy-start | bytes 3145732
  161.9 6.2 %copy-start.4 = (bf16[1,64,2,4096]{3,2,1,0:T(2,128)(2,1)S(1)}, bf16[1,64,2,4096]{3,2,1,0:T(2,128)(2,1)}, u32[]{:S(2)}) copy-start(bf16[1,64,2,4096]{3,2,1,0:T(2,128)(2,1)} %param.19) | copy-start | bytes 3145732
  161.9 14.8 %collective-permute-start.17 = (bf16[128,2048]{1,0:T(8,128)(2,1)}, bf16[128,2048]{1,0:T(8,128)(2,1)S(1)}, u32[]{:S(2)}, u32[]{:S(2)}) collective-permute-start(bf16[128,2048]{1,0:T(8,128)(2,1)} %add_convert_fusion), channel_id=1, source_target_pairs={{0,64},{32,96},{64,0},{96,32},{1,65},{33,97},{65,1},{97,33},{2,66}... | collective-permute-start | bytes 1572872 | tf_op jit(solution)/shard_map/ppermute | solution.py:611
  165.6 22.4 %collective-permute-start.16 = (bf16[128,2048]{1,0:T(8,128)(2,1)}, bf16[128,2048]{1,0:T(8,128)(2,1)}, u32[]{:S(2)}, u32[]{:S(2)}) collective-permute-start(bf16[128,2048]{1,0:T(8,128)(2,1)} %add_convert_fusion.1), channel_id=1, source_target_pairs={{0,64},{32,96},{64,0},{96,32},{1,65},{33,97},{65,1},{97,33},{2,66}... | collective-permute-start | bytes 1572872 | tf_op jit(solution)/shard_map/ppermute | solution.py:611
  176.6 11.3 %copy-start.6 = (bf16[128,2048]{1,0:T(8,128)(2,1)}, bf16[128,2048]{1,0:T(8,128)(2,1)S(1)}, u32[]{:S(2)}) copy-start(bf16[128,2048]{1,0:T(8,128)(2,1)S(1)} %collective-permute-done.17.r1) | copy-start | bytes 1572868
  355.6 14.8 %copy-start.5 = (bf16[128,4096]{1,0:T(8,128)(2,1)S(1)}, bf16[128,4096]{1,0:T(8,128)(2,1)}, u32[]{:S(2)}) copy-start(bf16[128,4096]{1,0:T(8,128)(2,1)} %get-tuple-element.30) | copy-start | bytes 3145732
  355.6 127.2 %all-to-all-start.1 = ((bf16[64,544,128]{2,1,0:T(8,128)(2,1)}), bf16[64,544,128]{2,1,0:T(8,128)(2,1)}, u32[]{:S(2)}, u32[]{:S(2)}) async-start(bf16[64,544,128]{2,1,0:T(8,128)(2,1)} %experts.1), calls=%async_computation.1 | async-start | bytes 17825792 | tf_op jit(solution)/shard_map/all_to_all | solution.py:623

commit v3 on v2

--- a/solution.py
+++ b/solution.py
@@ -26,7 +26,10 @@
 SLOT = 16
 NMAIN = NE * SLOT
 NALL = NMAIN + NE
-XR = 17 * 32
+HALF = 8
+NHALF = NE * HALF
+XA = HALF * 32
+XB = XA + 32
 VMEM_BIG = 60 * 1024 * 1024
 
 
@@ -289,11 +292,15 @@
                 lhs[at : at + 64, :] = a_ref[pl.ds(base, 64), s * 1024 : (s + 1) * 1024]
     for cp, dy in zip(copies, (0, 1, 3, 2)):
         cp.wait()
-        for i in range(2):
+
+        def column(i, _, dy=dy):
             res = jnp.dot(lhs[...], w[i, dy], preferred_element_type=F32).astype(BF)
-            lane = (i * 4 + dy) * 256
-            keep[:, lane : lane + 256] = res[:256]
-            send[:, lane : lane + 256] = res[256:]
+            lane = pl.multiple_of((i * 4 + dy) * 256, 256)
+            keep[:, pl.ds(lane, 256)] = res[:256]
+            send[:, pl.ds(lane, 256)] = res[256:]
+            return 0
+
+        lax.fori_loop(0, 2, column, 0)
 
 
 def project(part, scal, attn, pa):
@@ -320,8 +327,38 @@
     )(scal, attn, *pieces)
 
 
+def pair_tile(x):
+    both = [x[:, k * 128 : (k + 1) * 128].reshape(NE, HALF, 128) for k in range(2)]
+    return jnp.concatenate(both, axis=1).astype(BF)
+
+
+def open_tiles(ref, count):
+    out = []
+    for i in range(count):
+        x = ref[:, i * 16 : (i + 1) * 16, :].astype(F32)
+        out += [x[:, :HALF].reshape(NHALF, 128), x[:, HALF:].reshape(NHALF, 128)]
+    return jnp.concatenate(out, axis=1).astype(BF)
+
+
+def pick_kernel(tgt_ref, o_ref):
+    line = lax.broadcasted_iota(jnp.int32, (NALL, ROWS), 0)
+    hit = jnp.zeros((NALL, ROWS), F32)
+    for k in range(TOP):
+        hit = jnp.where(line == tgt_ref[k : k + 1, :], 1.0, hit)
+    o_ref[...] = hit.astype(BF)
+
+
+def picking(tgt_t):
+    return pl.pallas_call(
+        pick_kernel,
+        out_shape=jax.ShapeDtypeStruct((NALL, ROWS), BF),
+        cost_estimate=pl.CostEstimate(flops=2**22, bytes_accessed=2**19, transcendentals=0),
+        name="picking",
+    )(tgt_t)
+
+
 def dispatch_kernel(
-    sc, k0, k1, g0, g1, r0, r1, h_ref, gain_ref, tgt_ref, st_ref, nm_ref, x_hbm, x_ref, sem
+    sc, k0, k1, g0, g1, r0, r1, h_ref, gain_ref, pick, st_ref, nm_ref, xa_hbm, xb_hbm, x_ref, sem
 ):
     z, y = sc[2], sc[3]
     square = jnp.zeros((ROWS, 1), F32)
@@ -342,36 +379,35 @@
             square = square + jnp.sum(sf * sf, axis=-1, keepdims=True)
     scale = lax.rsqrt(square / DM + eps_norm)
     nm_ref[...] = (st_ref[...].astype(F32) * scale * gain_ref[...]).astype(BF)
-    line = lax.broadcasted_iota(jnp.int32, (NALL, ROWS), 0)
-    hit = jnp.zeros((NALL, ROWS), F32)
-    for k in range(TOP):
-        hit = jnp.where(line == tgt_ref[k : k + 1, :], 1.0, hit)
-    pick = hit.astype(BF)
-    copies = [
-        pltpu.make_async_copy(
-            x_ref.at[:, pl.ds(j * 64, 64 if j < 8 else 32)],
-            x_hbm.at[:, pl.ds(j * 64, 64 if j < 8 else 32)],
-            sem.at[j],
-        )
-        for j in range(9)
-    ]
-    for j in range(8):
-        n = nm_ref[:, j * 512 : (j + 1) * 512]
-        main = jnp.dot(pick[:NMAIN], n, preferred_element_type=F32).astype(BF)
-        for i in range(4):
-            f = 4 * j + i
-            x_ref[:, f * SLOT : (f + 1) * SLOT, :] = main[:, i * 128 : (i + 1) * 128].reshape(
-                NE, SLOT, 128
+
+    def out_copy(chunk, j):
+        rows = pl.ds(pl.multiple_of(j * 32, 32), 32)
+        to = xa_hbm if chunk == 0 else xb_hbm
+        return pltpu.make_async_copy(x_ref.at[chunk, :, rows], to.at[:, rows], sem.at[chunk, j])
+
+    for chunk in range(2):
+
+        def send_part(j, _, chunk=chunk):
+            n = nm_ref[:, pl.ds(pl.multiple_of(j * 512, 512), 512)]
+            main = jnp.dot(
+                pick[chunk * NHALF : (chunk + 1) * NHALF, :], n, preferred_element_type=F32
             )
-        copies[j].start()
-    ov = jnp.dot(pick[NMAIN:], nm_ref[...], preferred_element_type=F32).astype(BF)
-    x_ref[:, 512:544, :] = ov.reshape(NE, 32, 128)
-    copies[8].start()
-    for cp in copies:
-        cp.wait()
-
-
-def dispatch(scal, keeps, gots, rests, hid, gain, tgt_t):
+            for i in range(2):
+                at = pl.multiple_of(j * 32 + i * 16, 16)
+                x_ref[chunk, :, pl.ds(at, 16), :] = pair_tile(main[:, i * 256 : (i + 1) * 256])
+            out_copy(chunk, j).start()
+            return 0
+
+        lax.fori_loop(0, 8, send_part, 0)
+    ov = jnp.dot(pick[NMAIN:, :], nm_ref[...], preferred_element_type=F32).astype(BF)
+    x_ref[1, :, XA:XB, :] = ov.reshape(NE, 32, 128)
+    out_copy(1, 8).start()
+    for chunk in range(2):
+        for j in range(8 + chunk):
+            out_copy(chunk, j).wait()
+
+
+def dispatch(scal, keeps, gots, rests, hid, gain, pick):
     at = lambda i, sc: (0, 0)
     half = pl.BlockSpec((ROWS, DM // 2), at)
     line = pl.BlockSpec((ROWS, DM), at)
@@ -380,39 +416,46 @@
         out_shape=(
             jax.ShapeDtypeStruct((ROWS, DM), BF),
             jax.ShapeDtypeStruct((ROWS, DM), BF),
-            jax.ShapeDtypeStruct((NE, XR, 128), BF),
+            jax.ShapeDtypeStruct((NE, XA, 128), BF),
+            jax.ShapeDtypeStruct((NE, XB, 128), BF),
         ),
         grid_spec=pltpu.PrefetchScalarGridSpec(
             num_scalar_prefetch=1,
             grid=(1,),
             in_specs=[half] * 6
-            + [line, pl.BlockSpec((1, DM), at), pl.BlockSpec((TOP, ROWS), at)],
-            out_specs=(line, line, pl.BlockSpec(memory_space=pl.ANY)),
-            scratch_shapes=[pltpu.VMEM((NE, XR, 128), BF), pltpu.SemaphoreType.DMA((9,))],
+            + [line, pl.BlockSpec((1, DM), at), pl.BlockSpec((NALL, ROWS), at)],
+            out_specs=(line, line) + (pl.BlockSpec(memory_space=pl.ANY),) * 2,
+            scratch_shapes=[pltpu.VMEM((2, NE, XB, 128), BF), pltpu.SemaphoreType.DMA((2, 9))],
         ),
         compiler_params=pltpu.CompilerParams(vmem_limit_bytes=VMEM_BIG),
         cost_estimate=pl.CostEstimate(
             flops=2**30, bytes_accessed=14 * 2**20, transcendentals=0
         ),
         name="dispatch",
-    )(scal, *keeps, *gots, *rests, hid, gain, tgt_t)
-
-
-def expert_kernel(x_ref, xo_ref, wg_ref, wu_ref, wd_ref, y_hbm, ga, ua, inner, xov, yb, yo, sem):
+    )(scal, *keeps, *gots, *rests, hid, gain, pick)
+
+
+def expert_kernel(over, *refs):
+    x_ref, refs = refs[0], refs[1:]
+    if over:
+        xo_ref, refs = refs[0], refs[1:]
+    wg_ref, wu_ref, wd_ref, y_hbm, ga, ua, inner, yb, sem = refs[:9]
+    if over:
+        xov, yo = refs[9:]
     step = pl.program_id(0)
 
-    @pl.when(step == 0)
-    def _():
-        xov[...] = xo_ref[...].reshape(NE, DM)
+    if over:
+
+        @pl.when(step == 0)
+        def _():
+            xov[...] = xo_ref[...].reshape(NE, DM)
 
     @pl.when(step < 4)
     def _():
-        pieces = [
-            x_ref[:, i * SLOT : (i + 1) * SLOT, :].reshape(NMAIN, 128) for i in range(8)
-        ]
-        main = jnp.concatenate(pieces, axis=1)
-        lane = pl.multiple_of(step * 1024, 1024)
-        rows = jnp.concatenate([main, xov[:, pl.ds(lane, 1024)]], axis=0)
+        rows = open_tiles(x_ref, 4)
+        if over:
+            lane = pl.multiple_of(step * 1024, 1024)
+            rows = jnp.concatenate([rows, xov[:, pl.ds(lane, 1024)]], axis=0)
         g = jnp.dot(rows, wg_ref[0], preferred_element_type=F32)
         u = jnp.dot(rows, wu_ref[0], preferred_element_type=F32)
 
@@ -431,64 +474,71 @@
         g = ga[...]
         inner[...] = (g / (1.0 + jnp.exp(-g)) * ua[...]).astype(BF)
 
-    for j in range(4):
-
-        @pl.when(step == 4 + j)
-        def _(j=j):
-            slot = j % 2
-            out = jnp.dot(inner[...], wd_ref[0], preferred_element_type=F32).astype(BF)
-            if j >= 2:
-                pltpu.make_async_copy(
-                    yb.at[slot], y_hbm.at[:, pl.ds((j - 2) * 128, 128)], sem.at[slot]
-                ).wait()
-            for i in range(8):
-                yb[slot, :, i * SLOT : (i + 1) * SLOT, :] = out[
-                    :NMAIN, i * 128 : (i + 1) * 128
-                ].reshape(NE, SLOT, 128)
-            xov[:, j * 1024 : (j + 1) * 1024] = out[NMAIN:]
-            pltpu.make_async_copy(
-                yb.at[slot], y_hbm.at[:, pl.ds(j * 128, 128)], sem.at[slot]
-            ).start()
-            if j == 3:
+    def out_copy(j):
+        rows = pl.ds(pl.multiple_of(j * 64, 64), 64)
+        return pltpu.make_async_copy(yb.at[j & 1], y_hbm.at[:, rows], sem.at[j & 1])
+
+    @pl.when(step >= 4)
+    def _():
+        j = step - 4
+        out = jnp.dot(inner[...], wd_ref[0], preferred_element_type=F32)
+
+        @pl.when(j >= 2)
+        def _():
+            out_copy(j - 2).wait()
+
+        for i in range(4):
+            yb[j & 1, :, i * 16 : (i + 1) * 16, :] = pair_tile(
+                out[:NHALF, i * 256 : (i + 1) * 256]
+            )
+        out_copy(j).start()
+        if over:
+            xov[:, pl.ds(pl.multiple_of(j * 1024, 1024), 1024)] = out[NHALF:].astype(BF)
+
+        @pl.when(j == 3)
+        def _():
+            if over:
                 yo[...] = xov[...].reshape(NE, 32, 128)
-                last = pltpu.make_async_copy(yo, y_hbm.at[:, pl.ds(512, 32)], sem.at[2])
+                last = pltpu.make_async_copy(yo, y_hbm.at[:, pl.ds(XA, 32)], sem.at[2])
                 last.start()
-                for k in (2, 3):
-                    pltpu.make_async_copy(
-                        yb.at[k % 2], y_hbm.at[:, pl.ds(k * 128, 128)], sem.at[k % 2]
-                    ).wait()
                 last.wait()
-
-
-def run_experts(x, wg, wu, wd):
+            out_copy(2).wait()
+            out_copy(3).wait()
+
+
+def run_experts(x, wg, wu, wd, over):
     lo = lambda i: jnp.minimum(i, 3)
+    n = NHALF + (NE if over else 0)
+    x_specs = [pl.BlockSpec((NE, 64, 128), lambda i: (0, lo(i), 0))]
+    extra = []
+    if over:
+        x_specs.append(pl.BlockSpec((NE, 32, 128), lambda i: (0, 8, 0)))
+        extra = [pltpu.VMEM((NE, DM), BF), pltpu.VMEM((NE, 32, 128), BF)]
     return pl.pallas_call(
-        expert_kernel,
+        functools.partial(expert_kernel, over),
         grid=(8,),
-        out_shape=jax.ShapeDtypeStruct((NE, XR, 128), BF),
-        in_specs=[
-            pl.BlockSpec((NE, 128, 128), lambda i: (0, lo(i), 0)),
-            pl.BlockSpec((NE, 32, 128), lambda i: (0, 16, 0)),
+        out_shape=jax.ShapeDtypeStruct(x.shape, BF),
+        in_specs=x_specs
+        + [
             pl.BlockSpec((1, 1024, FF), lambda i: (0, lo(i), 0)),
             pl.BlockSpec((1, 1024, FF), lambda i: (0, lo(i), 0)),
             pl.BlockSpec((1, FF, 1024), lambda i: (0, 0, jnp.maximum(i - 4, 0))),
         ],
         out_specs=pl.BlockSpec(memory_space=pl.ANY),
         scratch_shapes=[
-            pltpu.VMEM((NALL, FF), F32),
-            pltpu.VMEM((NALL, FF), F32),
-            pltpu.VMEM((NALL, FF), BF),
-            pltpu.VMEM((NE, DM), BF),
-            pltpu.VMEM((2, NE, 128, 128), BF),
-            pltpu.VMEM((NE, 32, 128), BF),
+            pltpu.VMEM((n, FF), F32),
+            pltpu.VMEM((n, FF), F32),
+            pltpu.VMEM((n, FF), BF),
+            pltpu.VMEM((2, NE, 64, 128), BF),
             pltpu.SemaphoreType.DMA((3,)),
-        ],
+        ]
+        + extra,
         compiler_params=pltpu.CompilerParams(vmem_limit_bytes=VMEM_BIG),
         cost_estimate=pl.CostEstimate(
-            flops=20 * 2**30, bytes_accessed=36 * 2**20, transcendentals=2**20
-        ),
-        name="experts",
-    )(x, x, wg, wu, wd)
+            flops=10 * 2**30, bytes_accessed=27 * 2**20, transcendentals=2**19
+        ),
+        name="experts_b" if over else "experts_a",
+    )(*([x] * len(x_specs)), wg, wu, wd)
 
 
 def mix_kernel(tgt_ref, gate_ref, gm, go):
@@ -516,15 +566,14 @@
     )(tgt, gates)
 
 
-def combine_kernel(y_ref, yo_ref, st_ref, gm_ref, go_ref, o_ref, yov):
+def combine_kernel(ya_ref, yb_ref, yo_ref, st_ref, gm_ref, go_ref, o_ref, yov):
     step = pl.program_id(0)
 
     @pl.when(step == 0)
     def _():
         yov[...] = yo_ref[...].reshape(NE, DM)
 
-    pieces = [y_ref[:, i * SLOT : (i + 1) * SLOT, :].reshape(NMAIN, 128) for i in range(8)]
-    main = jnp.concatenate(pieces, axis=1)
+    main = jnp.concatenate([open_tiles(ya_ref, 4), open_tiles(yb_ref, 4)], axis=0)
     at = pl.multiple_of(step * 1024, 1024)
     both = jnp.dot(gm_ref[...], main, preferred_element_type=F32) + jnp.dot(
         go_ref[...], yov[:, pl.ds(at, 1024)], preferred_element_type=F32
@@ -536,14 +585,15 @@
     o_ref[...] = (st + (both[:ROWS] + both[ROWS:])).astype(BF)
 
 
-def combine(y, stream, gm, go):
+def combine(ya, yb, stream, gm, go):
     return pl.pallas_call(
         combine_kernel,
         grid=(4,),
         out_shape=jax.ShapeDtypeStruct((ROWS, DM), BF),
         in_specs=[
-            pl.BlockSpec((NE, 128, 128), lambda i: (0, i, 0)),
-            pl.BlockSpec((NE, 32, 128), lambda i: (0, 16, 0)),
+            pl.BlockSpec((NE, 64, 128), lambda i: (0, i, 0)),
+            pl.BlockSpec((NE, 64, 128), lambda i: (0, i, 0)),
+            pl.BlockSpec((NE, 32, 128), lambda i: (0, 8, 0)),
             pl.BlockSpec((ROWS, 1024), lambda i: (0, i)),
             pl.BlockSpec((2 * ROWS, NMAIN), lambda i: (0, 0)),
             pl.BlockSpec((2 * ROWS, NE), lambda i: (0, 0)),
@@ -555,7 +605,7 @@
             flops=2 * 2**30, bytes_accessed=11 * 2**20, transcendentals=0
         ),
         name="combine",
-    )(y, y, stream, gm, go)
+    )(ya, yb, yb, stream, gm, go)
 
 
 def slots(ids):
@@ -566,7 +616,8 @@
     slot = jnp.sum(
         jnp.where(ids[:, :, None] == catalog, before[:, None, :], 0.0), axis=-1
     ).astype(jnp.int32)
-    return jnp.where(slot < SLOT, ids * SLOT + slot, NMAIN + ids)
+    main = ids * HALF + (slot & (HALF - 1)) + jnp.where(slot < HALF, 0, NHALF)
+    return jnp.where(slot < SLOT, main, NMAIN + ids)
 
 
 def on_device(
@@ -598,6 +649,7 @@
     ids = expert_ids[0].reshape(ROWS, TOP)
     tgt = slots(ids)
     tgt_t = jnp.transpose(tgt.reshape(64, SEQ, TOP), (2, 1, 0)).reshape(TOP, ROWS)
+    pick = picking(tgt_t)
     hid = jnp.transpose(hidden_in[0], (1, 0, 2)).reshape(ROWS, DM)
 
     attn = attention(scal, q2, cs, sn, q_gain.reshape(1, HD), kv_all)
@@ -609,19 +661,21 @@
         keeps.append(keep)
         gots.append(got)
         rests.append(lax.ppermute(other, "tensor", X_SWAP))
-    stream, normed, x = dispatch(
-        scal, keeps, gots, rests, hid, norm_gain.reshape(1, DM), tgt_t
-    )
-    arrived = lax.all_to_all(x, ("tensor", "expert"), split_axis=0, concat_axis=0, tiled=True)
+    stream, normed, xa, xb = dispatch(scal, keeps, gots, rests, hid, norm_gain.reshape(1, DM), pick)
+
+    def exchange(x):
+        return lax.all_to_all(x, ("tensor", "expert"), split_axis=0, concat_axis=0, tiled=True)
+
+    in_a, in_b = exchange(xa), exchange(xb)
 
     logits = jnp.dot(normed, router, preferred_element_type=F32)
     logits = jnp.transpose(logits.reshape(SEQ, 64, NE), (1, 0, 2)).reshape(ROWS, NE)
     chosen = ids[:, :, None] == jnp.arange(NE, dtype=jnp.int32)
     gates = jax.nn.softmax(jnp.sum(jnp.where(chosen, logits[:, None, :], 0.0), axis=-1), axis=-1)
 
-    done = run_experts(arrived, w_gate, w_up, w_down)
-    back = lax.all_to_all(done, ("tensor", "expert"), split_axis=0, concat_axis=0, tiled=True)
-    out = combine(back, stream, *mixing(tgt, gates))
+    back_a = exchange(run_experts(in_a, w_gate, w_up, w_down, False))
+    back_b = exchange(run_experts(in_b, w_gate, w_up, w_down, True))
+    out = combine(back_a, back_b, stream, *mixing(tgt, gates))
     return out.reshape(hidden_in.shape)
 
 

time: 495 us -> 491 us (level)
  the two profiles are of different devices: /device:TPU:45 before, /device:TPU:11 now
where the time goes in v3:
time: 491 us; the launch traced here: 490 us
  waiting for transfers between devices  230 us (47%)
  Pallas kernels  101 us (21%)
  blocking collectives  77.2 us (16%)
  starting transfers between devices  54.4 us (11%)
  local copies, waits for them, and re-layouts  16.4 us (3%)
  other arithmetic  9.71 us (2%)
    all_to_all x3, waiting for transfers between devices, exchange(): lax.all_to_all(x, ('tensor', 'expert'), split_axis=0, concat_axis=0, tile...  132 us
    all_to_all x1, blocking collectives, exchange(): lax.all_to_all(x, ('tensor', 'expert'), split_axis=0, concat_axis=0, tile...  77.2 us
    ppermute x6, waiting for transfers between devices, ring_four(): return [x] + [lax.ppermute(x, 'expert', move(k)) for k in (1, 2, 3)]  67.8 us
    pallas_call x2, Pallas kernels, run_experts(): pl.pallas_call(functools.partial(expert_kernel, over), grid=(8,), out_sha...  37.9 us
    all_to_all x3, starting transfers between devices, exchange(): lax.all_to_all(x, ('tensor', 'expert'), split_axis=0, concat_axis=0, tile...  25.4 us
    ppermute x2, waiting for transfers between devices, on_device(): rests.append(lax.ppermute(other, 'tensor', X_SWAP))  14.7 us
    pallas_call x2, Pallas kernels, project(): pl.pallas_call(functools.partial(proj_kernel, part), out_shape=(jax.Shape...  14.6 us
    pallas_call x1, Pallas kernels, attention(): attn_call(attn_first, [Q_SPEC, table, table, pl.BlockSpec((1, HD), lambda...  13.2 us
  transfers between devices with their start and end apart: 21, of which 12 were waited for; matrix products, arithmetic and copies ran while one was open for 4% of the time, Pallas kernels for 17%

profile of v3, /device:TPU:11, one launch (start us, length us, event | category | flops | bytes accessed | tf_op | source)
XLA Modules:
  0.0 489.6 jit_solution(14494767840865543242)
XLA Ops:
  0.0 1.6 collective-permute-start.7
  1.6 3.3 collective-permute-start.8
  4.9 0.7 collective-permute-start.9
  5.7 9.9 %collective-permute-done.7 = bf16[1024,256]{1,0:T(8,128)(2,1)S(1)} collective-permute-done((bf16[1024,256]{1,0:T(8,128)(2,1)}, bf16[1024,256]{1,0:T(8,128)(2,1)S(1)}, u32[]{:S(2)}, u32[]{:S(2)}) %collective-permute-start.7) | collective-permute-done | bytes 524320 | tf_op jit(solution)/shard_map/ppermute | solution.py:53
  15.6 12.1 %collective-permute-done.8 = bf16[1024,256]{1,0:T(8,128)(2,1)S(1)} collective-permute-done((bf16[1024,256]{1,0:T(8,128)(2,1)}, bf16[1024,256]{1,0:T(8,128)(2,1)S(1)}, u32[]{:S(2)}, u32[]{:S(2)}) %collective-permute-start.8) | collective-permute-done | bytes 524320 | tf_op jit(solution)/shard_map/ppermute | solution.py:53
  27.7 0.8 copy-done.6
  28.7 1.7 pad_maximum_fusion.rest_0_
  30.4 0.2 collective-permute-start.11
  30.6 1.3 collective-permute-start.10
  31.9 0.5 fusion.5
  32.5 0.9 pad_maximum_fusion.2
  33.3 0.7 copy_bitcast_fusion
  34.0 2.2 ready_keys.1
  36.3 1.3 collective-permute-start
  37.6 1.9 collective-permute-start.1
  39.5 2.1 collective-permute-start.2
  41.6 41.7 %collective-permute-done = bf16[2,512,128]{2,1,0:T(8,128)(2,1)S(1)} collective-permute-done((bf16[2,512,128]{2,1,0:T(8,128)(2,1)}, bf16[2,512,128]{2,1,0:T(8,128)(2,1)S(1)}, u32[]{:S(2)}, u32[]{:S(2)}) %collective-permute-start) | collective-permute-done | bytes 262176 | tf_op jit(solution)/shard_map/ppermute | solution.py:53
  83.3 4.1 collective-permute-done.2
  87.3 2.0 pad_maximum_fusion.1.kv_ref
  89.4 2.1 collective-permute-start.3
  91.5 1.7 collective-permute-start.4
  93.2 2.5 copy.49
  95.6 0.7 pad_add_fusion.sc
  96.3 13.2 %shard_map.127 = (bf16[256,2048]{1,0:T(8,128)(2,1)}, f32[16,8,256]{2,1,0:T(8,128)}, f32[16,144,256]{2,1,0:T(8,128)}) custom-call(s32[4]{0:T(128)} %pad_add_fusion.sc, bf16[256,2048]{1,0:T(8,128)(2,1)} %bitcast.56, f32[256,128]{1,0:T(8,128)} %get-tuple-element.46.cos_ref, f32[256,128]{1,0:T(8,128)} %get-tuple-element.47.sin_ref, f32[1,128]{1,0:T(1,128)} %bitcast.74, ...), custom_call_target="tpu_custom_call" | custom-call | flops 4294967296 | bytes 8388608 | tf_op jit(solution)/shard_map/pallas_call | solution.py:255
  109.5 6.0 %collective-permute-done.3.ka_ref = bf16[4,2,512,128]{3,2,1,0:T(8,128)(2,1)} collective-permute-done((bf16[4,2,512,128]{3,2,1,0:T(8,128)(2,1)}, bf16[4,2,512,128]{3,2,1,0:T(8,128)(2,1)}, u32[]{:S(2)}, u32[]{:S(2)}) %collective-permute-start.3) | collective-permute-done | bytes 1048608 | tf_op jit(solution)/shard_map/ppermute | solution.py:58
  115.4 1.1 slice.32
  116.6 1.1 slice.33
  117.7 2.7 collective-permute-start.6
  120.4 2.3 slice.35
  122.8 1.6 collective-permute-start.13
  124.3 2.3 slice.34
  126.6 1.0 collective-permute-start.12
  127.7 4.6 shard_map.128
  132.2 4.9 shard_map.129.a_ref
  137.1 9.4 %collective-permute-done.13.rest_3_ = bf16[2,1024,256]{2,1,0:T(8,128)(2,1)} collective-permute-done((bf16[2,1024,256]{2,1,0:T(8,128)(2,1)}, bf16[2,1024,256]{2,1,0:T(8,128)(2,1)}, u32[]{:S(2)}, u32[]{:S(2)}) %collective-permute-start.13) | collective-permute-done | bytes 1048608 | tf_op jit(solution)/shard_map/ppermute | solution.py:61
  146.5 7.3 %shard_map.131 = (bf16[256,2048]{1,0:T(8,128)(2,1)}, bf16[256,2048]{1,0:T(8,128)(2,1)}) custom-call(s32[4]{0:T(128)} %pad_add_fusion.sc, bf16[256,2048]{1,0:T(8,128)(2,1)} %shard_map.129.a_ref, bf16[4,1024,256]{2,1,0:T(8,128)(2,1)} %copy-done.1, bf16[4,1024,256]{2,1,0:T(8,128)(2,1)} %collective-permute-done.10.rest_1_, ...), custom_call_target="tpu_custom_call" | custom-call | flops 2147483648 | bytes 7340032 | tf_op jit(solution)/shard_map/pallas_call | solution.py:309
  153.9 3.4 collective-permute-start.15
  157.2 7.3 %shard_map.130 = (bf16[256,2048]{1,0:T(8,128)(2,1)}, bf16[256,2048]{1,0:T(8,128)(2,1)}) custom-call(s32[4]{0:T(128)} %pad_add_fusion.sc, bf16[256,2048]{1,0:T(8,128)(2,1)} %shard_map.129.a_ref, bf16[4,1024,256]{2,1,0:T(8,128)(2,1)} %copy-done.1, bf16[4,1024,256]{2,1,0:T(8,128)(2,1)} %collective-permute-done.10.rest_1_, ...), custom_call_target="tpu_custom_call" | custom-call | flops 2147483648 | bytes 7340032 | tf_op jit(solution)/shard_map/pallas_call | solution.py:309
  164.5 0.2 collective-permute-start.14
  165.3 1.9 collective-permute-start.17
  167.2 0.4 collective-permute-done.14.g0
  167.6 2.1 add_convert_fusion.1
  169.8 1.9 collective-permute-start.16
  171.8 0.7 convert_and_fusion
  172.6 0.7 reshape.57.tgt_ref
  173.3 1.6 copy.39
  174.9 1.7 picking.1.pick
  176.6 3.4 collective-permute-done.17.r1
  180.0 11.2 %collective-permute-done.16.r0 = bf16[128,2048]{1,0:T(8,128)(2,1)} collective-permute-done((bf16[128,2048]{1,0:T(8,128)(2,1)}, bf16[128,2048]{1,0:T(8,128)(2,1)}, u32[]{:S(2)}, u32[]{:S(2)}) %collective-permute-start.16) | collective-permute-done | bytes 524320 | tf_op jit(solution)/shard_map/ppermute | solution.py:663
  191.2 11.8 %dispatch.1 = (bf16[128,4096]{1,0:T(8,128)(2,1)}, bf16[128,4096]{1,0:T(8,128)(2,1)}, bf16[64,256,128]{2,1,0:T(8,128)(2,1)}, bf16[64,288,128]{2,1,0:T(8,128)(2,1)}) custom-call(s32[4]{0:T(128)} %pad_add_fusion.sc, bf16[256,2048]{1,0:T(8,128)(2,1)} %get-tuple-element.25.k0, bf16[256,2048]{1,0:T(8,128)(2,1)} %get-tuple-element.26.k1, ...), custom_call_target="tpu_custom_call" | custom-call | flops 1073741824 | bytes 14680064 | tf_op jit(solution)/shard_map/dispatch/pallas_call | solution.py:414
  203.0 77.2 %all_to_all.20.refs_0_ = bf16[64,256,128]{2,1,0:T(8,128)(2,1)} all-to-all(bf16[64,256,128]{2,1,0:T(8,128)(2,1)} %get-tuple-element.29), channel_id=1, replica_groups=mesh['tensor'=4,'expert'=16,'dp'=2] {'tensor','expert'}, dimensions={0} | all-to-all | bytes 8388608 | tf_op jit(solution)/shard_map/all_to_all | solution.py:667
  280.2 6.9 %all-to-all-start.2 = ((bf16[64,288,128]{2,1,0:T(8,128)(2,1)}), bf16[64,288,128]{2,1,0:T(8,128)(2,1)}, u32[]{:S(2)}, u32[]{:S(2)}) async-start(bf16[64,288,128]{2,1,0:T(8,128)(2,1)} %get-tuple-element.30), calls=%async_computation.2 | async-start | bytes 9437184 | tf_op jit(solution)/shard_map/all_to_all | solution.py:667
  287.2 18.0 %experts_a.1 = bf16[64,256,128]{2,1,0:T(8,128)(2,1)} custom-call(bf16[64,256,128]{2,1,0:T(8,128)(2,1)} %all_to_all.20.refs_0_, bf16[1,4096,768]{2,1,0:T(8,128)(2,1)} %refs_2_.3, bf16[1,4096,768]{2,1,0:T(8,128)(2,1)} %refs_3_.3, bf16[1,768,4096]{2,1,0:T(8,128)(2,1)} %refs_4_.1), custom_call_target="tpu_custom_call" | custom-call | flops 10737418240 | bytes 28311552 | tf_op jit(solution)/shard_map/experts_a/pallas_call | solution.py:517
  305.2 43.0 %all-to-all-done.2.refs_0_.refs_1_ = bf16[64,288,128]{2,1,0:T(8,128)(2,1)} async-done(((bf16[64,288,128]{2,1,0:T(8,128)(2,1)}), bf16[64,288,128]{2,1,0:T(8,128)(2,1)}, u32[]{:S(2)}, u32[]{:S(2)}) %all-to-all-start.2) | async-done | bytes 4718624 | tf_op jit(solution)/shard_map/all_to_all | solution.py:667
  348.3 8.0 %all-to-all-start.1 = ((bf16[64,256,128]{2,1,0:T(8,128)(2,1)}), bf16[64,256,128]{2,1,0:T(8,128)(2,1)}, u32[]{:S(2)}, u32[]{:S(2)}) async-start(bf16[64,256,128]{2,1,0:T(8,128)(2,1)} %experts_a.1), calls=%async_computation.1 | async-start | bytes 8388608 | tf_op jit(solution)/shard_map/all_to_all | solution.py:667
  356.2 19.8 %experts_b.1 = bf16[64,288,128]{2,1,0:T(8,128)(2,1)} custom-call(bf16[64,288,128]{2,1,0:T(8,128)(2,1)} %all-to-all-done.2.refs_0_.refs_1_, bf16[64,288,128]{2,1,0:T(8,128)(2,1)} %all-to-all-done.2.refs_0_.refs_1_, bf16[1,4096,768]{2,1,0:T(8,128)(2,1)} %refs_2_.3, bf16[1,4096,768]{2,1,0:T(8,128)(2,1)} %refs_3_.3, bf16[1,768,4096]{2,1,0:T(8,128)(2,1)} %refs_4_.1), custom_call_target="tpu_custom_call" | custom-call | flops 10737418240 | bytes 28311552 | tf_op jit(solution)/shard_map/experts_b/pallas_call | solution.py:517
  376.1 31.9 %all-to-all-done.1.ya_ref = bf16[64,256,128]{2,1,0:T(8,128)(2,1)} async-done(((bf16[64,256,128]{2,1,0:T(8,128)(2,1)}), bf16[64,256,128]{2,1,0:T(8,128)(2,1)}, u32[]{:S(2)}, u32[]{:S(2)}) %all-to-all-start.1) | async-done | bytes 4194336 | tf_op jit(solution)/shard_map/all_to_all | solution.py:667
  407.9 10.5 %all-to-all-start.3 = ((bf16[64,288,128]{2,1,0:T(8,128)(2,1)}), bf16[64,288,128]{2,1,0:T(8,128)(2,1)}, u32[]{:S(2)}, u32[]{:S(2)}) async-start(bf16[64,288,128]{2,1,0:T(8,128)(2,1)} %experts_b.1), calls=%async_computation.3 | async-start | bytes 9437184 | tf_op jit(solution)/shard_map/all_to_all | solution.py:667
  418.5 0.5 fusion.7
  419.4 0.7 broadcast_divide_fusion.gate_ref
  420.1 2.6 mixing.1
  422.7 56.9 %all-to-all-done.3.yb_ref.yo_ref = bf16[64,288,128]{2,1,0:T(8,128)(2,1)} async-done(((bf16[64,288,128]{2,1,0:T(8,128)(2,1)}), bf16[64,288,128]{2,1,0:T(8,128)(2,1)}, u32[]{:S(2)}, u32[]{:S(2)}) %all-to-all-start.3) | async-done | bytes 4718624 | tf_op jit(solution)/shard_map/all_to_all | solution.py:667
  479.6 7.4 %combine.1 = bf16[128,4096]{1,0:T(8,128)(2,1)} custom-call(bf16[64,256,128]{2,1,0:T(8,128)(2,1)} %all-to-all-done.1.ya_ref, bf16[64,288,128]{2,1,0:T(8,128)(2,1)} %all-to-all-done.3.yb_ref.yo_ref, bf16[64,288,128]{2,1,0:T(8,128)(2,1)} %all-to-all-done.3.yb_ref.yo_ref, bf16[128,4096]{1,0:T(8,128)(2,1)} %get-tuple-element.31.st_ref, ...), custom_call_target="tpu_custom_call" | custom-call | flops 2147483648 | bytes 11534336 | tf_op jit(solution)/shard_map/combine/pallas_call | solution.py:589
  487.0 2.5 reshape.59
  (50 shorter events, 1.6 us)
Async XLA Ops:
  0.0 418.4 %copy-start = (bf16[4096,64]{0,1:T(8,128)(2,1)S(1)}, bf16[4096,64]{0,1:T(8,128)(2,1)}, u32[]{:S(2)}) copy-start(bf16[4096,64]{0,1:T(8,128)(2,1)} %param.21) | copy-start | bytes 1572868
  0.0 15.6 %collective-permute-start.7 = (bf16[1024,256]{1,0:T(8,128)(2,1)}, bf16[1024,256]{1,0:T(8,128)(2,1)S(1)}, u32[]{:S(2)}, u32[]{:S(2)}) collective-permute-start(bf16[1024,256]{1,0:T(8,128)(2,1)} %param.18), channel_id=1, source_target_pairs={{0,8},{2,10},{4,12},{6,14},{8,16},{10,18},{12,20},{14,22},{16,24},... | collective-permute-start | bytes 1572872 | tf_op jit(solution)/shard_map/ppermute | solution.py:53
  1.6 26.1 %collective-permute-start.8 = (bf16[1024,256]{1,0:T(8,128)(2,1)}, bf16[1024,256]{1,0:T(8,128)(2,1)S(1)}, u32[]{:S(2)}, u32[]{:S(2)}) collective-permute-start(bf16[1024,256]{1,0:T(8,128)(2,1)} %param.18), channel_id=1, source_target_pairs={{0,16},{2,18},{4,20},{6,22},{8,24},{10,26},{12,28},{14,30},{16,0},... | collective-permute-start | bytes 1572872 | tf_op jit(solution)/shard_map/ppermute | solution.py:53
  4.9 22.8 %collective-permute-start.9 = (bf16[1024,256]{1,0:T(8,128)(2,1)}, bf16[1024,256]{1,0:T(8,128)(2,1)S(1)}, u32[]{:S(2)}, u32[]{:S(2)}) collective-permute-start(bf16[1024,256]{1,0:T(8,128)(2,1)} %param.18), channel_id=1, source_target_pairs={{0,24},{2,26},{4,28},{6,30},{8,0},{10,2},{12,4},{14,6},{16,8},{18,... | collective-permute-start | bytes 1572872 | tf_op jit(solution)/shard_map/ppermute | solution.py:53
  27.7 0.8 copy-start.6
  27.7 1.0 copy-start.7
  28.7 4.6 copy-start.8
  28.7 4.6 copy-start.9
  30.4 65.3 %copy-start.1 = (bf16[4,1024,256]{2,1,0:T(8,128)(2,1)}, bf16[4,1024,256]{2,1,0:T(8,128)(2,1)S(1)}, u32[]{:S(2)}) copy-start(bf16[4,1024,256]{2,1,0:T(8,128)(2,1)S(1)} %pad_maximum_fusion.rest_0_) | copy-start | bytes 6291460
  30.4 90.1 %collective-permute-start.11 = (bf16[4,1024,256]{2,1,0:T(8,128)(2,1)S(1)}, bf16[4,1024,256]{2,1,0:T(8,128)(2,1)}, u32[]{:S(2)}, u32[]{:S(2)}) collective-permute-start(bf16[4,1024,256]{2,1,0:T(8,128)(2,1)S(1)} %pad_maximum_fusion.rest_0_), channel_id=1, source_target_pairs={{0,6},{2,0},{4,2},{6,4},{8,14},{10,8},{12,10},{14,12},{16,22},{18,... | collective-permute-start | bytes 6291464 | tf_op jit(solution)/shard_map/ppermute | solution.py:59
  30.6 93.7 %collective-permute-start.10 = (bf16[4,1024,256]{2,1,0:T(8,128)(2,1)S(1)}, bf16[4,1024,256]{2,1,0:T(8,128)(2,1)}, u32[]{:S(2)}, u32[]{:S(2)}) collective-permute-start(bf16[4,1024,256]{2,1,0:T(8,128)(2,1)S(1)} %pad_maximum_fusion.rest_0_), channel_id=1, source_target_pairs={{0,2},{2,4},{4,6},{6,0},{8,10},{10,12},{12,14},{14,8},{16,18},{18,... | collective-permute-start | bytes 6291464 | tf_op jit(solution)/shard_map/ppermute | solution.py:58
  36.3 47.0 %collective-permute-start = (bf16[2,512,128]{2,1,0:T(8,128)(2,1)}, bf16[2,512,128]{2,1,0:T(8,128)(2,1)S(1)}, u32[]{:S(2)}, u32[]{:S(2)}) collective-permute-start(bf16[2,512,128]{2,1,0:T(8,128)(2,1)} %ready_keys.1), channel_id=1, source_target_pairs={{0,2},{2,4},{4,6},{6,0},{8,10},{10,12},{12,14},{14,8},{16,18},{18,... | collective-permute-start | bytes 786440 | tf_op jit(solution)/shard_map/ppermute | solution.py:53
  37.6 45.7 %collective-permute-start.1 = (bf16[2,512,128]{2,1,0:T(8,128)(2,1)}, bf16[2,512,128]{2,1,0:T(8,128)(2,1)S(1)}, u32[]{:S(2)}, u32[]{:S(2)}) collective-permute-start(bf16[2,512,128]{2,1,0:T(8,128)(2,1)} %ready_keys.1), channel_id=1, source_target_pairs={{0,4},{2,6},{4,0},{6,2},{8,12},{10,14},{12,8},{14,10},{16,20},{18,... | collective-permute-start | bytes 786440 | tf_op jit(solution)/shard_map/ppermute | solution.py:53
  39.5 47.8 %collective-permute-start.2 = (bf16[2,512,128]{2,1,0:T(8,128)(2,1)}, bf16[2,512,128]{2,1,0:T(8,128)(2,1)S(1)}, u32[]{:S(2)}, u32[]{:S(2)}) collective-permute-start(bf16[2,512,128]{2,1,0:T(8,128)(2,1)} %ready_keys.1), channel_id=1, source_target_pairs={{0,6},{2,0},{4,2},{6,4},{8,14},{10,8},{12,10},{14,12},{16,22},{18,... | collective-permute-start | bytes 786440 | tf_op jit(solution)/shard_map/ppermute | solution.py:53
  89.4 26.1 %collective-permute-start.3 = (bf16[4,2,512,128]{3,2,1,0:T(8,128)(2,1)}, bf16[4,2,512,128]{3,2,1,0:T(8,128)(2,1)}, u32[]{:S(2)}, u32[]{:S(2)}) collective-permute-start(bf16[4,2,512,128]{3,2,1,0:T(8,128)(2,1)} %pad_maximum_fusion.1.kv_ref), channel_id=1, source_target_pairs={{0,8},{2,10},{4,12},{6,14},{8,16},{10,18},{12,20},{14,22},{16,24},... | collective-permute-start | bytes 3145736 | tf_op jit(solution)/shard_map/ppermute | solution.py:58
  91.5 25.1 %collective-permute-start.4 = (bf16[4,2,512,128]{3,2,1,0:T(8,128)(2,1)}, bf16[4,2,512,128]{3,2,1,0:T(8,128)(2,1)}, u32[]{:S(2)}, u32[]{:S(2)}) collective-permute-start(bf16[4,2,512,128]{3,2,1,0:T(8,128)(2,1)} %pad_maximum_fusion.1.kv_ref), channel_id=1, source_target_pairs={{0,24},{2,26},{4,28},{6,30},{8,0},{10,2},{12,4},{14,6},{16,8},{18,... | collective-permute-start | bytes 3145736 | tf_op jit(solution)/shard_map/ppermute | solution.py:59
  116.5 15.7 %collective-permute-start.5 = (bf16[2,2,512,128]{3,2,1,0:T(8,128)(2,1)S(1)}, bf16[2,2,512,128]{3,2,1,0:T(8,128)(2,1)}, u32[]{:S(2)}, u32[]{:S(2)}) collective-permute-start(bf16[2,2,512,128]{3,2,1,0:T(8,128)(2,1)S(1)} %slice.32), channel_id=1, source_target_pairs={{0,8},{2,10},{4,12},{6,14},{8,16},{10,18},{12,20},{14,22},{16,24},... | collective-permute-start | bytes 1572872 | tf_op jit(solution)/shard_map/ppermute | solution.py:60
  117.7 14.5 %collective-permute-start.6 = (bf16[2,2,512,128]{3,2,1,0:T(8,128)(2,1)S(1)}, bf16[2,2,512,128]{3,2,1,0:T(8,128)(2,1)}, u32[]{:S(2)}, u32[]{:S(2)}) collective-permute-start(bf16[2,2,512,128]{3,2,1,0:T(8,128)(2,1)S(1)} %slice.33), channel_id=1, source_target_pairs={{0,24},{2,26},{4,28},{6,30},{8,0},{10,2},{12,4},{14,6},{16,8},{18,... | collective-permute-start | bytes 1572872 | tf_op jit(solution)/shard_map/ppermute | solution.py:61
  122.8 23.8 %collective-permute-start.13 = (bf16[2,1024,256]{2,1,0:T(8,128)(2,1)}, bf16[2,1024,256]{2,1,0:T(8,128)(2,1)}, u32[]{:S(2)}, u32[]{:S(2)}) collective-permute-start(bf16[2,1024,256]{2,1,0:T(8,128)(2,1)} %slice.35), channel_id=1, source_target_pairs={{0,6},{2,0},{4,2},{6,4},{8,14},{10,8},{12,10},{14,12},{16,22},{18,... | collective-permute-start | bytes 3145736 | tf_op jit(solution)/shard_map/ppermute | solution.py:61
  126.6 30.6 %collective-permute-start.12 = (bf16[2,1024,256]{2,1,0:T(8,128)(2,1)}, bf16[2,1024,256]{2,1,0:T(8,128)(2,1)}, u32[]{:S(2)}, u32[]{:S(2)}) collective-permute-start(bf16[2,1024,256]{2,1,0:T(8,128)(2,1)} %slice.34), channel_id=1, source_target_pairs={{0,2},{2,4},{4,6},{6,0},{8,10},{10,12},{12,14},{14,8},{16,18},{18,... | collective-permute-start | bytes 3145736 | tf_op jit(solution)/shard_map/ppermute | solution.py:60
  153.9 10.9 %copy-start.10 = (s32[1,64,2,8]{1,3,2,0:T(8,128)S(1)}, s32[1,64,2,8]{1,3,2,0:T(8,128)}, u32[]{:S(2)}) copy-start(s32[1,64,2,8]{1,3,2,0:T(8,128)} %param.22) | copy-start | bytes 12292
  153.9 11.2 %copy-start.2 = (bf16[256,2048]{1,0:T(8,128)(2,1)S(1)}, bf16[256,2048]{1,0:T(8,128)(2,1)}, u32[]{:S(2)}) copy-start(bf16[256,2048]{1,0:T(8,128)(2,1)} %get-tuple-element.26.k1) | copy-start | bytes 3145732
  153.9 11.2 %collective-permute-start.15 = (bf16[256,2048]{1,0:T(8,128)(2,1)}, bf16[256,2048]{1,0:T(8,128)(2,1)S(1)}, u32[]{:S(2)}, u32[]{:S(2)}) collective-permute-start(bf16[256,2048]{1,0:T(8,128)(2,1)} %get-tuple-element.28), channel_id=1, source_target_pairs={{0,32},{32,0},{64,96},{96,64},{1,33},{33,1},{65,97},{97,65},{2,34}... | collective-permute-start | bytes 3145736 | tf_op jit(solution)/shard_map/ppermute | solution.py:659
  164.5 3.1 collective-permute-start.14
  165.1 9.8 %copy-start.3 = (bf16[256,2048]{1,0:T(8,128)(2,1)}, bf16[256,2048]{1,0:T(8,128)(2,1)S(1)}, u32[]{:S(2)}) copy-start(bf16[256,2048]{1,0:T(8,128)(2,1)S(1)} %collective-permute-done.15.g1) | copy-start | bytes 3145732
  165.2 8.1 %copy-start.4 = (bf16[1,64,2,4096]{3,2,1,0:T(2,128)(2,1)S(1)}, bf16[1,64,2,4096]{3,2,1,0:T(2,128)(2,1)}, u32[]{:S(2)}) copy-start(bf16[1,64,2,4096]{3,2,1,0:T(2,128)(2,1)} %param.19) | copy-start | bytes 3145732
  165.3 14.8 %collective-permute-start.17 = (bf16[128,2048]{1,0:T(8,128)(2,1)S(1)}, bf16[128,2048]{1,0:T(8,128)(2,1)}, u32[]{:S(2)}, u32[]{:S(2)}) collective-permute-start(bf16[128,2048]{1,0:T(8,128)(2,1)S(1)} %add_convert_fusion), channel_id=1, source_target_pairs={{0,64},{32,96},{64,0},{96,32},{1,65},{33,97},{65,1},{97,33},{2,66}... | collective-permute-start | bytes 1572872 | tf_op jit(solution)/shard_map/ppermute | solution.py:663
  169.8 21.5 %collective-permute-start.16 = (bf16[128,2048]{1,0:T(8,128)(2,1)}, bf16[128,2048]{1,0:T(8,128)(2,1)}, u32[]{:S(2)}, u32[]{:S(2)}) collective-permute-start(bf16[128,2048]{1,0:T(8,128)(2,1)} %add_convert_fusion.1), channel_id=1, source_target_pairs={{0,64},{32,96},{64,0},{96,32},{1,65},{33,97},{65,1},{97,33},{2,66}... | collective-permute-start | bytes 1572872 | tf_op jit(solution)/shard_map/ppermute | solution.py:663
  280.2 68.0 %all-to-all-start.2 = ((bf16[64,288,128]{2,1,0:T(8,128)(2,1)}), bf16[64,288,128]{2,1,0:T(8,128)(2,1)}, u32[]{:S(2)}, u32[]{:S(2)}) async-start(bf16[64,288,128]{2,1,0:T(8,128)(2,1)} %get-tuple-element.30), calls=%async_computation.2 | async-start | bytes 9437184 | tf_op jit(solution)/shard_map/all_to_all | solution.py:667
  348.3 59.7 %all-to-all-start.1 = ((bf16[64,256,128]{2,1,0:T(8,128)(2,1)}), bf16[64,256,128]{2,1,0:T(8,128)(2,1)}, u32[]{:S(2)}, u32[]{:S(2)}) async-start(bf16[64,256,128]{2,1,0:T(8,128)(2,1)} %experts_a.1), calls=%async_computation.1 | async-start | bytes 8388608 | tf_op jit(solution)/shard_map/all_to_all | solution.py:667
  376.1 42.4 %copy-start.5 = (bf16[128,4096]{1,0:T(8,128)(2,1)S(1)}, bf16[128,4096]{1,0:T(8,128)(2,1)}, u32[]{:S(2)}) copy-start(bf16[128,4096]{1,0:T(8,128)(2,1)} %get-tuple-element.32) | copy-start | bytes 3145732
  407.9 71.7 %all-to-all-start.3 = ((bf16[64,288,128]{2,1,0:T(8,128)(2,1)}), bf16[64,288,128]{2,1,0:T(8,128)(2,1)}, u32[]{:S(2)}, u32[]{:S(2)}) async-start(bf16[64,288,128]{2,1,0:T(8,128)(2,1)} %experts_b.1), calls=%async_computation.3 | async-start | bytes 9437184 | tf_op jit(solution)/shard_map/all_to_all | solution.py:667

commit v4 on v3

--- a/solution.py
+++ b/solution.py
@@ -140,10 +140,15 @@
 def attn_first(sc, q_ref, cos_ref, sin_ref, gain_ref, kv_ref, qr_ref, m_ref, acc_ref, s_buf):
     y = sc[3]
     cs, sn, gain = cos_ref[...], sin_ref[...], gain_ref[...]
-    for h in range(HEADS):
-        q = q_ref[:, h * HD : (h + 1) * HD].astype(F32)
+
+    def turn_head(h, _):
+        lanes = pl.ds(pl.multiple_of(h * HD, HD), HD)
+        q = q_ref[:, lanes].astype(F32)
         q = q * lax.rsqrt(jnp.mean(q * q, axis=-1, keepdims=True) + eps_norm) * gain
-        qr_ref[:, h * HD : (h + 1) * HD] = (q * cs + pltpu.roll(q, HD // 2, 1) * sn).astype(BF)
+        qr_ref[:, lanes] = (q * cs + pltpu.roll(q, HD // 2, 1) * sn).astype(BF)
+        return 0
+
+    lax.fori_loop(0, HEADS, turn_head, 0)
 
     def mask(j, s):
         if j > 0:
@@ -272,17 +277,17 @@
 
 
 def proj_kernel(part, sc, a_ref, *rest):
-    w_in, (keep, send, lhs, w, sem) = rest[:4], rest[4:]
+    w_in, (keep, send, lhs, w, sem) = rest[:8], rest[8:]
     c, xh = sc[0], sc[1]
     two = pl.ds(2 * part, 2)
-    moves = [
-        (w_in[0].at[two], w.at[:, 0]),
-        (w_in[1].at[two], w.at[:, 1]),
-        (w_in[2].at[two], w.at[:, 3]),
-        (w_in[3], w.at[:, 2]),
-    ]
-    copies = [pltpu.make_async_copy(a, b, sem.at[i]) for i, (a, b) in enumerate(moves)]
-    for cp in copies:
+    moves = []
+    for half in range(2):
+        rows = pl.ds(half * 512, 512)
+        for k, dy in enumerate((0, 1, 3)):
+            moves.append((dy, w_in[4 * half + k].at[two], w.at[:, dy, rows]))
+        moves.append((2, w_in[4 * half + 3], w.at[:, 2, rows]))
+    copies = [(d, pltpu.make_async_copy(a, b, sem.at[i])) for i, (d, a, b) in enumerate(moves)]
+    for _, cp in copies:
         cp.start()
     for cc in (1, 0):
         for xx in range(2):
@@ -290,21 +295,19 @@
             for s in range(SEQ):
                 at = cc * 256 + xx * 128 + s * 64
                 lhs[at : at + 64, :] = a_ref[pl.ds(base, 64), s * 1024 : (s + 1) * 1024]
-    for cp, dy in zip(copies, (0, 1, 3, 2)):
-        cp.wait()
-
-        def column(i, _, dy=dy):
+    for dy in (0, 1, 3, 2):
+        for d, cp in copies:
+            if d == dy:
+                cp.wait()
+        for i in range(2):
             res = jnp.dot(lhs[...], w[i, dy], preferred_element_type=F32).astype(BF)
-            lane = pl.multiple_of((i * 4 + dy) * 256, 256)
-            keep[:, pl.ds(lane, 256)] = res[:256]
-            send[:, pl.ds(lane, 256)] = res[256:]
-            return 0
-
-        lax.fori_loop(0, 2, column, 0)
-
-
-def project(part, scal, attn, pa):
-    pieces = list(pa[:3]) + [pa[3 + part]]
+            lane = (i * 4 + dy) * 256
+            keep[:, lane : lane + 256] = res[:256]
+            send[:, lane : lane + 256] = res[256:]
+
+
+def project(part, scal, attn, halves):
+    pieces = [x for h in halves for x in (h[0], h[1], h[2], h[3 + part])]
     full = pl.BlockSpec(memory_space=pltpu.VMEM)
     return pl.pallas_call(
         functools.partial(proj_kernel, part),
@@ -318,7 +321,7 @@
         scratch_shapes=[
             pltpu.VMEM((512, 1024), BF),
             pltpu.VMEM((2, 4, 1024, 256), BF),
-            pltpu.SemaphoreType.DMA((4,)),
+            pltpu.SemaphoreType.DMA((8,)),
         ],
         compiler_params=pltpu.CompilerParams(vmem_limit_bytes=VMEM_BIG),
         cost_estimate=pl.CostEstimate(
@@ -341,11 +344,16 @@
 
 
 def pick_kernel(tgt_ref, o_ref):
-    line = lax.broadcasted_iota(jnp.int32, (NALL, ROWS), 0)
-    hit = jnp.zeros((NALL, ROWS), F32)
-    for k in range(TOP):
-        hit = jnp.where(line == tgt_ref[k : k + 1, :], 1.0, hit)
-    o_ref[...] = hit.astype(BF)
+    def block(b, _):
+        base = pl.multiple_of(b * 64, 64)
+        line = lax.broadcasted_iota(jnp.int32, (64, ROWS), 0) + base
+        hit = jnp.zeros((64, ROWS), F32)
+        for k in range(TOP):
+            hit = jnp.where(line == tgt_ref[k : k + 1, :], 1.0, hit)
+        o_ref[pl.ds(base, 64), :] = hit.astype(BF)
+        return 0
+
+    lax.fori_loop(0, NALL // 64, block, 0)
 
 
 def picking(tgt_t):
@@ -385,20 +393,23 @@
         to = xa_hbm if chunk == 0 else xb_hbm
         return pltpu.make_async_copy(x_ref.at[chunk, :, rows], to.at[:, rows], sem.at[chunk, j])
 
-    for chunk in range(2):
-
-        def send_part(j, _, chunk=chunk):
+    def send_part(it, _):
+        for jj in range(2):
+            j = 2 * it + jj
             n = nm_ref[:, pl.ds(pl.multiple_of(j * 512, 512), 512)]
-            main = jnp.dot(
-                pick[chunk * NHALF : (chunk + 1) * NHALF, :], n, preferred_element_type=F32
-            )
-            for i in range(2):
-                at = pl.multiple_of(j * 32 + i * 16, 16)
-                x_ref[chunk, :, pl.ds(at, 16), :] = pair_tile(main[:, i * 256 : (i + 1) * 256])
-            out_copy(chunk, j).start()
-            return 0
-
-        lax.fori_loop(0, 8, send_part, 0)
+            for chunk in range(2):
+                main = jnp.dot(
+                    pick[chunk * NHALF : (chunk + 1) * NHALF, :], n, preferred_element_type=F32
+                )
+                for i in range(2):
+                    at = pl.multiple_of(j * 32 + i * 16, 16)
+                    x_ref[chunk, :, pl.ds(at, 16), :] = pair_tile(
+                        main[:, i * 256 : (i + 1) * 256]
+                    )
+                out_copy(chunk, j).start()
+        return 0
+
+    lax.fori_loop(0, 4, send_part, 0)
     ov = jnp.dot(pick[NMAIN:, :], nm_ref[...], preferred_element_type=F32).astype(BF)
     x_ref[1, :, XA:XB, :] = ov.reshape(NE, 32, 128)
     out_copy(1, 8).start()
@@ -542,16 +553,22 @@
 
 
 def mix_kernel(tgt_ref, gate_ref, gm, go):
-    lane = lax.broadcasted_iota(jnp.int32, (ROWS, NALL), 1)
-    mix = jnp.zeros((ROWS, NALL), F32)
-    for k in range(TOP):
-        mix = jnp.where(lane == tgt_ref[:, k : k + 1], gate_ref[:, k : k + 1], mix)
-    hi = mix.astype(BF)
-    lo = (mix - hi.astype(F32)).astype(BF)
-    gm[:ROWS] = hi[:, :NMAIN]
-    gm[ROWS:] = lo[:, :NMAIN]
-    go[:ROWS] = hi[:, NMAIN:]
-    go[ROWS:] = lo[:, NMAIN:]
+    def block(b, _):
+        base = pl.multiple_of(b * 32, 32)
+        own, other = pl.ds(base, 32), pl.ds(base + ROWS, 32)
+        lane = lax.broadcasted_iota(jnp.int32, (32, NALL), 1)
+        mix = jnp.zeros((32, NALL), F32)
+        for k in range(TOP):
+            mix = jnp.where(lane == tgt_ref[own, k : k + 1], gate_ref[own, k : k + 1], mix)
+        hi = mix.astype(BF)
+        lo = (mix - hi.astype(F32)).astype(BF)
+        gm[own, :] = hi[:, :NMAIN]
+        gm[other, :] = lo[:, :NMAIN]
+        go[own, :] = hi[:, NMAIN:]
+        go[other, :] = lo[:, NMAIN:]
+        return 0
+
+    lax.fori_loop(0, ROWS // 32, block, 0)
 
 
 def mixing(tgt, gates):
@@ -566,46 +583,61 @@
     )(tgt, gates)
 
 
-def combine_kernel(ya_ref, yb_ref, yo_ref, st_ref, gm_ref, go_ref, o_ref, yov):
-    step = pl.program_id(0)
-
-    @pl.when(step == 0)
-    def _():
-        yov[...] = yo_ref[...].reshape(NE, DM)
-
-    main = jnp.concatenate([open_tiles(ya_ref, 4), open_tiles(yb_ref, 4)], axis=0)
-    at = pl.multiple_of(step * 1024, 1024)
-    both = jnp.dot(gm_ref[...], main, preferred_element_type=F32) + jnp.dot(
-        go_ref[...], yov[:, pl.ds(at, 1024)], preferred_element_type=F32
-    )
+def combine_first(y_ref, st_ref, gm_ref, o_ref):
+    both = jnp.dot(gm_ref[...], open_tiles(y_ref, 4), preferred_element_type=F32)
     r = lax.broadcasted_iota(jnp.int32, (ROWS, ROWS), 0)
     c = lax.broadcasted_iota(jnp.int32, (ROWS, ROWS), 1)
     turn = jnp.where(c == (r & 1) * 64 + (r >> 1), 1.0, 0.0).astype(BF)
     st = jnp.dot(turn, st_ref[...], preferred_element_type=F32)
-    o_ref[...] = (st + (both[:ROWS] + both[ROWS:])).astype(BF)
+    o_ref[...] = st + (both[:ROWS] + both[ROWS:])
+
+
+def combine_last(y_ref, yo_ref, sum_ref, gm_ref, go_ref, o_ref, yov):
+    step = pl.program_id(0)
+
+    @pl.when(step == 0)
+    def _():
+        yov[...] = yo_ref[...].reshape(NE, DM)
+
+    at = pl.multiple_of(step * 1024, 1024)
+    both = jnp.dot(gm_ref[...], open_tiles(y_ref, 4), preferred_element_type=F32) + jnp.dot(
+        go_ref[...], yov[:, pl.ds(at, 1024)], preferred_element_type=F32
+    )
+    o_ref[...] = (sum_ref[...] + (both[:ROWS] + both[ROWS:])).astype(BF)
 
 
 def combine(ya, yb, stream, gm, go):
+    tile = pl.BlockSpec((NE, 64, 128), lambda i: (0, i, 0))
+    line = pl.BlockSpec((ROWS, 1024), lambda i: (0, i))
+    params = pltpu.CompilerParams(vmem_limit_bytes=VMEM_BIG)
+    cost = pl.CostEstimate(flops=2**30, bytes_accessed=6 * 2**20, transcendentals=0)
+    total = pl.pallas_call(
+        combine_first,
+        grid=(4,),
+        out_shape=jax.ShapeDtypeStruct((ROWS, DM), F32),
+        in_specs=[tile, line, pl.BlockSpec((2 * ROWS, NHALF), lambda i: (0, 0))],
+        out_specs=line,
+        compiler_params=params,
+        cost_estimate=cost,
+        name="combine_first",
+    )(ya, stream, gm)
     return pl.pallas_call(
-        combine_kernel,
+        combine_last,
         grid=(4,),
         out_shape=jax.ShapeDtypeStruct((ROWS, DM), BF),
         in_specs=[
-            pl.BlockSpec((NE, 64, 128), lambda i: (0, i, 0)),
-            pl.BlockSpec((NE, 64, 128), lambda i: (0, i, 0)),
+            tile,
             pl.BlockSpec((NE, 32, 128), lambda i: (0, 8, 0)),
-            pl.BlockSpec((ROWS, 1024), lambda i: (0, i)),
-            pl.BlockSpec((2 * ROWS, NMAIN), lambda i: (0, 0)),
+            line,
+            pl.BlockSpec((2 * ROWS, NHALF), lambda i: (0, 1)),
             pl.BlockSpec((2 * ROWS, NE), lambda i: (0, 0)),
         ],
-        out_specs=pl.BlockSpec((ROWS, 1024), lambda i: (0, i)),
+        out_specs=line,
         scratch_shapes=[pltpu.VMEM((NE, DM), BF)],
-        compiler_params=pltpu.CompilerParams(vmem_limit_bytes=VMEM_BIG),
-        cost_estimate=pl.CostEstimate(
-            flops=2 * 2**30, bytes_accessed=11 * 2**20, transcendentals=0
-        ),
-        name="combine",
-    )(ya, yb, yb, stream, gm, go)
+        compiler_params=params,
+        cost_estimate=cost,
+        name="combine_last",
+    )(yb, yb, total, gm, go)
 
 
 def slots(ids):
@@ -643,7 +675,10 @@
         keys[0].reshape(PB, SEQ * HD), values[0].reshape(PB, SEQ * HD), cs, sn, k_gain.reshape(1, HD)
     )
     kv_all = ring_relay(jnp.stack(ring_four(kv, y_move)), z_move)
-    w_all = ring_relay(jnp.stack(ring_four(out_weight, z_move)), y_move)
+    w_all = [
+        ring_relay(jnp.stack(ring_four(w, z_move)), y_move)
+        for w in (out_weight[:512], out_weight[512:])
+    ]
 
     q2 = queries[0].reshape(PB, SEQ * 1024)
     ids = expert_ids[0].reshape(ROWS, TOP)

time: 491 us -> 474 us (0.965)
  waiting for transfers between devices: 230 us -> 188 us
  starting transfers between devices: 54.4 us -> 67.5 us
  local copies, waits for them, and re-layouts: 16.4 us -> 24.1 us
    ppermute x6 -> x9, waiting for transfers between devices: 67.8 us -> 33 us  [ring_four(): return [x] + [lax.ppermute(x, 'expert', move(k)) for k in (1, 2, 3)]]
    ppermute x2 -> x3, waiting for transfers between devices: 0.01 us -> 9.44 us  [ring_relay(): right = lax.ppermute(x, 'expert', move(3))]
    ppermute x2 -> x3, waiting for transfers between devices: 9.44 us -> 2.37 us  [ring_relay(): hi = lax.ppermute(right[half:], 'expert', move(3))]
    ppermute x2 -> x3, waiting for transfers between devices: 5.97 us -> 0.01 us  [ring_relay(): left = lax.ppermute(x, 'expert', move(1))]
    all_to_all x3, waiting for transfers between devices: 132 us -> 126 us  [exchange(): lax.all_to_all(x, ('tensor', 'expert'), split_axis=0, concat_axis=0, tile...]
    ppermute x6 -> x9, starting transfers between devices: 11 us -> 15.4 us  [ring_four(): return [x] + [lax.ppermute(x, 'expert', move(k)) for k in (1, 2, 3)]]
    pallas_call x1 -> x2, Pallas kernels: 7.44 us -> 11.1 us  [the longest x1 5.8 us: combine(): pl.pallas_call(combine_last, grid=(4,), out_shape=jax.ShapeDtypeStruct((R...]
  transfers between devices with their start and end apart: 21 -> 28, of which waited for: 12 -> 12; matrix products, arithmetic and copies ran while one was open for 4% -> 5% of each run, Pallas kernels for 17% -> 18%
where the time goes in v4:
time: 474 us; the launch traced here: 473 us
  waiting for transfers between devices  188 us (40%)
  Pallas kernels  104 us (22%)
  blocking collectives  80.9 us (17%)
  starting transfers between devices  67.5 us (14%)
  local copies, waits for them, and re-layouts  24.1 us (5%)
  other arithmetic  7.42 us (2%)
    all_to_all x3, waiting for transfers between devices, exchange(): lax.all_to_all(x, ('tensor', 'expert'), split_axis=0, concat_axis=0, tile...  126 us
    all_to_all x1, blocking collectives, exchange(): lax.all_to_all(x, ('tensor', 'expert'), split_axis=0, concat_axis=0, tile...  80.9 us
    pallas_call x2, Pallas kernels, run_experts(): pl.pallas_call(functools.partial(expert_kernel, over), grid=(8,), out_sha...  37.9 us
    ppermute x9, waiting for transfers between devices, ring_four(): return [x] + [lax.ppermute(x, 'expert', move(k)) for k in (1, 2, 3)]  33 us
    all_to_all x3, starting transfers between devices, exchange(): lax.all_to_all(x, ('tensor', 'expert'), split_axis=0, concat_axis=0, tile...  25.4 us
    ppermute x9, starting transfers between devices, ring_four(): return [x] + [lax.ppermute(x, 'expert', move(k)) for k in (1, 2, 3)]  15.4 us
    ppermute x2, waiting for transfers between devices, on_device(): rests.append(lax.ppermute(other, 'tensor', X_SWAP))  14.8 us
    pallas_call x1, Pallas kernels, attention(): attn_call(attn_first, [Q_SPEC, table, table, pl.BlockSpec((1, HD), lambda...  14.4 us
  transfers between devices with their start and end apart: 28, of which 12 were waited for; matrix products, arithmetic and copies ran while one was open for 5% of the time, Pallas kernels for 18%

profile of v4, /device:TPU:11, one launch (start us, length us, event | category | flops | bytes accessed | tf_op | source)
XLA Modules:
  0.0 472.8 jit_solution(4014245852129857008)
XLA Ops:
  0.6 1.7 copy_bitcast_fusion
  2.3 0.8 pad_maximum_fusion.3
  3.1 2.2 ready_keys.1
  5.3 1.3 collective-permute-start
  6.6 0.7 collective-permute-start.1
  7.3 2.1 collective-permute-start.2
  9.4 1.1 slice_bitcast_fusion
  10.5 1.7 collective-permute-start.7
  12.2 3.3 collective-permute-start.8
  15.5 1.0 collective-permute-start.9
  16.5 4.1 collective-permute-done.2
  20.6 2.1 pad_maximum_fusion.kv_ref
  22.7 1.6 collective-permute-start.3
  24.3 1.6 collective-permute-start.13
  25.9 1.7 collective-permute-start.14
  27.6 2.1 collective-permute-start.15
  29.9 24.8 %collective-permute-done.13 = bf16[512,256]{1,0:T(8,128)(2,1)S(1)} collective-permute-done((bf16[512,256]{1,0:T(8,128)(2,1)S(1)}, bf16[512,256]{1,0:T(8,128)(2,1)S(1)}, u32[]{:S(2)}, u32[]{:S(2)}) %collective-permute-start.13) | collective-permute-done | bytes 262176 | tf_op jit(solution)/shard_map/ppermute | solution.py:53
  54.7 2.3 collective-permute-start.11
  57.0 4.0 collective-permute-done.14
  61.4 1.4 collective-permute-start.10
  62.7 2.5 copy.49
  65.8 2.0 collective-permute-start.16
  67.8 14.4 %shard_map.127 = (bf16[256,2048]{1,0:T(8,128)(2,1)}, f32[16,8,256]{2,1,0:T(8,128)}, f32[16,144,256]{2,1,0:T(8,128)}) custom-call(s32[4]{0:T(128)} %pad_add_fusion.sc, bf16[256,2048]{1,0:T(8,128)(2,1)} %bitcast.62, f32[256,128]{1,0:T(8,128)} %get-tuple-element.50.cos_ref, f32[256,128]{1,0:T(8,128)} %get-tuple-element.51.sin_ref, f32[1,128]{1,0:T(1,128)} %bitcast.82, ...), custom_call_target="tpu_custom_call" | custom-call | flops 4294967296 | bytes 8388608 | tf_op jit(solution)/shard_map/pallas_call | solution.py:260
  82.1 1.9 slice.48
  84.0 1.9 slice.49
  85.9 2.7 collective-permute-start.6
  88.5 1.9 slice.52
  90.4 9.4 %collective-permute-done.17.rest_6_ = bf16[4,512,256]{2,1,0:T(8,128)(2,1)} collective-permute-done((bf16[4,512,256]{2,1,0:T(8,128)(2,1)S(1)}, bf16[4,512,256]{2,1,0:T(8,128)(2,1)}, u32[]{:S(2)}, u32[]{:S(2)}) %collective-permute-start.17) | collective-permute-done | bytes 1048608 | tf_op jit(solution)/shard_map/ppermute | solution.py:59
  99.9 2.5 collective-permute-start.19
  102.4 1.9 slice.53
  104.3 3.5 collective-permute-start.20
  107.8 4.4 shard_map.128
  112.2 1.9 slice.50
  114.1 1.9 slice.51
  116.0 4.9 %shard_map.129.a_ref = bf16[256,2048]{1,0:T(8,128)(2,1)} custom-call(s32[4]{0:T(128)} %pad_add_fusion.sc, bf16[256,2048]{1,0:T(8,128)(2,1)} %get-tuple-element.20.q_ref, f32[16,8,256]{2,1,0:T(8,128)} %get-tuple-element.23.m_in, f32[16,144,256]{2,1,0:T(8,128)} %get-tuple-element.24.acc_in, bf16[2,2,512,128]{3,2,1,0:T(8,128)(2,1)} %collective-permute-done.5.ka_ref, ...), custom_call_target="tpu_custom_call" | custom-call | flops 4294967296 | bytes 8388608 | tf_op jit(solution)/shard_map/pallas_call | solution.py:270
  120.9 2.4 collective-permute-done.20.rest_7_
  123.3 0.8 copy-done.8
  124.0 7.1 %shard_map.131 = (bf16[256,2048]{1,0:T(8,128)(2,1)}, bf16[256,2048]{1,0:T(8,128)(2,1)}) custom-call(s32[4]{0:T(128)} %pad_add_fusion.sc, bf16[256,2048]{1,0:T(8,128)(2,1)} %shard_map.129.a_ref, bf16[4,512,256]{2,1,0:T(8,128)(2,1)} %copy-done.1, bf16[4,512,256]{2,1,0:T(8,128)(2,1)} %collective-permute-done.10.rest_1_, ...), custom_call_target="tpu_custom_call" | custom-call | flops 2147483648 | bytes 7340032 | tf_op jit(solution)/shard_map/pallas_call | solution.py:312
  131.2 3.2 collective-permute-start.22
  134.4 2.2 collective-permute-done.18.rest_7_
  136.7 7.1 %shard_map.130 = (bf16[256,2048]{1,0:T(8,128)(2,1)}, bf16[256,2048]{1,0:T(8,128)(2,1)}) custom-call(s32[4]{0:T(128)} %pad_add_fusion.sc, bf16[256,2048]{1,0:T(8,128)(2,1)} %shard_map.129.a_ref, bf16[4,512,256]{2,1,0:T(8,128)(2,1)} %copy-done.1, bf16[4,512,256]{2,1,0:T(8,128)(2,1)} %collective-permute-done.10.rest_1_, ...), custom_call_target="tpu_custom_call" | custom-call | flops 2147483648 | bytes 7340032 | tf_op jit(solution)/shard_map/pallas_call | solution.py:312
  143.8 3.4 collective-permute-start.21
  147.7 1.9 collective-permute-start.24
  149.8 1.3 add_convert_fusion.1
  151.1 1.9 collective-permute-start.23
  154.7 2.8 copy.39
  157.5 1.8 picking.1.pick
  159.3 3.4 collective-permute-done.24.r1
  162.7 11.3 %collective-permute-done.23.r0 = bf16[128,2048]{1,0:T(8,128)(2,1)} collective-permute-done((bf16[128,2048]{1,0:T(8,128)(2,1)S(1)}, bf16[128,2048]{1,0:T(8,128)(2,1)}, u32[]{:S(2)}, u32[]{:S(2)}) %collective-permute-start.23) | collective-permute-done | bytes 524320 | tf_op jit(solution)/shard_map/ppermute | solution.py:698
  174.1 10.1 %dispatch.1 = (bf16[128,4096]{1,0:T(8,128)(2,1)}, bf16[128,4096]{1,0:T(8,128)(2,1)}, bf16[64,256,128]{2,1,0:T(8,128)(2,1)}, bf16[64,288,128]{2,1,0:T(8,128)(2,1)}) custom-call(s32[4]{0:T(128)} %pad_add_fusion.sc, bf16[256,2048]{1,0:T(8,128)(2,1)} %get-tuple-element.25.k0, bf16[256,2048]{1,0:T(8,128)(2,1)} %get-tuple-element.26.k1, ...), custom_call_target="tpu_custom_call" | custom-call | flops 1073741824 | bytes 14680064 | tf_op jit(solution)/shard_map/dispatch/pallas_call | solution.py:425
  184.2 80.9 %all_to_all.20.refs_0_ = bf16[64,256,128]{2,1,0:T(8,128)(2,1)} all-to-all(bf16[64,256,128]{2,1,0:T(8,128)(2,1)} %get-tuple-element.30), channel_id=1, replica_groups=mesh['tensor'=4,'expert'=16,'dp'=2] {'tensor','expert'}, dimensions={0} | all-to-all | bytes 8388608 | tf_op jit(solution)/shard_map/all_to_all | solution.py:702
  265.1 6.9 %all-to-all-start = ((bf16[64,288,128]{2,1,0:T(8,128)(2,1)}), bf16[64,288,128]{2,1,0:T(8,128)(2,1)}, u32[]{:S(2)}, u32[]{:S(2)}) async-start(bf16[64,288,128]{2,1,0:T(8,128)(2,1)} %get-tuple-element.29), calls=%async_computation | async-start | bytes 9437184 | tf_op jit(solution)/shard_map/all_to_all | solution.py:702
  272.0 18.0 %experts_a.1 = bf16[64,256,128]{2,1,0:T(8,128)(2,1)} custom-call(bf16[64,256,128]{2,1,0:T(8,128)(2,1)} %all_to_all.20.refs_0_, bf16[1,4096,768]{2,1,0:T(8,128)(2,1)} %refs_1_.1, bf16[1,4096,768]{2,1,0:T(8,128)(2,1)} %refs_2_.3, bf16[1,768,4096]{2,1,0:T(8,128)(2,1)} %refs_3_.3), custom_call_target="tpu_custom_call" | custom-call | flops 10737418240 | bytes 28311552 | tf_op jit(solution)/shard_map/experts_a/pallas_call | solution.py:528
  290.1 43.0 %all-to-all-done.refs_0_.refs_1_ = bf16[64,288,128]{2,1,0:T(8,128)(2,1)} async-done(((bf16[64,288,128]{2,1,0:T(8,128)(2,1)}), bf16[64,288,128]{2,1,0:T(8,128)(2,1)}, u32[]{:S(2)}, u32[]{:S(2)}) %all-to-all-start) | async-done | bytes 4718624 | tf_op jit(solution)/shard_map/all_to_all | solution.py:702
  333.1 7.9 %all-to-all-start.3 = ((bf16[64,256,128]{2,1,0:T(8,128)(2,1)}), bf16[64,256,128]{2,1,0:T(8,128)(2,1)}, u32[]{:S(2)}, u32[]{:S(2)}) async-start(bf16[64,256,128]{2,1,0:T(8,128)(2,1)} %experts_a.1), calls=%async_computation.3 | async-start | bytes 8388608 | tf_op jit(solution)/shard_map/all_to_all | solution.py:702
  341.1 19.8 %experts_b.1 = bf16[64,288,128]{2,1,0:T(8,128)(2,1)} custom-call(bf16[64,288,128]{2,1,0:T(8,128)(2,1)} %all-to-all-done.refs_0_.refs_1_, bf16[64,288,128]{2,1,0:T(8,128)(2,1)} %all-to-all-done.refs_0_.refs_1_, bf16[1,4096,768]{2,1,0:T(8,128)(2,1)} %refs_1_.1, bf16[1,4096,768]{2,1,0:T(8,128)(2,1)} %refs_2_.3, bf16[1,768,4096]{2,1,0:T(8,128)(2,1)} %refs_3_.3), custom_call_target="tpu_custom_call" | custom-call | flops 10737418240 | bytes 28311552 | tf_op jit(solution)/shard_map/experts_b/pallas_call | solution.py:528
  360.9 31.9 %all-to-all-done.3.y_ref = bf16[64,256,128]{2,1,0:T(8,128)(2,1)} async-done(((bf16[64,256,128]{2,1,0:T(8,128)(2,1)}), bf16[64,256,128]{2,1,0:T(8,128)(2,1)}, u32[]{:S(2)}, u32[]{:S(2)}) %all-to-all-start.3) | async-done | bytes 4194336 | tf_op jit(solution)/shard_map/all_to_all | solution.py:702
  392.8 10.5 %all-to-all-start.1 = ((bf16[64,288,128]{2,1,0:T(8,128)(2,1)}), bf16[64,288,128]{2,1,0:T(8,128)(2,1)}, u32[]{:S(2)}, u32[]{:S(2)}) async-start(bf16[64,288,128]{2,1,0:T(8,128)(2,1)} %experts_b.1), calls=%async_computation.1 | async-start | bytes 9437184 | tf_op jit(solution)/shard_map/all_to_all | solution.py:702
  404.3 0.7 broadcast_divide_fusion.gate_ref
  405.0 2.7 mixing.1
  407.7 5.3 %combine_first.1.sum_ref = f32[128,4096]{1,0:T(8,128)} custom-call(bf16[64,256,128]{2,1,0:T(8,128)(2,1)} %all-to-all-done.3.y_ref, bf16[128,4096]{1,0:T(8,128)(2,1)} %get-tuple-element.31.st_ref, bf16[256,1024]{1,0:T(8,128)(2,1)} %get-tuple-element.33.gm_ref), custom_call_target="tpu_custom_call" | custom-call | flops 1073741824 | bytes 6291456 | tf_op jit(solution)/shard_map/combine_first/pallas_call | solution.py:614
  413.0 51.5 %all-to-all-done.1.y_ref.yo_ref = bf16[64,288,128]{2,1,0:T(8,128)(2,1)} async-done(((bf16[64,288,128]{2,1,0:T(8,128)(2,1)}), bf16[64,288,128]{2,1,0:T(8,128)(2,1)}, u32[]{:S(2)}, u32[]{:S(2)}) %all-to-all-start.1) | async-done | bytes 4718624 | tf_op jit(solution)/shard_map/all_to_all | solution.py:702
  464.4 5.8 %combine_last.1 = bf16[128,4096]{1,0:T(8,128)(2,1)} custom-call(bf16[64,288,128]{2,1,0:T(8,128)(2,1)} %all-to-all-done.1.y_ref.yo_ref, bf16[64,288,128]{2,1,0:T(8,128)(2,1)} %all-to-all-done.1.y_ref.yo_ref, f32[128,4096]{1,0:T(8,128)} %combine_first.1.sum_ref, bf16[256,1024]{1,0:T(8,128)(2,1)} %get-tuple-element.33.gm_ref, ...), custom_call_target="tpu_custom_call" | custom-call | flops 1073741824 | bytes 6291456 | tf_op jit(solution)/shard_map/combine_last/pallas_call | solution.py:624
  470.2 2.5 reshape.59
  (69 shorter events, 5.0 us)
Async XLA Ops:
  0.0 403.3 %copy-start = (bf16[4096,64]{0,1:T(8,128)(2,1)S(1)}, bf16[4096,64]{0,1:T(8,128)(2,1)}, u32[]{:S(2)}) copy-start(bf16[4096,64]{0,1:T(8,128)(2,1)} %param.21) | copy-start | bytes 1572868
  5.3 10.2 %collective-permute-start = (bf16[2,512,128]{2,1,0:T(8,128)(2,1)}, bf16[2,512,128]{2,1,0:T(8,128)(2,1)S(1)}, u32[]{:S(2)}, u32[]{:S(2)}) collective-permute-start(bf16[2,512,128]{2,1,0:T(8,128)(2,1)} %ready_keys.1), channel_id=1, source_target_pairs={{0,2},{2,4},{4,6},{6,0},{8,10},{10,12},{12,14},{14,8},{16,18},{18,... | collective-permute-start | bytes 786440 | tf_op jit(solution)/shard_map/ppermute | solution.py:53
  6.6 9.9 %collective-permute-start.1 = (bf16[2,512,128]{2,1,0:T(8,128)(2,1)}, bf16[2,512,128]{2,1,0:T(8,128)(2,1)S(1)}, u32[]{:S(2)}, u32[]{:S(2)}) collective-permute-start(bf16[2,512,128]{2,1,0:T(8,128)(2,1)} %ready_keys.1), channel_id=1, source_target_pairs={{0,4},{2,6},{4,0},{6,2},{8,12},{10,14},{12,8},{14,10},{16,20},{18,... | collective-permute-start | bytes 786440 | tf_op jit(solution)/shard_map/ppermute | solution.py:53
  7.3 13.3 %collective-permute-start.2 = (bf16[2,512,128]{2,1,0:T(8,128)(2,1)}, bf16[2,512,128]{2,1,0:T(8,128)(2,1)S(1)}, u32[]{:S(2)}, u32[]{:S(2)}) collective-permute-start(bf16[2,512,128]{2,1,0:T(8,128)(2,1)} %ready_keys.1), channel_id=1, source_target_pairs={{0,6},{2,0},{4,2},{6,4},{8,14},{10,8},{12,10},{14,12},{16,22},{18,... | collective-permute-start | bytes 786440 | tf_op jit(solution)/shard_map/ppermute | solution.py:53
  10.5 15.4 %collective-permute-start.7 = (bf16[512,256]{1,0:T(8,128)(2,1)S(1)}, bf16[512,256]{1,0:T(8,128)(2,1)S(1)}, u32[]{:S(2)}, u32[]{:S(2)}) collective-permute-start(bf16[512,256]{1,0:T(8,128)(2,1)S(1)} %get-tuple-element.42), channel_id=1, source_target_pairs={{0,8},{2,10},{4,12},{6,14},{8,16},{10,18},{12,20},{14,22},{16,24},... | collective-permute-start | bytes 786440 | tf_op jit(solution)/shard_map/ppermute | solution.py:53
  12.2 15.4 %collective-permute-start.8 = (bf16[512,256]{1,0:T(8,128)(2,1)S(1)}, bf16[512,256]{1,0:T(8,128)(2,1)S(1)}, u32[]{:S(2)}, u32[]{:S(2)}) collective-permute-start(bf16[512,256]{1,0:T(8,128)(2,1)S(1)} %get-tuple-element.42), channel_id=1, source_target_pairs={{0,16},{2,18},{4,20},{6,22},{8,24},{10,26},{12,28},{14,30},{16,0},... | collective-permute-start | bytes 786440 | tf_op jit(solution)/shard_map/ppermute | solution.py:53
  15.5 14.2 %collective-permute-start.9 = (bf16[512,256]{1,0:T(8,128)(2,1)S(1)}, bf16[512,256]{1,0:T(8,128)(2,1)S(1)}, u32[]{:S(2)}, u32[]{:S(2)}) collective-permute-start(bf16[512,256]{1,0:T(8,128)(2,1)S(1)} %get-tuple-element.42), channel_id=1, source_target_pairs={{0,24},{2,26},{4,28},{6,30},{8,0},{10,2},{12,4},{14,6},{16,8},{18,... | collective-permute-start | bytes 786440 | tf_op jit(solution)/shard_map/ppermute | solution.py:53
  22.7 43.1 %collective-permute-start.3 = (bf16[4,2,512,128]{3,2,1,0:T(8,128)(2,1)}, bf16[4,2,512,128]{3,2,1,0:T(8,128)(2,1)}, u32[]{:S(2)}, u32[]{:S(2)}) collective-permute-start(bf16[4,2,512,128]{3,2,1,0:T(8,128)(2,1)} %pad_maximum_fusion.kv_ref), channel_id=1, source_target_pairs={{0,8},{2,10},{4,12},{6,14},{8,16},{10,18},{12,20},{14,22},{16,24},... | collective-permute-start | bytes 3145736 | tf_op jit(solution)/shard_map/ppermute | solution.py:58
  24.3 30.4 %collective-permute-start.13 = (bf16[512,256]{1,0:T(8,128)(2,1)S(1)}, bf16[512,256]{1,0:T(8,128)(2,1)S(1)}, u32[]{:S(2)}, u32[]{:S(2)}) collective-permute-start(bf16[512,256]{1,0:T(8,128)(2,1)S(1)} %get-tuple-element.41), channel_id=1, source_target_pairs={{0,8},{2,10},{4,12},{6,14},{8,16},{10,18},{12,20},{14,22},{16,24},... | collective-permute-start | bytes 786440 | tf_op jit(solution)/shard_map/ppermute | solution.py:53
  25.9 35.1 %collective-permute-start.14 = (bf16[512,256]{1,0:T(8,128)(2,1)S(1)}, bf16[512,256]{1,0:T(8,128)(2,1)S(1)}, u32[]{:S(2)}, u32[]{:S(2)}) collective-permute-start(bf16[512,256]{1,0:T(8,128)(2,1)S(1)} %get-tuple-element.41), channel_id=1, source_target_pairs={{0,16},{2,18},{4,20},{6,22},{8,24},{10,26},{12,28},{14,30},{16,0},... | collective-permute-start | bytes 786440 | tf_op jit(solution)/shard_map/ppermute | solution.py:53
  27.6 33.4 %collective-permute-start.15 = (bf16[512,256]{1,0:T(8,128)(2,1)S(1)}, bf16[512,256]{1,0:T(8,128)(2,1)S(1)}, u32[]{:S(2)}, u32[]{:S(2)}) collective-permute-start(bf16[512,256]{1,0:T(8,128)(2,1)S(1)} %get-tuple-element.41), channel_id=1, source_target_pairs={{0,24},{2,26},{4,28},{6,30},{8,0},{10,2},{12,4},{14,6},{16,8},{18,... | collective-permute-start | bytes 786440 | tf_op jit(solution)/shard_map/ppermute | solution.py:53
  29.7 54.3 %collective-permute-start.4 = (bf16[4,2,512,128]{3,2,1,0:T(8,128)(2,1)}, bf16[4,2,512,128]{3,2,1,0:T(8,128)(2,1)}, u32[]{:S(2)}, u32[]{:S(2)}) collective-permute-start(bf16[4,2,512,128]{3,2,1,0:T(8,128)(2,1)} %pad_maximum_fusion.kv_ref), channel_id=1, source_target_pairs={{0,24},{2,26},{4,28},{6,30},{8,0},{10,2},{12,4},{14,6},{16,8},{18,... | collective-permute-start | bytes 3145736 | tf_op jit(solution)/shard_map/ppermute | solution.py:59
  29.9 52.2 %copy-start.1 = (bf16[4,512,256]{2,1,0:T(8,128)(2,1)}, bf16[4,512,256]{2,1,0:T(8,128)(2,1)S(1)}, u32[]{:S(2)}) copy-start(bf16[4,512,256]{2,1,0:T(8,128)(2,1)S(1)} %pad_maximum_fusion.1.rest_0_) | copy-start | bytes 3145732
  54.7 31.1 %collective-permute-start.11 = (bf16[4,512,256]{2,1,0:T(8,128)(2,1)S(1)}, bf16[4,512,256]{2,1,0:T(8,128)(2,1)}, u32[]{:S(2)}, u32[]{:S(2)}) collective-permute-start(bf16[4,512,256]{2,1,0:T(8,128)(2,1)S(1)} %pad_maximum_fusion.1.rest_0_), channel_id=1, source_target_pairs={{0,6},{2,0},{4,2},{6,4},{8,14},{10,8},{12,10},{14,12},{16,22},{18,... | collective-permute-start | bytes 3145736 | tf_op jit(solution)/shard_map/ppermute | solution.py:59
  61.2 21.0 %copy-start.2 = (bf16[4,512,256]{2,1,0:T(8,128)(2,1)}, bf16[4,512,256]{2,1,0:T(8,128)(2,1)S(1)}, u32[]{:S(2)}) copy-start(bf16[4,512,256]{2,1,0:T(8,128)(2,1)S(1)} %pad_maximum_fusion.2.rest_4_) | copy-start | bytes 3145732
  61.2 38.7 %collective-permute-start.17 = (bf16[4,512,256]{2,1,0:T(8,128)(2,1)S(1)}, bf16[4,512,256]{2,1,0:T(8,128)(2,1)}, u32[]{:S(2)}, u32[]{:S(2)}) collective-permute-start(bf16[4,512,256]{2,1,0:T(8,128)(2,1)S(1)} %pad_maximum_fusion.2.rest_4_), channel_id=1, source_target_pairs={{0,6},{2,0},{4,2},{6,4},{8,14},{10,8},{12,10},{14,12},{16,22},{18,... | collective-permute-start | bytes 3145736 | tf_op jit(solution)/shard_map/ppermute | solution.py:59
  61.4 42.9 %collective-permute-start.10 = (bf16[4,512,256]{2,1,0:T(8,128)(2,1)S(1)}, bf16[4,512,256]{2,1,0:T(8,128)(2,1)}, u32[]{:S(2)}, u32[]{:S(2)}) collective-permute-start(bf16[4,512,256]{2,1,0:T(8,128)(2,1)S(1)} %pad_maximum_fusion.1.rest_0_), channel_id=1, source_target_pairs={{0,2},{2,4},{4,6},{6,0},{8,10},{10,12},{12,14},{14,8},{16,18},{18,... | collective-permute-start | bytes 3145736 | tf_op jit(solution)/shard_map/ppermute | solution.py:58
  65.8 48.3 %collective-permute-start.16 = (bf16[4,512,256]{2,1,0:T(8,128)(2,1)S(1)}, bf16[4,512,256]{2,1,0:T(8,128)(2,1)}, u32[]{:S(2)}, u32[]{:S(2)}) collective-permute-start(bf16[4,512,256]{2,1,0:T(8,128)(2,1)S(1)} %pad_maximum_fusion.2.rest_4_), channel_id=1, source_target_pairs={{0,2},{2,4},{4,6},{6,0},{8,10},{10,12},{12,14},{14,8},{16,18},{18,... | collective-permute-start | bytes 3145736 | tf_op jit(solution)/shard_map/ppermute | solution.py:58
  84.0 32.0 %collective-permute-start.5 = (bf16[2,2,512,128]{3,2,1,0:T(8,128)(2,1)}, bf16[2,2,512,128]{3,2,1,0:T(8,128)(2,1)}, u32[]{:S(2)}, u32[]{:S(2)}) collective-permute-start(bf16[2,2,512,128]{3,2,1,0:T(8,128)(2,1)} %slice.48), channel_id=1, source_target_pairs={{0,8},{2,10},{4,12},{6,14},{8,16},{10,18},{12,20},{14,22},{16,24},... | collective-permute-start | bytes 1572872 | tf_op jit(solution)/shard_map/ppermute | solution.py:60
  85.9 30.2 %collective-permute-start.6 = (bf16[2,2,512,128]{3,2,1,0:T(8,128)(2,1)}, bf16[2,2,512,128]{3,2,1,0:T(8,128)(2,1)}, u32[]{:S(2)}, u32[]{:S(2)}) collective-permute-start(bf16[2,2,512,128]{3,2,1,0:T(8,128)(2,1)} %slice.49), channel_id=1, source_target_pairs={{0,24},{2,26},{4,28},{6,30},{8,0},{10,2},{12,4},{14,6},{16,8},{18,... | collective-permute-start | bytes 1572872 | tf_op jit(solution)/shard_map/ppermute | solution.py:61
  99.9 21.0 %collective-permute-start.19 = (bf16[2,512,256]{2,1,0:T(8,128)(2,1)}, bf16[2,512,256]{2,1,0:T(8,128)(2,1)S(1)}, u32[]{:S(2)}, u32[]{:S(2)}) collective-permute-start(bf16[2,512,256]{2,1,0:T(8,128)(2,1)} %slice.52), channel_id=1, source_target_pairs={{0,6},{2,0},{4,2},{6,4},{8,14},{10,8},{12,10},{14,12},{16,22},{18,... | collective-permute-start | bytes 1572872 | tf_op jit(solution)/shard_map/ppermute | solution.py:61
  104.3 19.0 %collective-permute-start.20 = (bf16[2,512,256]{2,1,0:T(8,128)(2,1)}, bf16[2,512,256]{2,1,0:T(8,128)(2,1)S(1)}, u32[]{:S(2)}, u32[]{:S(2)}) collective-permute-start(bf16[2,512,256]{2,1,0:T(8,128)(2,1)} %slice.53), channel_id=1, source_target_pairs={{0,6},{2,0},{4,2},{6,4},{8,14},{10,8},{12,10},{14,12},{16,22},{18,... | collective-permute-start | bytes 1572872 | tf_op jit(solution)/shard_map/ppermute | solution.py:61
  114.1 20.3 %collective-permute-start.12 = (bf16[2,512,256]{2,1,0:T(8,128)(2,1)}, bf16[2,512,256]{2,1,0:T(8,128)(2,1)S(1)}, u32[]{:S(2)}, u32[]{:S(2)}) collective-permute-start(bf16[2,512,256]{2,1,0:T(8,128)(2,1)} %slice.50), channel_id=1, source_target_pairs={{0,2},{2,4},{4,6},{6,0},{8,10},{10,12},{12,14},{14,8},{16,18},{18,... | collective-permute-start | bytes 1572872 | tf_op jit(solution)/shard_map/ppermute | solution.py:60
  116.0 20.6 %collective-permute-start.18 = (bf16[2,512,256]{2,1,0:T(8,128)(2,1)}, bf16[2,512,256]{2,1,0:T(8,128)(2,1)}, u32[]{:S(2)}, u32[]{:S(2)}) collective-permute-start(bf16[2,512,256]{2,1,0:T(8,128)(2,1)} %slice.51), channel_id=1, source_target_pairs={{0,2},{2,4},{4,6},{6,0},{8,10},{10,12},{12,14},{14,8},{16,18},{18,... | collective-permute-start | bytes 1572872 | tf_op jit(solution)/shard_map/ppermute | solution.py:60
  120.9 2.4 copy-start.6
  123.3 0.8 copy-start.8
  131.2 16.0 %copy-start.10 = (s32[1,64,2,8]{1,3,2,0:T(8,128)S(1)}, s32[1,64,2,8]{1,3,2,0:T(8,128)}, u32[]{:S(2)}) copy-start(s32[1,64,2,8]{1,3,2,0:T(8,128)} %param.22) | copy-start | bytes 12292
  131.2 16.4 %copy-start.3 = (bf16[256,2048]{1,0:T(8,128)(2,1)S(1)}, bf16[256,2048]{1,0:T(8,128)(2,1)}, u32[]{:S(2)}) copy-start(bf16[256,2048]{1,0:T(8,128)(2,1)} %get-tuple-element.26.k1) | copy-start | bytes 3145732
  131.2 16.3 %collective-permute-start.22 = (bf16[256,2048]{1,0:T(8,128)(2,1)}, bf16[256,2048]{1,0:T(8,128)(2,1)S(1)}, u32[]{:S(2)}, u32[]{:S(2)}) collective-permute-start(bf16[256,2048]{1,0:T(8,128)(2,1)} %get-tuple-element.28), channel_id=1, source_target_pairs={{0,32},{32,0},{64,96},{96,64},{1,33},{33,1},{65,97},{97,65},{2,34}... | collective-permute-start | bytes 3145736 | tf_op jit(solution)/shard_map/ppermute | solution.py:694
  134.4 2.2 copy-start.7
  143.8 6.1 %collective-permute-start.21 = (bf16[256,2048]{1,0:T(8,128)(2,1)}, bf16[256,2048]{1,0:T(8,128)(2,1)}, u32[]{:S(2)}, u32[]{:S(2)}) collective-permute-start(bf16[256,2048]{1,0:T(8,128)(2,1)} %get-tuple-element.27), channel_id=1, source_target_pairs={{0,32},{32,0},{64,96},{96,64},{1,33},{33,1},{65,97},{97,65},{2,34}... | collective-permute-start | bytes 3145736 | tf_op jit(solution)/shard_map/ppermute | solution.py:694
  147.5 26.6 %copy-start.4 = (bf16[256,2048]{1,0:T(8,128)(2,1)}, bf16[256,2048]{1,0:T(8,128)(2,1)S(1)}, u32[]{:S(2)}) copy-start(bf16[256,2048]{1,0:T(8,128)(2,1)S(1)} %collective-permute-done.22.g1) | copy-start | bytes 3145732
  147.7 15.0 %collective-permute-start.24 = (bf16[128,2048]{1,0:T(8,128)(2,1)S(1)}, bf16[128,2048]{1,0:T(8,128)(2,1)S(1)}, u32[]{:S(2)}, u32[]{:S(2)}) collective-permute-start(bf16[128,2048]{1,0:T(8,128)(2,1)S(1)} %add_convert_fusion), channel_id=1, source_target_pairs={{0,64},{32,96},{64,0},{96,32},{1,65},{33,97},{65,1},{97,33},{2,66}... | collective-permute-start | bytes 1572872 | tf_op jit(solution)/shard_map/ppermute | solution.py:698
  151.1 23.0 %collective-permute-start.23 = (bf16[128,2048]{1,0:T(8,128)(2,1)S(1)}, bf16[128,2048]{1,0:T(8,128)(2,1)}, u32[]{:S(2)}, u32[]{:S(2)}) collective-permute-start(bf16[128,2048]{1,0:T(8,128)(2,1)S(1)} %add_convert_fusion.1), channel_id=1, source_target_pairs={{0,64},{32,96},{64,0},{96,32},{1,65},{33,97},{65,1},{97,33},{2,66}... | collective-permute-start | bytes 1572872 | tf_op jit(solution)/shard_map/ppermute | solution.py:698
  162.7 11.3 %copy-start.9 = (bf16[128,2048]{1,0:T(8,128)(2,1)}, bf16[128,2048]{1,0:T(8,128)(2,1)S(1)}, u32[]{:S(2)}) copy-start(bf16[128,2048]{1,0:T(8,128)(2,1)S(1)} %collective-permute-done.24.r1) | copy-start | bytes 1572868
  265.1 68.0 %all-to-all-start = ((bf16[64,288,128]{2,1,0:T(8,128)(2,1)}), bf16[64,288,128]{2,1,0:T(8,128)(2,1)}, u32[]{:S(2)}, u32[]{:S(2)}) async-start(bf16[64,288,128]{2,1,0:T(8,128)(2,1)} %get-tuple-element.29), calls=%async_computation | async-start | bytes 9437184 | tf_op jit(solution)/shard_map/all_to_all | solution.py:702
  333.1 59.7 %all-to-all-start.3 = ((bf16[64,256,128]{2,1,0:T(8,128)(2,1)}), bf16[64,256,128]{2,1,0:T(8,128)(2,1)}, u32[]{:S(2)}, u32[]{:S(2)}) async-start(bf16[64,256,128]{2,1,0:T(8,128)(2,1)} %experts_a.1), calls=%async_computation.3 | async-start | bytes 8388608 | tf_op jit(solution)/shard_map/all_to_all | solution.py:702
  360.9 42.4 %copy-start.5 = (bf16[128,4096]{1,0:T(8,128)(2,1)S(1)}, bf16[128,4096]{1,0:T(8,128)(2,1)}, u32[]{:S(2)}) copy-start(bf16[128,4096]{1,0:T(8,128)(2,1)} %get-tuple-element.32) | copy-start | bytes 3145732
  392.8 71.7 %all-to-all-start.1 = ((bf16[64,288,128]{2,1,0:T(8,128)(2,1)}), bf16[64,288,128]{2,1,0:T(8,128)(2,1)}, u32[]{:S(2)}, u32[]{:S(2)}) async-start(bf16[64,288,128]{2,1,0:T(8,128)(2,1)} %experts_b.1), calls=%async_computation.1 | async-start | bytes 9437184 | tf_op jit(solution)/shard_map/all_to_all | solution.py:702

commit v5 on v4

--- a/solution.py
+++ b/solution.py
@@ -53,13 +53,16 @@
     return [x] + [lax.ppermute(x, "expert", move(k)) for k in (1, 2, 3)]
 
 
-def ring_relay(x, move):
-    half = x.shape[0] // 2
+def ring_parts(x, move, far):
     left = lax.ppermute(x, "expert", move(1))
     right = lax.ppermute(x, "expert", move(3))
-    lo = lax.ppermute(left[:half], "expert", move(1))
-    hi = lax.ppermute(right[half:], "expert", move(3))
-    return x, left, right, lo, hi
+    if far == "left":
+        last = lax.ppermute(left, "expert", move(1))
+    elif far == "right":
+        last = lax.ppermute(right, "expert", move(3))
+    else:
+        last = lax.ppermute(x, "expert", move(2))
+    return x, left, right, last
 
 
 def rotate_tables(positions):
@@ -191,7 +194,7 @@
             attn_part(q_ref, key_of, val_of, load, save, s_buf, None)
 
 
-def attn_last(sc, q_ref, m_in, acc_in, ka_ref, kb_ref, o_ref, s_buf):
+def attn_last(sc, q_ref, m_in, acc_in, kv_ref, o_ref, s_buf):
     z = sc[2]
 
     def finish(h, acc):
@@ -200,12 +203,11 @@
 
     @pl.when(z >= 2)
     def _():
-        ka, va = block_keys(ka_ref)
-        kb, vb = block_keys(kb_ref)
+        key_of, val_of = block_keys(kv_ref)
         attn_part(
             q_ref,
-            lambda j: ka(j) if j < 2 else kb(j - 2),
-            lambda j: va(j) if j < 2 else vb(j - 2),
+            key_of,
+            val_of,
             lambda h: (m_in[h, 0:1, :], acc_in[h]),
             lambda h, m, acc: finish(h, acc),
             s_buf,
@@ -255,7 +257,7 @@
 
 
 def attention(scal, q2, cs, sn, gain, pieces):
-    own, left, right, lo, hi = pieces
+    own, left, right, far = pieces
     table = pl.BlockSpec((PB, HD), lambda i, sc: (0, 0))
     qr, m, acc = attn_call(
         attn_first,
@@ -269,11 +271,14 @@
     )(scal, qr, m, acc, left, right)
     return attn_call(
         attn_last,
-        [Q_SPEC, M_SPEC, A_SPEC, kv_spec(2), kv_spec(2)],
+        [Q_SPEC, M_SPEC, A_SPEC, kv_spec(4)],
         Q_SPEC,
         jax.ShapeDtypeStruct((PB, SEQ * 1024), BF),
         1,
-    )(scal, qr, m, acc, lo, hi)
+    )(scal, qr, m, acc, far)
+
+
+WSPLIT = 576
 
 
 def proj_kernel(part, sc, a_ref, *rest):
@@ -282,10 +287,9 @@
     two = pl.ds(2 * part, 2)
     moves = []
     for half in range(2):
-        rows = pl.ds(half * 512, 512)
-        for k, dy in enumerate((0, 1, 3)):
+        rows = pl.ds(0, WSPLIT) if half == 0 else pl.ds(WSPLIT, 1024 - WSPLIT)
+        for k, dy in enumerate((0, 1, 3, 2)):
             moves.append((dy, w_in[4 * half + k].at[two], w.at[:, dy, rows]))
-        moves.append((2, w_in[4 * half + 3], w.at[:, 2, rows]))
     copies = [(d, pltpu.make_async_copy(a, b, sem.at[i])) for i, (d, a, b) in enumerate(moves)]
     for _, cp in copies:
         cp.start()
@@ -307,7 +311,7 @@
 
 
 def project(part, scal, attn, halves):
-    pieces = [x for h in halves for x in (h[0], h[1], h[2], h[3 + part])]
+    pieces = [x for h in halves for x in h]
     full = pl.BlockSpec(memory_space=pltpu.VMEM)
     return pl.pallas_call(
         functools.partial(proj_kernel, part),
@@ -674,10 +678,10 @@
     kv = ready_keys(
         keys[0].reshape(PB, SEQ * HD), values[0].reshape(PB, SEQ * HD), cs, sn, k_gain.reshape(1, HD)
     )
-    kv_all = ring_relay(jnp.stack(ring_four(kv, y_move)), z_move)
+    kv_all = ring_parts(jnp.stack(ring_four(kv, y_move)), z_move, "direct")
     w_all = [
-        ring_relay(jnp.stack(ring_four(w, z_move)), y_move)
-        for w in (out_weight[:512], out_weight[512:])
+        ring_parts(jnp.stack(ring_four(w, z_move)), y_move, far)
+        for w, far in ((out_weight[:WSPLIT], "left"), (out_weight[WSPLIT:], "right"))
     ]
 
     q2 = queries[0].reshape(PB, SEQ * 1024)

time: 474 us -> 441 us (0.930)
  waiting for transfers between devices: 188 us -> 169 us
  starting transfers between devices: 67.5 us -> 82.4 us
  blocking collectives: 80.9 us -> 66.6 us
  local copies, waits for them, and re-layouts: 24.1 us -> 9.85 us
    ppermute x9, waiting for transfers between devices: 33 us -> 11.1 us  [ring_four(): return [x] + [lax.ppermute(x, 'expert', move(k)) for k in (1, 2, 3)]]
    all_to_all x1, blocking collectives: 80.9 us -> 66.6 us  [exchange(): lax.all_to_all(x, ('tensor', 'expert'), split_axis=0, concat_axis=0, tile...]
    slice x6 -> x0, local copies, waits for them, and re-layouts: 11.3 us -> none  [the longest x3 5.67 us: ring_relay(): lo = lax.ppermute(left[:half], 'expert', move(1))]
    ppermute x12 -> x9, starting transfers between devices: 16.2 us -> 27.1 us  [the longest x1 18.4 us: ring_parts(): last = lax.ppermute(left, 'expert', move(1))]
    ppermute x2, starting transfers between devices: 6.63 us -> 12.3 us  [on_device(): got = lax.ppermute(send, 'tensor', CORE_SWAP)]
    ppermute x12 -> x9, waiting for transfers between devices: 14.1 us -> 16.8 us  [the longest x1 8.55 us: ring_parts(): last = lax.ppermute(right, 'expert', move(3))]
  transfers between devices with their start and end apart: 28 -> 25, of which waited for: 12 -> 15; matrix products, arithmetic and copies ran while one was open for 5% -> 3% of each run, Pallas kernels for 18% -> 18%
where the time goes in v5:
time: 441 us; the launch traced here: 440 us
  waiting for transfers between devices  169 us (38%)
  Pallas kernels  104 us (24%)
  starting transfers between devices  82.4 us (19%)
  blocking collectives  66.6 us (15%)
  local copies, waits for them, and re-layouts  9.85 us (2%)
  other arithmetic  7.29 us (2%)
    all_to_all x3, waiting for transfers between devices, exchange(): lax.all_to_all(x, ('tensor', 'expert'), split_axis=0, concat_axis=0, tile...  126 us
    all_to_all x1, blocking collectives, exchange(): lax.all_to_all(x, ('tensor', 'expert'), split_axis=0, concat_axis=0, tile...  66.6 us
    pallas_call x2, Pallas kernels, run_experts(): pl.pallas_call(functools.partial(expert_kernel, over), grid=(8,), out_sha...  37.9 us
    all_to_all x3, starting transfers between devices, exchange(): lax.all_to_all(x, ('tensor', 'expert'), split_axis=0, concat_axis=0, tile...  25.6 us
    ppermute x1, starting transfers between devices, ring_parts(): last = lax.ppermute(left, 'expert', move(1))  18.4 us
    ppermute x2, waiting for transfers between devices, on_device(): rests.append(lax.ppermute(other, 'tensor', X_SWAP))  14.6 us
    pallas_call x1, Pallas kernels, attention(): attn_call(attn_first, [Q_SPEC, table, table, pl.BlockSpec((1, HD), lambda...  14.3 us
    pallas_call x2, Pallas kernels, project(): pl.pallas_call(functools.partial(proj_kernel, part), out_shape=(jax.Shape...  14.3 us
  transfers between devices with their start and end apart: 25, of which 15 were waited for; matrix products, arithmetic and copies ran while one was open for 3% of the time, Pallas kernels for 18%

profile of v5, /device:TPU:11, one launch (start us, length us, event | category | flops | bytes accessed | tf_op | source)
XLA Modules:
  0.0 439.9 jit_solution(10596694107070334478)
XLA Ops:
  0.0 0.5 fusion.5
  0.6 1.7 copy_bitcast_fusion
  2.3 0.8 pad_maximum_fusion.3
  3.1 2.2 ready_keys.1
  5.3 1.3 collective-permute-start
  6.7 1.7 collective-permute-start.6
  8.4 3.3 collective-permute-start.7
  11.7 0.7 collective-permute-start.8
  12.4 0.7 collective-permute-start.1
  13.2 2.1 collective-permute-start.2
  15.3 1.7 collective-permute-done.6
  16.9 7.3 %collective-permute-done.7 = bf16[576,256]{1,0:T(8,128)(2,1)S(1)} collective-permute-done((bf16[576,256]{1,0:T(8,128)(2,1)S(1)}, bf16[576,256]{1,0:T(8,128)(2,1)S(1)}, u32[]{:S(2)}, u32[]{:S(2)}) %collective-permute-start.7) | collective-permute-done | bytes 294944 | tf_op jit(solution)/shard_map/ppermute | solution.py:53
  24.2 0.5 collective-permute-done.8
  24.7 3.9 collective-permute-start.14
  28.8 1.1 collective-permute-start.9
  29.9 1.1 pad_maximum_fusion.1.kv_ref
  31.0 0.9 collective-permute-done.12
  31.9 1.8 collective-permute-start.4
  33.7 0.2 collective-permute-done.13
  33.8 0.6 collective-permute-done.14
  34.5 0.2 collective-permute-start.16
  34.8 2.6 copy.49
  37.3 0.6 pad_add_fusion.sc
  37.9 1.7 collective-permute-start.5
  39.6 14.3 %shard_map.127 = (bf16[256,2048]{1,0:T(8,128)(2,1)}, f32[16,8,256]{2,1,0:T(8,128)}, f32[16,144,256]{2,1,0:T(8,128)}) custom-call(s32[4]{0:T(128)} %pad_add_fusion.sc, bf16[256,2048]{1,0:T(8,128)(2,1)} %bitcast.62, f32[256,128]{1,0:T(8,128)} %get-tuple-element.50.cos_ref, f32[256,128]{1,0:T(8,128)} %get-tuple-element.51.sin_ref, f32[1,128]{1,0:T(1,128)} %bitcast.82, ...), custom_call_target="tpu_custom_call" | custom-call | flops 4294967296 | bytes 8388608 | tf_op jit(solution)/shard_map/pallas_call | solution.py:262
  53.9 1.3 collective-permute-start.15
  55.2 4.1 collective-permute-done.3.ka_ref
  59.3 0.5 collective-permute-start.10
  59.9 2.1 collective-permute-start.17
  61.9 18.4 %collective-permute-start.11 = (bf16[4,576,256]{2,1,0:T(8,128)(2,1)}, bf16[4,576,256]{2,1,0:T(8,128)(2,1)}, u32[]{:S(2)}, u32[]{:S(2)}) collective-permute-start(bf16[4,576,256]{2,1,0:T(8,128)(2,1)} %collective-permute-done.9.rest_1_), channel_id=1, source_target_pairs={{0,2},{2,4},{4,6},{6,0},{8,10},{10,12},{12,14},{14,8},{16,18},{18,... | collective-permute-start | bytes 3538952 | tf_op jit(solution)/shard_map/ppermute | solution.py:60
  80.3 4.4 %shard_map.128 = (f32[16,8,256]{2,1,0:T(8,128)}, f32[16,144,256]{2,1,0:T(8,128)}) custom-call(s32[4]{0:T(128)} %pad_add_fusion.sc, bf16[256,2048]{1,0:T(8,128)(2,1)} %get-tuple-element.20.q_ref, f32[16,8,256]{2,1,0:T(8,128)} %get-tuple-element.21.m_in, f32[16,144,256]{2,1,0:T(8,128)} %get-tuple-element.22.acc_in, ...), custom_call_target="tpu_custom_call" | custom-call | flops 8589934592 | bytes 8388608 | tf_op jit(solution)/shard_map/pallas_call | solution.py:269
  84.8 4.9 %shard_map.129.a_ref = bf16[256,2048]{1,0:T(8,128)(2,1)} custom-call(s32[4]{0:T(128)} %pad_add_fusion.sc, bf16[256,2048]{1,0:T(8,128)(2,1)} %get-tuple-element.20.q_ref, f32[16,8,256]{2,1,0:T(8,128)} %get-tuple-element.23.m_in, f32[16,144,256]{2,1,0:T(8,128)} %get-tuple-element.24.acc_in, bf16[4,2,512,128]{3,2,1,0:T(8,128)(2,1)} %collective-permute-done.5.kv_ref), custom_call_target="tpu_custom_call" | custom-call | flops 4294967296 | bytes 8388608 | tf_op jit(solution)/shard_map/pallas_call | solution.py:272
  89.6 8.6 %collective-permute-done.17.rest_7_ = bf16[4,448,256]{2,1,0:T(8,128)(2,1)} collective-permute-done((bf16[4,448,256]{2,1,0:T(8,128)(2,1)S(1)}, bf16[4,448,256]{2,1,0:T(8,128)(2,1)}, u32[]{:S(2)}, u32[]{:S(2)}) %collective-permute-start.17) | collective-permute-done | bytes 917536 | tf_op jit(solution)/shard_map/ppermute | solution.py:62
  98.2 4.1 collective-permute-done.11.rest_3_
  102.3 7.1 %shard_map.131 = (bf16[256,2048]{1,0:T(8,128)(2,1)}, bf16[256,2048]{1,0:T(8,128)(2,1)}) custom-call(s32[4]{0:T(128)} %pad_add_fusion.sc, bf16[256,2048]{1,0:T(8,128)(2,1)} %shard_map.129.a_ref, bf16[4,576,256]{2,1,0:T(8,128)(2,1)} %copy-done.1, bf16[4,576,256]{2,1,0:T(8,128)(2,1)} %collective-permute-done.9.rest_1_, ...), custom_call_target="tpu_custom_call" | custom-call | flops 2147483648 | bytes 7340032 | tf_op jit(solution)/shard_map/pallas_call | solution.py:316
  109.5 12.1 %collective-permute-start.19 = (bf16[256,2048]{1,0:T(8,128)(2,1)}, bf16[256,2048]{1,0:T(8,128)(2,1)S(1)}, u32[]{:S(2)}, u32[]{:S(2)}) collective-permute-start(bf16[256,2048]{1,0:T(8,128)(2,1)} %get-tuple-element.28), channel_id=1, source_target_pairs={{0,32},{32,0},{64,96},{96,64},{1,33},{33,1},{65,97},{97,65},{2,34}... | collective-permute-start | bytes 3145736 | tf_op jit(solution)/shard_map/ppermute | solution.py:698
  121.6 7.1 %shard_map.130 = (bf16[256,2048]{1,0:T(8,128)(2,1)}, bf16[256,2048]{1,0:T(8,128)(2,1)}) custom-call(s32[4]{0:T(128)} %pad_add_fusion.sc, bf16[256,2048]{1,0:T(8,128)(2,1)} %shard_map.129.a_ref, bf16[4,576,256]{2,1,0:T(8,128)(2,1)} %copy-done.1, bf16[4,576,256]{2,1,0:T(8,128)(2,1)} %collective-permute-done.9.rest_1_, ...), custom_call_target="tpu_custom_call" | custom-call | flops 2147483648 | bytes 7340032 | tf_op jit(solution)/shard_map/pallas_call | solution.py:316
  128.8 0.2 collective-permute-start.18
  129.5 1.9 collective-permute-start.21
  131.4 0.4 collective-permute-done.18.g0
  131.9 2.1 add_convert_fusion.1
  134.0 1.8 collective-permute-start.20
  136.0 0.7 convert_and_fusion
  136.8 0.7 reshape.57.tgt_ref
  137.5 1.6 copy.39
  139.1 1.8 picking.1.pick
  140.9 3.4 collective-permute-done.21.r1
  144.2 11.2 %collective-permute-done.20.r0 = bf16[128,2048]{1,0:T(8,128)(2,1)} collective-permute-done((bf16[128,2048]{1,0:T(8,128)(2,1)}, bf16[128,2048]{1,0:T(8,128)(2,1)}, u32[]{:S(2)}, u32[]{:S(2)}) %collective-permute-start.20) | collective-permute-done | bytes 524320 | tf_op jit(solution)/shard_map/ppermute | solution.py:702
  155.5 10.1 %dispatch.1 = (bf16[128,4096]{1,0:T(8,128)(2,1)}, bf16[128,4096]{1,0:T(8,128)(2,1)}, bf16[64,256,128]{2,1,0:T(8,128)(2,1)}, bf16[64,288,128]{2,1,0:T(8,128)(2,1)}) custom-call(s32[4]{0:T(128)} %pad_add_fusion.sc, bf16[256,2048]{1,0:T(8,128)(2,1)} %get-tuple-element.25.k0, bf16[256,2048]{1,0:T(8,128)(2,1)} %get-tuple-element.26.k1, ...), custom_call_target="tpu_custom_call" | custom-call | flops 1073741824 | bytes 14680064 | tf_op jit(solution)/shard_map/dispatch/pallas_call | solution.py:429
  165.5 66.6 %all_to_all.20.refs_0_ = bf16[64,256,128]{2,1,0:T(8,128)(2,1)} all-to-all(bf16[64,256,128]{2,1,0:T(8,128)(2,1)} %get-tuple-element.30), channel_id=1, replica_groups=mesh['tensor'=4,'expert'=16,'dp'=2] {'tensor','expert'}, dimensions={0} | all-to-all | bytes 8388608 | tf_op jit(solution)/shard_map/all_to_all | solution.py:706
  232.1 7.2 %all-to-all-start = ((bf16[64,288,128]{2,1,0:T(8,128)(2,1)}), bf16[64,288,128]{2,1,0:T(8,128)(2,1)}, u32[]{:S(2)}, u32[]{:S(2)}) async-start(bf16[64,288,128]{2,1,0:T(8,128)(2,1)} %get-tuple-element.29), calls=%async_computation | async-start | bytes 9437184 | tf_op jit(solution)/shard_map/all_to_all | solution.py:706
  239.3 18.0 %experts_a.1 = bf16[64,256,128]{2,1,0:T(8,128)(2,1)} custom-call(bf16[64,256,128]{2,1,0:T(8,128)(2,1)} %all_to_all.20.refs_0_, bf16[1,4096,768]{2,1,0:T(8,128)(2,1)} %refs_1_.1, bf16[1,4096,768]{2,1,0:T(8,128)(2,1)} %refs_2_.3, bf16[1,768,4096]{2,1,0:T(8,128)(2,1)} %refs_3_.3), custom_call_target="tpu_custom_call" | custom-call | flops 10737418240 | bytes 28311552 | tf_op jit(solution)/shard_map/experts_a/pallas_call | solution.py:532
  257.3 43.1 %all-to-all-done.refs_0_.refs_1_ = bf16[64,288,128]{2,1,0:T(8,128)(2,1)} async-done(((bf16[64,288,128]{2,1,0:T(8,128)(2,1)}), bf16[64,288,128]{2,1,0:T(8,128)(2,1)}, u32[]{:S(2)}, u32[]{:S(2)}) %all-to-all-start) | async-done | bytes 4718624 | tf_op jit(solution)/shard_map/all_to_all | solution.py:706
  300.4 7.9 %all-to-all-start.3 = ((bf16[64,256,128]{2,1,0:T(8,128)(2,1)}), bf16[64,256,128]{2,1,0:T(8,128)(2,1)}, u32[]{:S(2)}, u32[]{:S(2)}) async-start(bf16[64,256,128]{2,1,0:T(8,128)(2,1)} %experts_a.1), calls=%async_computation.3 | async-start | bytes 8388608 | tf_op jit(solution)/shard_map/all_to_all | solution.py:706
  308.3 19.9 %experts_b.1 = bf16[64,288,128]{2,1,0:T(8,128)(2,1)} custom-call(bf16[64,288,128]{2,1,0:T(8,128)(2,1)} %all-to-all-done.refs_0_.refs_1_, bf16[64,288,128]{2,1,0:T(8,128)(2,1)} %all-to-all-done.refs_0_.refs_1_, bf16[1,4096,768]{2,1,0:T(8,128)(2,1)} %refs_1_.1, bf16[1,4096,768]{2,1,0:T(8,128)(2,1)} %refs_2_.3, bf16[1,768,4096]{2,1,0:T(8,128)(2,1)} %refs_3_.3), custom_call_target="tpu_custom_call" | custom-call | flops 10737418240 | bytes 28311552 | tf_op jit(solution)/shard_map/experts_b/pallas_call | solution.py:532
  328.2 31.8 %all-to-all-done.3.y_ref = bf16[64,256,128]{2,1,0:T(8,128)(2,1)} async-done(((bf16[64,256,128]{2,1,0:T(8,128)(2,1)}), bf16[64,256,128]{2,1,0:T(8,128)(2,1)}, u32[]{:S(2)}, u32[]{:S(2)}) %all-to-all-start.3) | async-done | bytes 4194336 | tf_op jit(solution)/shard_map/all_to_all | solution.py:706
  360.0 10.5 %all-to-all-start.1 = ((bf16[64,288,128]{2,1,0:T(8,128)(2,1)}), bf16[64,288,128]{2,1,0:T(8,128)(2,1)}, u32[]{:S(2)}, u32[]{:S(2)}) async-start(bf16[64,288,128]{2,1,0:T(8,128)(2,1)} %experts_b.1), calls=%async_computation.1 | async-start | bytes 9437184 | tf_op jit(solution)/shard_map/all_to_all | solution.py:706
  370.5 0.5 fusion.7
  371.5 0.7 broadcast_divide_fusion.gate_ref
  372.2 2.7 mixing.1
  374.9 5.3 %combine_first.1.sum_ref = f32[128,4096]{1,0:T(8,128)} custom-call(bf16[64,256,128]{2,1,0:T(8,128)(2,1)} %all-to-all-done.3.y_ref, bf16[128,4096]{1,0:T(8,128)(2,1)} %get-tuple-element.31.st_ref, bf16[256,1024]{1,0:T(8,128)(2,1)} %get-tuple-element.33.gm_ref), custom_call_target="tpu_custom_call" | custom-call | flops 1073741824 | bytes 6291456 | tf_op jit(solution)/shard_map/combine_first/pallas_call | solution.py:618
  380.2 51.5 %all-to-all-done.1.y_ref.yo_ref = bf16[64,288,128]{2,1,0:T(8,128)(2,1)} async-done(((bf16[64,288,128]{2,1,0:T(8,128)(2,1)}), bf16[64,288,128]{2,1,0:T(8,128)(2,1)}, u32[]{:S(2)}, u32[]{:S(2)}) %all-to-all-start.1) | async-done | bytes 4718624 | tf_op jit(solution)/shard_map/all_to_all | solution.py:706
  431.7 5.8 %combine_last.1 = bf16[128,4096]{1,0:T(8,128)(2,1)} custom-call(bf16[64,288,128]{2,1,0:T(8,128)(2,1)} %all-to-all-done.1.y_ref.yo_ref, bf16[64,288,128]{2,1,0:T(8,128)(2,1)} %all-to-all-done.1.y_ref.yo_ref, f32[128,4096]{1,0:T(8,128)} %combine_first.1.sum_ref, bf16[256,1024]{1,0:T(8,128)(2,1)} %get-tuple-element.33.gm_ref, ...), custom_call_target="tpu_custom_call" | custom-call | flops 1073741824 | bytes 6291456 | tf_op jit(solution)/shard_map/combine_last/pallas_call | solution.py:628
  437.4 2.5 reshape.59
  (58 shorter events, 1.7 us)
Async XLA Ops:
  0.0 370.5 %copy-start = (bf16[4096,64]{0,1:T(8,128)(2,1)S(1)}, bf16[4096,64]{0,1:T(8,128)(2,1)}, u32[]{:S(2)}) copy-start(bf16[4096,64]{0,1:T(8,128)(2,1)} %param.21) | copy-start | bytes 1572868
  0.0 6.6 %copy-start.9 = (bf16[1024,256]{1,0:T(8,128)(2,1)S(1)}, bf16[1024,256]{1,0:T(8,128)(2,1)}, u32[]{:S(2)}) copy-start(bf16[1024,256]{1,0:T(8,128)(2,1)} %param.18) | copy-start | bytes 1572868
  5.3 24.5 %copy-start.8 = (bf16[2,512,128]{2,1,0:T(8,128)(2,1)S(1)}, bf16[2,512,128]{2,1,0:T(8,128)(2,1)}, u32[]{:S(2)}) copy-start(bf16[2,512,128]{2,1,0:T(8,128)(2,1)} %ready_keys.1) | copy-start | bytes 786436
  5.3 7.8 %collective-permute-start = (bf16[2,512,128]{2,1,0:T(8,128)(2,1)}, bf16[2,512,128]{2,1,0:T(8,128)(2,1)S(1)}, u32[]{:S(2)}, u32[]{:S(2)}) collective-permute-start(bf16[2,512,128]{2,1,0:T(8,128)(2,1)} %ready_keys.1), channel_id=1, source_target_pairs={{0,2},{2,4},{4,6},{6,0},{8,10},{10,12},{12,14},{14,8},{16,18},{18,... | collective-permute-start | bytes 786440 | tf_op jit(solution)/shard_map/ppermute | solution.py:53
  6.7 10.3 %collective-permute-start.6 = (bf16[576,256]{1,0:T(8,128)(2,1)S(1)}, bf16[576,256]{1,0:T(8,128)(2,1)S(1)}, u32[]{:S(2)}, u32[]{:S(2)}) collective-permute-start(bf16[576,256]{1,0:T(8,128)(2,1)S(1)} %get-tuple-element.42), channel_id=1, source_target_pairs={{0,8},{2,10},{4,12},{6,14},{8,16},{10,18},{12,20},{14,22},{16,24},... | collective-permute-start | bytes 884744 | tf_op jit(solution)/shard_map/ppermute | solution.py:53
  8.4 15.8 %collective-permute-start.7 = (bf16[576,256]{1,0:T(8,128)(2,1)S(1)}, bf16[576,256]{1,0:T(8,128)(2,1)S(1)}, u32[]{:S(2)}, u32[]{:S(2)}) collective-permute-start(bf16[576,256]{1,0:T(8,128)(2,1)S(1)} %get-tuple-element.42), channel_id=1, source_target_pairs={{0,16},{2,18},{4,20},{6,22},{8,24},{10,26},{12,28},{14,30},{16,0},... | collective-permute-start | bytes 884744 | tf_op jit(solution)/shard_map/ppermute | solution.py:53
  11.7 13.0 %collective-permute-start.8 = (bf16[576,256]{1,0:T(8,128)(2,1)S(1)}, bf16[576,256]{1,0:T(8,128)(2,1)S(1)}, u32[]{:S(2)}, u32[]{:S(2)}) collective-permute-start(bf16[576,256]{1,0:T(8,128)(2,1)S(1)} %get-tuple-element.42), channel_id=1, source_target_pairs={{0,24},{2,26},{4,28},{6,30},{8,0},{10,2},{12,4},{14,6},{16,8},{18,... | collective-permute-start | bytes 884744 | tf_op jit(solution)/shard_map/ppermute | solution.py:53
  12.4 16.4 %collective-permute-start.1 = (bf16[2,512,128]{2,1,0:T(8,128)(2,1)}, bf16[2,512,128]{2,1,0:T(8,128)(2,1)S(1)}, u32[]{:S(2)}, u32[]{:S(2)}) collective-permute-start(bf16[2,512,128]{2,1,0:T(8,128)(2,1)} %ready_keys.1), channel_id=1, source_target_pairs={{0,4},{2,6},{4,0},{6,2},{8,12},{10,14},{12,8},{14,10},{16,20},{18,... | collective-permute-start | bytes 786440 | tf_op jit(solution)/shard_map/ppermute | solution.py:53
  13.2 16.7 %collective-permute-start.2 = (bf16[2,512,128]{2,1,0:T(8,128)(2,1)}, bf16[2,512,128]{2,1,0:T(8,128)(2,1)S(1)}, u32[]{:S(2)}, u32[]{:S(2)}) collective-permute-start(bf16[2,512,128]{2,1,0:T(8,128)(2,1)} %ready_keys.1), channel_id=1, source_target_pairs={{0,6},{2,0},{4,2},{6,4},{8,14},{10,8},{12,10},{14,12},{16,22},{18,... | collective-permute-start | bytes 786440 | tf_op jit(solution)/shard_map/ppermute | solution.py:53
  16.9 14.9 %collective-permute-start.12 = (bf16[448,256]{1,0:T(8,128)(2,1)S(1)}, bf16[448,256]{1,0:T(8,128)(2,1)S(1)}, u32[]{:S(2)}, u32[]{:S(2)}) collective-permute-start(bf16[448,256]{1,0:T(8,128)(2,1)S(1)} %get-tuple-element.40), channel_id=1, source_target_pairs={{0,8},{2,10},{4,12},{6,14},{8,16},{10,18},{12,20},{14,22},{16,24},... | collective-permute-start | bytes 688136 | tf_op jit(solution)/shard_map/ppermute | solution.py:53
  24.2 9.6 %collective-permute-start.13 = (bf16[448,256]{1,0:T(8,128)(2,1)S(1)}, bf16[448,256]{1,0:T(8,128)(2,1)S(1)}, u32[]{:S(2)}, u32[]{:S(2)}) collective-permute-start(bf16[448,256]{1,0:T(8,128)(2,1)S(1)} %get-tuple-element.40), channel_id=1, source_target_pairs={{0,16},{2,18},{4,20},{6,22},{8,24},{10,26},{12,28},{14,30},{16,0},... | collective-permute-start | bytes 688136 | tf_op jit(solution)/shard_map/ppermute | solution.py:53
  24.7 9.7 %collective-permute-start.14 = (bf16[448,256]{1,0:T(8,128)(2,1)S(1)}, bf16[448,256]{1,0:T(8,128)(2,1)S(1)}, u32[]{:S(2)}, u32[]{:S(2)}) collective-permute-start(bf16[448,256]{1,0:T(8,128)(2,1)S(1)} %get-tuple-element.40), channel_id=1, source_target_pairs={{0,24},{2,26},{4,28},{6,30},{8,0},{10,2},{12,4},{14,6},{16,8},{18,... | collective-permute-start | bytes 688136 | tf_op jit(solution)/shard_map/ppermute | solution.py:53
  28.8 30.5 %copy-start.1 = (bf16[4,576,256]{2,1,0:T(8,128)(2,1)}, bf16[4,576,256]{2,1,0:T(8,128)(2,1)S(1)}, u32[]{:S(2)}) copy-start(bf16[4,576,256]{2,1,0:T(8,128)(2,1)S(1)} %pad_maximum_fusion.rest_0_) | copy-start | bytes 3538948
  28.8 33.1 %collective-permute-start.9 = (bf16[4,576,256]{2,1,0:T(8,128)(2,1)S(1)}, bf16[4,576,256]{2,1,0:T(8,128)(2,1)}, u32[]{:S(2)}, u32[]{:S(2)}) collective-permute-start(bf16[4,576,256]{2,1,0:T(8,128)(2,1)S(1)} %pad_maximum_fusion.rest_0_), channel_id=1, source_target_pairs={{0,2},{2,4},{4,6},{6,0},{8,10},{10,12},{12,14},{14,8},{16,18},{18,... | collective-permute-start | bytes 3538952 | tf_op jit(solution)/shard_map/ppermute | solution.py:57
  31.0 28.3 %collective-permute-start.3 = (bf16[4,2,512,128]{3,2,1,0:T(8,128)(2,1)}, bf16[4,2,512,128]{3,2,1,0:T(8,128)(2,1)}, u32[]{:S(2)}, u32[]{:S(2)}) collective-permute-start(bf16[4,2,512,128]{3,2,1,0:T(8,128)(2,1)} %pad_maximum_fusion.1.kv_ref), channel_id=1, source_target_pairs={{0,8},{2,10},{4,12},{6,14},{8,16},{10,18},{12,20},{14,22},{16,24},... | collective-permute-start | bytes 3145736 | tf_op jit(solution)/shard_map/ppermute | solution.py:57
  31.9 28.0 %collective-permute-start.4 = (bf16[4,2,512,128]{3,2,1,0:T(8,128)(2,1)}, bf16[4,2,512,128]{3,2,1,0:T(8,128)(2,1)}, u32[]{:S(2)}, u32[]{:S(2)}) collective-permute-start(bf16[4,2,512,128]{3,2,1,0:T(8,128)(2,1)} %pad_maximum_fusion.1.kv_ref), channel_id=1, source_target_pairs={{0,24},{2,26},{4,28},{6,30},{8,0},{10,2},{12,4},{14,6},{16,8},{18,... | collective-permute-start | bytes 3145736 | tf_op jit(solution)/shard_map/ppermute | solution.py:58
  34.5 19.4 %copy-start.2 = (bf16[4,448,256]{2,1,0:T(8,128)(2,1)}, bf16[4,448,256]{2,1,0:T(8,128)(2,1)S(1)}, u32[]{:S(2)}) copy-start(bf16[4,448,256]{2,1,0:T(8,128)(2,1)S(1)} %pad_maximum_fusion.2.rest_4_) | copy-start | bytes 2752516
  34.5 19.4 %collective-permute-start.16 = (bf16[4,448,256]{2,1,0:T(8,128)(2,1)S(1)}, bf16[4,448,256]{2,1,0:T(8,128)(2,1)S(1)}, u32[]{:S(2)}, u32[]{:S(2)}) collective-permute-start(bf16[4,448,256]{2,1,0:T(8,128)(2,1)S(1)} %pad_maximum_fusion.2.rest_4_), channel_id=1, source_target_pairs={{0,6},{2,0},{4,2},{6,4},{8,14},{10,8},{12,10},{14,12},{16,22},{18,... | collective-permute-start | bytes 2752520 | tf_op jit(solution)/shard_map/ppermute | solution.py:58
  37.9 46.8 %collective-permute-start.5 = (bf16[4,2,512,128]{3,2,1,0:T(8,128)(2,1)}, bf16[4,2,512,128]{3,2,1,0:T(8,128)(2,1)}, u32[]{:S(2)}, u32[]{:S(2)}) collective-permute-start(bf16[4,2,512,128]{3,2,1,0:T(8,128)(2,1)} %pad_maximum_fusion.1.kv_ref), channel_id=1, source_target_pairs={{0,16},{2,18},{4,20},{6,22},{8,24},{10,26},{12,28},{14,30},{16,0},... | collective-permute-start | bytes 3145736 | tf_op jit(solution)/shard_map/ppermute | solution.py:64
  53.9 30.8 %copy-start.3 = (bf16[4,448,256]{2,1,0:T(8,128)(2,1)}, bf16[4,448,256]{2,1,0:T(8,128)(2,1)S(1)}, u32[]{:S(2)}) copy-start(bf16[4,448,256]{2,1,0:T(8,128)(2,1)S(1)} %collective-permute-done.16.rest_6_) | copy-start | bytes 2752516
  53.9 35.7 %collective-permute-start.15 = (bf16[4,448,256]{2,1,0:T(8,128)(2,1)S(1)}, bf16[4,448,256]{2,1,0:T(8,128)(2,1)}, u32[]{:S(2)}, u32[]{:S(2)}) collective-permute-start(bf16[4,448,256]{2,1,0:T(8,128)(2,1)S(1)} %pad_maximum_fusion.2.rest_4_), channel_id=1, source_target_pairs={{0,2},{2,4},{4,6},{6,0},{8,10},{10,12},{12,14},{14,8},{16,18},{18,... | collective-permute-start | bytes 2752520 | tf_op jit(solution)/shard_map/ppermute | solution.py:57
  59.3 30.3 %collective-permute-start.10 = (bf16[4,576,256]{2,1,0:T(8,128)(2,1)S(1)}, bf16[4,576,256]{2,1,0:T(8,128)(2,1)}, u32[]{:S(2)}, u32[]{:S(2)}) collective-permute-start(bf16[4,576,256]{2,1,0:T(8,128)(2,1)S(1)} %pad_maximum_fusion.rest_0_), channel_id=1, source_target_pairs={{0,6},{2,0},{4,2},{6,4},{8,14},{10,8},{12,10},{14,12},{16,22},{18,... | collective-permute-start | bytes 3538952 | tf_op jit(solution)/shard_map/ppermute | solution.py:58
  59.9 38.3 %collective-permute-start.17 = (bf16[4,448,256]{2,1,0:T(8,128)(2,1)S(1)}, bf16[4,448,256]{2,1,0:T(8,128)(2,1)}, u32[]{:S(2)}, u32[]{:S(2)}) collective-permute-start(bf16[4,448,256]{2,1,0:T(8,128)(2,1)S(1)} %collective-permute-done.16.rest_6_), channel_id=1, source_target_pairs={{0,6},{2,0},{4,2},{6,4},{8,14},{10,8},{12,10},{14,12},{16,22},{18,... | collective-permute-start | bytes 2752520 | tf_op jit(solution)/shard_map/ppermute | solution.py:62
  61.9 40.4 %collective-permute-start.11 = (bf16[4,576,256]{2,1,0:T(8,128)(2,1)}, bf16[4,576,256]{2,1,0:T(8,128)(2,1)}, u32[]{:S(2)}, u32[]{:S(2)}) collective-permute-start(bf16[4,576,256]{2,1,0:T(8,128)(2,1)} %collective-permute-done.9.rest_1_), channel_id=1, source_target_pairs={{0,2},{2,4},{4,6},{6,0},{8,10},{10,12},{12,14},{14,8},{16,18},{18,... | collective-permute-start | bytes 3538952 | tf_op jit(solution)/shard_map/ppermute | solution.py:60
  109.5 19.5 %copy-start.10 = (s32[1,64,2,8]{1,3,2,0:T(8,128)S(1)}, s32[1,64,2,8]{1,3,2,0:T(8,128)}, u32[]{:S(2)}) copy-start(s32[1,64,2,8]{1,3,2,0:T(8,128)} %param.22) | copy-start | bytes 12292
  109.5 19.8 %copy-start.4 = (bf16[256,2048]{1,0:T(8,128)(2,1)S(1)}, bf16[256,2048]{1,0:T(8,128)(2,1)}, u32[]{:S(2)}) copy-start(bf16[256,2048]{1,0:T(8,128)(2,1)} %get-tuple-element.26.k1) | copy-start | bytes 3145732
  109.5 19.8 %collective-permute-start.19 = (bf16[256,2048]{1,0:T(8,128)(2,1)}, bf16[256,2048]{1,0:T(8,128)(2,1)S(1)}, u32[]{:S(2)}, u32[]{:S(2)}) collective-permute-start(bf16[256,2048]{1,0:T(8,128)(2,1)} %get-tuple-element.28), channel_id=1, source_target_pairs={{0,32},{32,0},{64,96},{96,64},{1,33},{33,1},{65,97},{97,65},{2,34}... | collective-permute-start | bytes 3145736 | tf_op jit(solution)/shard_map/ppermute | solution.py:698
  128.8 3.1 collective-permute-start.18
  129.3 9.8 %copy-start.5 = (bf16[256,2048]{1,0:T(8,128)(2,1)}, bf16[256,2048]{1,0:T(8,128)(2,1)S(1)}, u32[]{:S(2)}) copy-start(bf16[256,2048]{1,0:T(8,128)(2,1)S(1)} %collective-permute-done.19.g1) | copy-start | bytes 3145732
  129.5 8.0 %copy-start.6 = (bf16[1,64,2,4096]{3,2,1,0:T(2,128)(2,1)S(1)}, bf16[1,64,2,4096]{3,2,1,0:T(2,128)(2,1)}, u32[]{:S(2)}) copy-start(bf16[1,64,2,4096]{3,2,1,0:T(2,128)(2,1)} %param.19) | copy-start | bytes 3145732
  129.5 14.7 %collective-permute-start.21 = (bf16[128,2048]{1,0:T(8,128)(2,1)S(1)}, bf16[128,2048]{1,0:T(8,128)(2,1)}, u32[]{:S(2)}, u32[]{:S(2)}) collective-permute-start(bf16[128,2048]{1,0:T(8,128)(2,1)S(1)} %add_convert_fusion), channel_id=1, source_target_pairs={{0,64},{32,96},{64,0},{96,32},{1,65},{33,97},{65,1},{97,33},{2,66}... | collective-permute-start | bytes 1572872 | tf_op jit(solution)/shard_map/ppermute | solution.py:702
  134.0 21.5 %collective-permute-start.20 = (bf16[128,2048]{1,0:T(8,128)(2,1)}, bf16[128,2048]{1,0:T(8,128)(2,1)}, u32[]{:S(2)}, u32[]{:S(2)}) collective-permute-start(bf16[128,2048]{1,0:T(8,128)(2,1)} %add_convert_fusion.1), channel_id=1, source_target_pairs={{0,64},{32,96},{64,0},{96,32},{1,65},{33,97},{65,1},{97,33},{2,66}... | collective-permute-start | bytes 1572872 | tf_op jit(solution)/shard_map/ppermute | solution.py:702
  232.1 68.3 %all-to-all-start = ((bf16[64,288,128]{2,1,0:T(8,128)(2,1)}), bf16[64,288,128]{2,1,0:T(8,128)(2,1)}, u32[]{:S(2)}, u32[]{:S(2)}) async-start(bf16[64,288,128]{2,1,0:T(8,128)(2,1)} %get-tuple-element.29), calls=%async_computation | async-start | bytes 9437184 | tf_op jit(solution)/shard_map/all_to_all | solution.py:706
  300.4 59.6 %all-to-all-start.3 = ((bf16[64,256,128]{2,1,0:T(8,128)(2,1)}), bf16[64,256,128]{2,1,0:T(8,128)(2,1)}, u32[]{:S(2)}, u32[]{:S(2)}) async-start(bf16[64,256,128]{2,1,0:T(8,128)(2,1)} %experts_a.1), calls=%async_computation.3 | async-start | bytes 8388608 | tf_op jit(solution)/shard_map/all_to_all | solution.py:706
  328.2 42.3 %copy-start.7 = (bf16[128,4096]{1,0:T(8,128)(2,1)S(1)}, bf16[128,4096]{1,0:T(8,128)(2,1)}, u32[]{:S(2)}) copy-start(bf16[128,4096]{1,0:T(8,128)(2,1)} %get-tuple-element.32) | copy-start | bytes 3145732
  360.0 71.7 %all-to-all-start.1 = ((bf16[64,288,128]{2,1,0:T(8,128)(2,1)}), bf16[64,288,128]{2,1,0:T(8,128)(2,1)}, u32[]{:S(2)}, u32[]{:S(2)}) async-start(bf16[64,288,128]{2,1,0:T(8,128)(2,1)} %experts_b.1), calls=%async_computation.1 | async-start | bytes 9437184 | tf_op jit(solution)/shard_map/all_to_all | solution.py:706
